TPU v7x, 32 devices: a whole 2x2x4 slice. The times are simulated.
32 devices in a mesh: gx: 2 (over x), gy: 4 (over y, core), gz: 4 (over z).
Axes of the slice: x: 2, y: 2, z: 4, core: 2. Of those that a mesh axis runs over, the one named last changes fastest.
Arguments:
- positions: float32 [3, 4, 8, 8, 128], P(None, 'gx', 'gy', 'gz'), may hold values from 0 to 1
- velocities: float32 [3, 4, 8, 8, 128], P(None, 'gx', 'gy', 'gz'), may hold values from -3 to 3
- masses: float32 [4, 8, 8, 128], P('gx', 'gy', 'gz'), may hold values from 0.004 to 0.016
- alphas: float32 [4, 8, 8, 128], P('gx', 'gy', 'gz'), may hold values from 0.2 to 2
- counts: int32 [4, 8, 8], P('gx', 'gy', 'gz'), may hold values from 64 to 128, as said below
Outputs:
- density: float32 [4, 8, 8, 128], P('gx', 'gy', 'gz')
- acceleration: float32 [3, 4, 8, 8, 128], P(None, 'gx', 'gy', 'gz')
- heating: float32 [4, 8, 8, 128], P('gx', 'gy', 'gz')
Inputs may be any that keep to these rules, and one draw needn't show every extreme that they name: `counts`: every cell holds 64 to 128 live particles in its first slots, and some cell holds 128.
All inputs are finite; a program needn't handle non-finite values.
Results may differ from a plain program's by a relative error of at most 0.0001.
Values sent between devices are 32-bit elements; how exact they have to be, the bound alone decides.
No kernel may reach another device: no remote copies, remote signals or barrier semaphores. Data moves between devices by JAX's collectives and lax.ppermute only.
A program may use at most 64 MiB of HBM per device.

v0:
```python
import math

import jax
import jax.numpy as jnp
from jax import lax
from jax.experimental import pallas as pl
from jax.experimental.pallas import tpu as pltpu
from jax.sharding import PartitionSpec as P

f32 = jnp.float32
bf16 = jnp.bfloat16
kernel_norm = 21.0 / (2.0 * math.pi)
axes = ("gx", "gy", "gz")
tile_rows = 8
feature_rows = 64
tiny = 1e-12

vmem = pl.BlockSpec(memory_space=pltpu.VMEM)
smem = pl.BlockSpec(memory_space=pltpu.SMEM)


def shaped(*dims, kind=f32):
    return jax.ShapeDtypeStruct(dims, kind)


def paired(axis):
    return lax.axis_size(axis) % 2 == 0


def first_sends_high(axis):
    return lax.axis_index(axis) % 2 == 0 if paired(axis) else lax.axis_index(axis) >= 0


def first_gives_before(axis):
    return lax.axis_index(axis) % 2 == 1 if paired(axis) else lax.axis_index(axis) >= 0


def routes(axis):
    peers = lax.axis_size(axis)
    if peers % 2 == 0:
        first = [(i, i + 1 if i % 2 == 0 else i - 1) for i in range(peers)]
        second = [(i, (i - 1 if i % 2 == 0 else i + 1) % peers) for i in range(peers)]
    else:
        first = [(i, (i + 1) % peers) for i in range(peers)]
        second = [(i, (i - 1) % peers) for i in range(peers)]
    return first, second


def exchanged(axis, sends):
    first, second = routes(axis)
    if first == second:
        both = lax.ppermute(sends, axis, first)
        return (both,)
    return lax.ppermute(sends[0], axis, first), lax.ppermute(sends[1], axis, second)


def merged(axis, mesh_shape):
    return mesh_shape[axis] == 2


def split3(value):
    high = value.astype(bf16).astype(f32)
    rest = value - high
    middle = rest.astype(bf16).astype(f32)
    return high, middle, rest - middle


def row_ids():
    return lax.broadcasted_iota(jnp.int32, (tile_rows, 128), 0)


def rows_of(*rows):
    ids = row_ids()
    out = jnp.zeros((tile_rows, 128), f32)
    for place, row in enumerate(rows):
        out = jnp.where(ids == place, row, out)
    return out


def moments(tile, offsets):
    ids = row_ids()
    shift = jnp.where(ids == 0, offsets[0], jnp.where(ids == 1, offsets[1], jnp.where(ids == 2, offsets[2], 0.0)))
    moved = tile + shift
    x, y, z, vx, vy, vz = (moved[i : i + 1] for i in range(6))
    sq = x * x + y * y + z * z
    xv = x * vx + y * vy + z * vz
    return jnp.where(ids == 6, sq, jnp.where(ids == 7, xv, moved)), tile[6:7]


def other_features(table, mass):
    p1, p2, p3 = split3(table)
    m1, m2, m3 = split3(mass)
    extra = rows_of(1.0, 1.0, 1.0, m1, m2, m3)
    lanes = jnp.concatenate([p1, p1, p1, p2, p2, p3, extra, jnp.zeros_like(extra)], 0)
    return lanes.T.astype(bf16)


def own_features(table):
    ids = row_ids()
    sq = split3(table[6:7])
    xv = split3(table[7:8])
    down = pltpu.roll(table, 3, 0)
    up = pltpu.roll(table, 5, 0)
    left = jnp.where(ids < 3, -2.0 * table, jnp.where(ids == 6, 1.0, 0.0))
    right = jnp.where(ids < 3, -up, jnp.where(ids < 6, -down, jnp.where(ids == 7, 1.0, 0.0)))
    halves = []
    for part, fixed in ((left, sq), (right, xv)):
        q1, q2, q3 = split3(part)
        extra = rows_of(*fixed)
        halves.append(jnp.concatenate([q1, q2, q3, q1, q2, q1, extra, jnp.zeros_like(extra)], 0))
    return jnp.concatenate(halves, 1).astype(bf16)


def mass_columns(table, mass):
    weighted = mass * table
    w1, w2, _ = split3(weighted)
    m1, m2, _ = split3(mass)
    extra = rows_of(m1, m2)
    return jnp.concatenate([w1, w2, extra, jnp.zeros_like(extra)], 0).astype(bf16)


def picker(first_row):
    ids = lax.broadcasted_iota(jnp.int32, (feature_rows, 128), 0)
    return jnp.where((ids >= first_row) & (ids < first_row + 3), 1.0, 0.0).astype(bf16)


def prepare(tile, offsets, at, feats, masses, columns):
    table, mass = moments(tile, offsets)
    lanes = other_features(table, mass)
    feats[at] = lanes
    masses[at] = jnp.dot(lanes, picker(51), preferred_element_type=f32)
    columns[at] = mass_columns(table, mass)


def density_pairs(own, cells, near, feats, masses, columns, ghi, glo, visc, sums, weighted):
    def one(c, _):
        right = own[c]
        total = jnp.zeros((tile_rows, 128), f32)
        picks = near(c)
        for k, n in enumerate(picks):
            both = jnp.dot(feats[n], right, preferred_element_type=f32)
            for r in range(0, 128, 16):
                dist = jnp.maximum(both[r : r + 16, :128], tiny)
                run = both[r : r + 16, 128:]
                q = dist * lax.rsqrt(dist)
                fall = jnp.maximum(1.0 - q, 0.0)
                g = fall * fall * fall
                part = g * q * masses[n, r : r + 16]
                total = total + part[:8] + part[8:]
                high = g.astype(bf16)
                ghi[c, k * 128 + r : k * 128 + r + 16] = high
                glo[c, k * 128 + r : k * 128 + r + 16] = (g - high.astype(f32)).astype(bf16)
                visc[c, k * 128 + r : k * 128 + r + 16] = g * jnp.minimum(run, 0.0) * (1.0 / (dist + 0.01))
        left = jnp.concatenate([columns[n] for n in picks], 1)
        sums[c] = jnp.dot(left, ghi[c], preferred_element_type=f32) + jnp.dot(
            left, glo[c], preferred_element_type=f32
        )
        weighted[c] = total
        return 0

    lax.fori_loop(0, cells, one, 0)


def prepare_force(tile, offsets, press, at, rhos, columns, gradients):
    table, mass = moments(tile, offsets)
    rho = press[0:1]
    weight = press[1:2]
    heavy = mass * table
    h1, h2, _ = split3(heavy)
    s1, s2, _ = split3(weight * heavy)
    m1, m2, _ = split3(mass)
    w1, w2, _ = split3(weight * mass)
    extra = rows_of(m1, m2, w1, w2)
    columns[at] = jnp.concatenate([h1, h2, s1, s2, extra, jnp.zeros_like(extra)], 0).astype(bf16)
    light = (mass / rho) * jnp.where(row_ids() < 3, table, 1.0)
    l1, l2, _ = split3(light)
    gradients[at] = jnp.concatenate([l1, l2], 0).astype(bf16)
    r1, r2, r3 = split3(rho)
    lanes = jnp.concatenate([rows_of(r1, r2, r3), jnp.zeros((tile_rows, 128), f32)], 0).T.astype(bf16)
    ids = lax.broadcasted_iota(jnp.int32, (16, 128), 0)
    rhos[at] = jnp.dot(lanes, jnp.where(ids < 3, 1.0, 0.0).astype(bf16), preferred_element_type=f32)


def force_pairs(cells, near, press_row, rhos, columns, gradients, ghi, glo, visc, thi, tlo, sums, slopes):
    def one(c, _):
        picks = near(c)
        mine = press_row(c)
        for k, n in enumerate(picks):
            for r in range(0, 128, 16):
                at = slice(k * 128 + r, k * 128 + r + 16)
                t = visc[c, at] * (1.0 / (rhos[n, r : r + 16] + mine))
                high = t.astype(bf16)
                thi[at] = high
                tlo[at] = (t - high.astype(f32)).astype(bf16)
        left = jnp.concatenate([columns[n] for n in picks], 1)
        sums[c] = jnp.dot(left, thi[...], preferred_element_type=f32) + jnp.dot(
            left, tlo[...], preferred_element_type=f32
        )
        left = jnp.concatenate([gradients[n] for n in picks], 1)
        slopes[c] = jnp.dot(left, ghi[c], preferred_element_type=f32) + jnp.dot(
            left, glo[c], preferred_element_type=f32
        )
        return 0

    lax.fori_loop(0, cells, one, 0)


def parts_of(c):
    return c // 4, (c // 2) % 2, c % 2


def flat(*pairs):
    at = 0
    for size, index in pairs:
        at = at * size + index
    return at


def near_own(c):
    return list(range(8))


def near_z(c):
    cx, cy, cz = parts_of(c)
    return [flat((2, cz), (2, x), (2, y)) for x in range(2) for y in range(2)]


def near_y(c):
    cx, cy, cz = parts_of(c)
    return [flat((2, cy), (2, x), (4, cz + dz)) for x in range(2) for dz in range(3)]


def near_x(c):
    cx, cy, cz = parts_of(c)
    return [flat((2, cx), (4, cy + dy), (4, cz + dz)) for dy in range(3) for dz in range(3)]


def place_own(e):
    x, y, z = parts_of(e)
    return x - 1, y - 1, z - 1


def place_z(e):
    side, x, y = parts_of(e)
    return x - 1, y - 1, 3 * side - 2


def place_y(e):
    return (e // 4) % 2 - 1, 3 * (e // 8) - 2, e % 4 - 2


def place_x(e):
    return 3 * (e // 16) - 2, (e // 4) % 4 - 2, e % 4 - 2


def offsets_of(place):
    return [jnp.asarray(v, jnp.int32).astype(f32) for v in place]


groups = {
    "own": (8, near_own, place_own, 8),
    "z": (8, near_z, place_z, 4),
    "y": (16, near_y, place_y, 6),
    "x": (32, near_x, place_x, 9),
}


def scratch_density(entries):
    return [
        pltpu.VMEM((entries, 128, feature_rows), bf16),
        pltpu.VMEM((entries, 128, 128), f32),
        pltpu.VMEM((entries, 32, 128), bf16),
    ]


def pair_outputs(count):
    return [
        shaped(8, count * 128, 128, kind=bf16),
        shaped(8, count * 128, 128, kind=bf16),
        shaped(8, count * 128, 128),
        shaped(8, 32, 128),
        shaped(8, tile_rows, 128),
    ]


def call(body, outs, operands, specs=None, scratch=(), limit=24, name=None):
    return pl.pallas_call(
        body,
        out_shape=tuple(outs),
        in_specs=specs or [vmem] * len(operands),
        out_specs=tuple([vmem] * len(outs)),
        scratch_shapes=list(scratch),
        compiler_params=pltpu.CompilerParams(vmem_limit_bytes=limit << 20),
        name=name,
    )(*operands)


def take_side(before, refs, side, rest):
    if len(refs) == 1:
        one, two = refs[0][(0,) + rest], refs[0][(1,) + rest]
    else:
        one, two = refs[0][rest], refs[1][rest]
    return jnp.where(before, one, two) if side == 0 else jnp.where(before, two, one)


def send_shapes(axis, plane):
    if lax.axis_size(axis) == 2:
        return [shaped(2, *plane)]
    return [shaped(*plane), shaped(*plane)]


def put_sends(axis, refs, high, tile_at, rest):
    top, bottom = tile_at(1), tile_at(0)
    one, two = jnp.where(high, top, bottom), jnp.where(high, bottom, top)
    if len(refs) == 1:
        refs[0][(0,) + rest] = one
        refs[0][(1,) + rest] = two
    else:
        refs[0][rest] = one
        refs[1][rest] = two


def receive(axis, sends):
    if len(sends) == 1:
        return exchanged(axis, sends[0])
    return exchanged(axis, sends)


def pack_y(own, from_z, rows, name):
    sends = send_shapes("gy", (2, 4, rows, 128))
    n = len(from_z)

    def body(own_ref, *refs):
        got, out = refs[:n], refs[n:]
        high = first_sends_high("gy")
        before = first_gives_before("gz")
        for x in range(2):
            for e in range(4):

                def tile_at(y, x=x, e=e):
                    if 1 <= e <= 2:
                        return own_ref[x, y, e - 1]
                    return take_side(before, got, 0 if e == 0 else 1, (x, y))

                put_sends("gy", out, high, tile_at, (x, e))

    return call(body, sends, (own, *from_z), name=name, limit=4)


def pack_x(own, from_z, from_y, rows, name):
    sends = send_shapes("gx", (4, 4, rows, 128))
    n, m = len(from_z), len(from_y)

    def body(own_ref, *refs):
        got_z, got_y, out = refs[:n], refs[n : n + m], refs[n + m :]
        high = first_sends_high("gx")
        before_z = first_gives_before("gz")
        before_y = first_gives_before("gy")
        for a in range(4):
            for e in range(4):

                def tile_at(x, a=a, e=e):
                    if not 1 <= a <= 2:
                        return take_side(before_y, got_y, 0 if a == 0 else 1, (x, e))
                    if 1 <= e <= 2:
                        return own_ref[x, a - 1, e - 1]
                    return take_side(before_z, got_z, 0 if e == 0 else 1, (x, a - 1))

                put_sends("gx", out, high, tile_at, (a, e))

    return call(body, sends, (own, *from_z, *from_y), name=name, limit=4)


inner_dims = {"z": (2, 2), "y": (2, 4), "x": (4, 4)}


def entry_tile(group, before, refs, e, sides):
    a, b = inner_dims[group]
    return take_side(before, refs, sides, (e // b, e % b))


def density_own(own):
    entries, near, place, count = groups["own"]

    def body(own_ref, ghi, glo, visc, sums, weighted, table_ref, feats, masses, columns):
        def one(c, _):
            x, y, z = parts_of(c)
            tile = own_ref[x, y, z]
            offsets = offsets_of(place(c))
            prepare(tile, offsets, c, feats, masses, columns)
            table, _mass = moments(tile, offsets)
            table_ref[c] = own_features(table)
            return 0

        lax.fori_loop(0, 8, one, 0)
        density_pairs(table_ref, 8, near, feats, masses, columns, ghi, glo, visc, sums, weighted)

    outs = pair_outputs(count) + [shaped(8, feature_rows, 256, kind=bf16)]
    return call(body, outs, (own,), scratch=scratch_density(entries), name="density_own")


def density_halo(group, axis, received, own_feats):
    entries, near, place, count = groups[group]
    n = len(received)
    half = entries // 2

    def body(*refs):
        got, own_ref = refs[:n], refs[n]
        ghi, glo, visc, sums, weighted, feats, masses, columns = refs[n + 1 :]
        before = first_gives_before(axis)
        for side in range(2):

            def one(e, _, side=side):
                tile = entry_tile(group, before, got, e, side)
                at = side * half + e
                prepare(tile, offsets_of(place(at)), at, feats, masses, columns)
                return 0

            lax.fori_loop(0, half, one, 0)
        density_pairs(own_ref, 8, near, feats, masses, columns, ghi, glo, visc, sums, weighted)

    return call(
        body,
        pair_outputs(count),
        (*received, own_feats),
        scratch=scratch_density(entries),
        name="density_" + group,
    )


def pressure(own, alphas, counts, partials):
    sends = send_shapes("gz", (2, 2, 2, 128))
    outs = [shaped(2, 2, 2, 2, 128), shaped(2, 2, 2, 128), shaped(8, tile_rows, 128)] + sends
    n = len(partials)

    def body(counts_ref, alphas_ref, own_ref, *refs):
        pieces, (press, density, first), out = refs[:n], refs[n : n + 3], refs[n + 3 :]
        high = first_sends_high("gz")
        lanes = lax.broadcasted_iota(jnp.int32, (1, 128), 1)
        for x in range(2):
            for y in range(2):
                for z in range(2):
                    c = 4 * x + 2 * y + z
                    table, _mass = moments(own_ref[x, y, z], [float(v - 1) for v in (x, y, z)])
                    s = sum(p[c] for p in pieces[0::2])
                    gq = jnp.sum(sum(p[c] for p in pieces[1::2]), 0, keepdims=True)
                    t = s[0:8] + s[8:16]
                    m0 = s[16:17] + s[17:18]
                    pos, vel = table[0:3], table[3:6]
                    x_mx = jnp.sum(pos * t[0:3], 0, keepdims=True)
                    x_mv = jnp.sum(pos * t[3:6], 0, keepdims=True)
                    v_mx = jnp.sum(vel * t[0:3], 0, keepdims=True)
                    gr2 = t[6:7] + table[6:7] * m0 - 2.0 * x_mx
                    rho = kernel_norm * (m0 + 3.0 * gq - 4.0 * gr2)
                    div = -20.0 * kernel_norm * (t[7:8] + table[7:8] * m0 - x_mv - v_mx)
                    rho = jnp.where(lanes < counts_ref[x, y, z], rho, 1.0)
                    compress = jnp.maximum(div / rho, 0.0)
                    weight = alphas_ref[x, y, z : z + 1, :] * compress / (compress + 1.0)
                    press[x, y, z] = jnp.concatenate([rho, weight], 0)
                    density[x, y, z : z + 1, :] = rho
                    first[c] = jnp.concatenate(
                        [pos * m0 - t[0:3], div, jnp.zeros((tile_rows - 4, 128), f32)], 0
                    )
        for x in range(2):
            for y in range(2):
                put_sends("gz", out, high, lambda z, x=x, y=y: press[x, y, z], (x, y))

    operands = (counts, alphas, own, *partials)
    specs = [smem] + [vmem] * (len(operands) - 1)
    return call(body, outs, operands, specs=specs, name="pressure", limit=8)


def scratch_force(entries, count):
    return [
        pltpu.VMEM((entries, 128, 128), f32),
        pltpu.VMEM((entries, 48, 128), bf16),
        pltpu.VMEM((entries, 16, 128), bf16),
        pltpu.VMEM((count * 128, 128), bf16),
        pltpu.VMEM((count * 128, 128), bf16),
    ]


def force_outputs():
    return [shaped(8, 48, 128), shaped(8, 16, 128)]


def force_own(own, press, kept):
    entries, near, place, count = groups["own"]

    def body(own_ref, press_ref, ghi, glo, visc, sums, slopes, rhos, columns, gradients, thi, tlo):
        def one(c, _):
            x, y, z = parts_of(c)
            prepare_force(
                own_ref[x, y, z], offsets_of(place(c)), press_ref[x, y, z], c, rhos, columns, gradients
            )
            return 0

        lax.fori_loop(0, 8, one, 0)

        def mine(c):
            x, y, z = parts_of(c)
            return press_ref[x, y, z, 0:1]

        force_pairs(8, near, mine, rhos, columns, gradients, ghi, glo, visc, thi, tlo, sums, slopes)

    return call(
        body,
        force_outputs(),
        (own, press, *kept),
        scratch=scratch_force(entries, count),
        name="force_own",
    )


def force_halo(group, axis, received, press_received, press, kept):
    entries, near, place, count = groups[group]
    n = len(received)
    half = entries // 2

    def body(*refs):
        got, got_press, press_ref = refs[:n], refs[n : 2 * n], refs[2 * n]
        ghi, glo, visc, sums, slopes, rhos, columns, gradients, thi, tlo = refs[2 * n + 1 :]
        before = first_gives_before(axis)
        for side in range(2):

            def one(e, _, side=side):
                tile = entry_tile(group, before, got, e, side)
                fields = entry_tile(group, before, got_press, e, side)
                at = side * half + e
                prepare_force(tile, offsets_of(place(at)), fields, at, rhos, columns, gradients)
                return 0

            lax.fori_loop(0, half, one, 0)

        def mine(c):
            x, y, z = parts_of(c)
            return press_ref[x, y, z, 0:1]

        force_pairs(8, near, mine, rhos, columns, gradients, ghi, glo, visc, thi, tlo, sums, slopes)

    return call(
        body,
        force_outputs(),
        (*received, *press_received, press, *kept),
        scratch=scratch_force(entries, count),
        name="force_" + group,
    )


def finish(own, press, first, counts, partials):
    outs = [shaped(3, 2, 2, 2, 128), shaped(2, 2, 2, 128)]
    n = len(partials)

    def body(counts_ref, own_ref, press_ref, first_ref, *refs):
        pieces, (accel, heating) = refs[:n], refs[n:]
        lanes = lax.broadcasted_iota(jnp.int32, (1, 128), 1)
        for x in range(2):
            for y in range(2):
                for z in range(2):
                    c = 4 * x + 2 * y + z
                    table, _mass = moments(own_ref[x, y, z], [float(v - 1) for v in (x, y, z)])
                    u = sum(p[c] for p in pieces[0::2])
                    v = sum(p[c] for p in pieces[1::2])
                    plain, scaled = u[0:8] + u[8:16], u[16:24] + u[24:32]
                    a0, b0 = u[32:33] + u[33:34], u[34:35] + u[35:36]
                    g = v[0:8] + v[8:16]
                    rho, weight = press_ref[x, y, z, 0:1], press_ref[x, y, z, 1:2]
                    inverse = 1.0 / rho
                    mixed = weight * plain + scaled
                    zero = weight * a0 + b0
                    pos, vel = table[0:3], table[3:6]
                    total = (
                        inverse * first_ref[c, 0:3]
                        + (pos * g[3:4] - g[0:3])
                        - (pos * zero - mixed[0:3])
                    )
                    live = jnp.where(lanes < counts_ref[x, y, z], 1.0, 0.0)
                    push = (20.0 * kernel_norm) * live * total
                    work = (
                        mixed[7:8]
                        + table[7:8] * zero
                        - jnp.sum(pos * mixed[3:6], 0, keepdims=True)
                        - jnp.sum(vel * mixed[0:3], 0, keepdims=True)
                    )
                    warm = live * (first_ref[c, 3:4] * inverse + (10.0 * kernel_norm) * work)
                    for i in range(3):
                        accel[i, x, y, z : z + 1, :] = push[i : i + 1]
                    heating[x, y, z : z + 1, :] = warm

    operands = (counts, own, press, first, *partials)
    specs = [smem] + [vmem] * (len(operands) - 1)
    return call(body, outs, operands, specs=specs, name="finish", limit=8)


def gather_own(positions, velocities, masses, counts):
    sends = send_shapes("gz", (2, 2, tile_rows, 128))

    def body(counts_ref, pos, vel, mass, own, *out):
        high = first_sends_high("gz")
        lanes = lax.broadcasted_iota(jnp.int32, (1, 128), 1)
        for x in range(2):
            for y in range(2):
                for z in range(2):
                    here = mass[x, y, z : z + 1, :] * jnp.where(lanes < counts_ref[x, y, z], 1.0, 0.0)
                    own[x, y, z] = rows_of(
                        *(pos[i, x, y, z : z + 1, :] for i in range(3)),
                        *(vel[i, x, y, z : z + 1, :] for i in range(3)),
                        here,
                    )
        for x in range(2):
            for y in range(2):
                put_sends("gz", out, high, lambda z, x=x, y=y: own[x, y, z], (x, y))

    outs = [shaped(2, 2, 2, tile_rows, 128)] + sends
    operands = (counts, positions, velocities, masses)
    return call(body, outs, operands, specs=[smem] + [vmem] * 3, name="gather_own", limit=4)


def per_block(positions, velocities, masses, alphas, counts):
    own, *sends = gather_own(positions, velocities, masses, counts)
    from_z = receive("gz", sends)
    *kept_own, sums_own, weighted_own, own_feats = density_own(own)
    from_y = receive("gy", pack_y(own, from_z, tile_rows, "pack_y"))
    *kept_z, sums_z, weighted_z = density_halo("z", "gz", from_z, own_feats)
    from_x = receive("gx", pack_x(own, from_z, from_y, tile_rows, "pack_x"))
    *kept_y, sums_y, weighted_y = density_halo("y", "gy", from_y, own_feats)
    *kept_x, sums_x, weighted_x = density_halo("x", "gx", from_x, own_feats)
    partials = (sums_own, weighted_own, sums_z, weighted_z, sums_y, weighted_y, sums_x, weighted_x)
    press, density, first, *sends = pressure(own, alphas, counts, partials)
    press_z = receive("gz", sends)
    forces = list(force_own(own, press, kept_own))
    press_y = receive("gy", pack_y(press, press_z, 2, "pack_press_y"))
    forces += force_halo("z", "gz", from_z, press_z, press, kept_z)
    press_x = receive("gx", pack_x(press, press_z, press_y, 2, "pack_press_x"))
    forces += force_halo("y", "gy", from_y, press_y, press, kept_y)
    forces += force_halo("x", "gx", from_x, press_x, press, kept_x)
    accel, heating = finish(own, press, first, counts, forces)
    return density, accel, heating


neighbour_shifts = [
    (shift_x, shift_y, shift_z)
    for shift_x in (-1, 0, 1)
    for shift_y in (-1, 0, 1)
    for shift_z in (-1, 0, 1)
]


def extended(shard, sides, width):
    for axis, dim in sides:
        peers, length = (lax.axis_size(axis), shard.shape[dim])
        up = [(i, (i + 1) % peers) for i in range(peers)]
        down = [(j, i) for i, j in up]
        last = lax.slice_in_dim(shard, length - width, length, axis=dim)
        leading = lax.slice_in_dim(shard, 0, width, axis=dim)
        before = lax.ppermute(last, axis, up)
        after = lax.ppermute(leading, axis, down)
        shard = jnp.concatenate([before, shard, after], axis=dim)
    return shard


def pair_geometry(own_rows, neighbour, cell_shift):
    offset_parts = [
        own_rows[axis_id][:, :, None] - neighbour[axis_id][:, None, :] - float(cell_shift[axis_id])
        for axis_id in range(3)
    ]
    dist_sq = (
        offset_parts[0] * offset_parts[0]
        + offset_parts[1] * offset_parts[1]
        + offset_parts[2] * offset_parts[2]
    )
    scaled = jnp.minimum(jnp.sqrt(dist_sq), 1.0)
    falloff = 1.0 - scaled
    kernel_value = kernel_norm * falloff**4 * (1.0 + 4.0 * scaled)
    kernel_slope = -20.0 * kernel_norm * falloff**3
    approach = sum(
        (
            (own_rows[3 + axis_id][:, :, None] - neighbour[3 + axis_id][:, None, :])
            * offset_parts[axis_id]
            for axis_id in range(3)
        )
    )
    return (offset_parts, dist_sq, kernel_value, kernel_slope, approach)


def density_terms(own_rows, neighbour, cell_shift):
    offset_parts, dist_sq, kernel_value, kernel_slope, approach = pair_geometry(
        own_rows, neighbour, cell_shift
    )
    other_mass = neighbour[6][:, None, :]
    return (
        jnp.sum(other_mass * kernel_value, -1),
        jnp.sum(other_mass * kernel_slope * approach, -1),
    )


def force_terms(own_rows, neighbour, cell_shift):
    offset_parts, dist_sq, kernel_value, kernel_slope, approach = pair_geometry(
        own_rows, neighbour, cell_shift
    )
    rho_own = own_rows[7][:, :, None]
    rho_other = neighbour[7][:, None, :]
    converge = jnp.minimum(approach, 0.0) / (dist_sq + 0.01)
    viscous = (
        -(own_rows[8][:, :, None] + neighbour[8][:, None, :]) * converge / (rho_own + rho_other)
    )
    mslope = neighbour[6][:, None, :] * kernel_slope
    pair_force = mslope * (1.0 / rho_own + 1.0 / rho_other + viscous)
    accel_terms = jnp.stack(
        [-jnp.sum(pair_force * offset_parts[axis_id], -1) for axis_id in range(3)], 0
    )
    heating = jnp.sum(mslope * (1.0 / rho_own + 0.5 * viscous) * approach, -1)
    return (accel_terms, heating)


def switch_fields(density, div_sum, live_rows, weights):
    rho_live = jnp.where(live_rows > 0, density, 1.0)
    compress = jnp.maximum(div_sum / rho_live, 0.0)
    return jnp.stack([rho_live, weights * compress / (compress + 1.0)], 0)


def sweep(terms, padded):
    count = padded.shape[0]
    slot_count = padded.shape[-1]
    span_x = padded.shape[1] - 2
    span_y = padded.shape[2] - 2
    span_z = padded.shape[3] - 2
    own_rows = padded[:, 1 : span_x + 1, 1 : span_y + 1, 1 : span_z + 1].reshape(
        count, -1, slot_count
    )
    totals = None
    for cell_shift in neighbour_shifts:
        neighbour = padded[
            :,
            1 + cell_shift[0] : 1 + cell_shift[0] + span_x,
            1 + cell_shift[1] : 1 + cell_shift[1] + span_y,
            1 + cell_shift[2] : 1 + cell_shift[2] + span_z,
        ]
        result = terms(own_rows, neighbour.reshape(count, -1, slot_count), cell_shift)
        totals = (
            result
            if totals is None
            else jax.tree.map(lambda left, right: left + right, totals, result)
        )
    return totals


def per_device(positions, velocities, masses, alphas, counts):
    slot_count = positions.shape[-1]
    cell_shape = positions.shape[1:4]
    occupied = (
        jnp.arange(slot_count, dtype=jnp.int32)[None, None, None, :] < counts[..., None]
    ).astype(jnp.float32)
    live_mass = masses * occupied
    carried = jnp.concatenate([positions, velocities, live_mass[None]], 0)
    padded = extended(carried, (("gx", 1), ("gy", 2), ("gz", 3)), 1)
    density, div_sum = sweep(density_terms, padded)
    live_rows = occupied.reshape(-1, slot_count)
    weights = alphas.reshape(-1, slot_count)
    pressure_fields = switch_fields(density, div_sum, live_rows, weights).reshape(
        (2,) + cell_shape + (slot_count,)
    )
    own_density = pressure_fields[0]
    pressure_pad = extended(pressure_fields, (("gx", 1), ("gy", 2), ("gz", 3)), 1)
    fields = jnp.concatenate([padded, pressure_pad], 0)
    accel_total, heat_total = sweep(force_terms, fields)
    acceleration = accel_total.reshape((3,) + cell_shape + (slot_count,)) * occupied[None]
    heating = heat_total.reshape(cell_shape + (slot_count,)) * occupied
    return (own_density, acceleration, heating)


def per_device_any(positions, velocities, masses, alphas, counts):
    if positions.shape[1:] == (2, 2, 2, 128):
        return per_block(positions, velocities, masses, alphas, counts)
    return per_device(positions, velocities, masses, alphas, counts)


def solution(mesh):
    return jax.shard_map(
        per_device_any,
        mesh=mesh,
        in_specs=(
            P(None, "gx", "gy", "gz", None),
            P(None, "gx", "gy", "gz", None),
            P("gx", "gy", "gz", None),
            P("gx", "gy", "gz", None),
            P("gx", "gy", "gz"),
        ),
        out_specs=(
            P("gx", "gy", "gz", None),
            P(None, "gx", "gy", "gz", None),
            P("gx", "gy", "gz", None),
        ),
        check_vma=False,
    )
```

profile of v0, /device:TPU:0, one launch (start us, length us, event | category | flops | bytes accessed | tf_op | source)
XLA Modules:
  0.0 92.5 jit_solution(11184195965489684206)
XLA Ops:
  1.3 0.7 copy-done.3
  2.0 0.7 copy-done.4
  2.7 0.7 copy-done.6
  4.0 3.1 %collective-permute-start = (f32[2,2,8,128]{3,2,1,0:T(8,128)S(1)}, f32[2,2,8,128]{3,2,1,0:T(8,128)S(1)}, u32[]{:S(2)}, u32[]{:S(2)}) collective-permute-start(f32[2,2,8,128]{3,2,1,0:T(8,128)S(1)} %get-tuple-element.49), channel_id=1, source_target_pairs={{0,1},{1,0},{2,3},{3,2},{4,5},{5,4},{6,7},{7,6},{8,9},{9,8},{10,11... | collective-permute-start | bytes 49160 | tf_op jit(solution)/shard_map/ppermute | solution.py:54
  7.1 2.5 %collective-permute-start.1 = (f32[2,2,8,128]{3,2,1,0:T(8,128)S(1)}, f32[2,2,8,128]{3,2,1,0:T(8,128)S(1)}, u32[]{:S(2)}, u32[]{:S(2)}) collective-permute-start(f32[2,2,8,128]{3,2,1,0:T(8,128)S(1)} %get-tuple-element.50), channel_id=1, source_target_pairs={{0,3},{1,2},{2,1},{3,0},{4,7},{5,6},{6,5},{7,4},{8,11},{9,10},{10,... | collective-permute-start | bytes 49160 | tf_op jit(solution)/shard_map/ppermute | solution.py:54
  9.6 3.1 %collective-permute-done.1.refs_1_ = f32[2,2,8,128]{3,2,1,0:T(8,128)S(1)} collective-permute-done((f32[2,2,8,128]{3,2,1,0:T(8,128)S(1)}, f32[2,2,8,128]{3,2,1,0:T(8,128)S(1)}, u32[]{:S(2)}, u32[]{:S(2)}) %collective-permute-start.1) | collective-permute-done | bytes 16416 | tf_op jit(solution)/shard_map/ppermute | solution.py:54
  12.8 1.6 %collective-permute-start.3 = (f32[2,4,8,128]{3,2,1,0:T(8,128)S(1)}, f32[2,4,8,128]{3,2,1,0:T(8,128)S(1)}, u32[]{:S(2)}, u32[]{:S(2)}) collective-permute-start(f32[2,4,8,128]{3,2,1,0:T(8,128)S(1)} %get-tuple-element.55), channel_id=1, source_target_pairs={{0,12},{4,8},{8,4},{12,0},{1,13},{5,9},{9,5},{13,1},{2,14},{6,10},... | collective-permute-start | bytes 98312 | tf_op jit(solution)/shard_map/ppermute | solution.py:54
  14.4 1.8 %collective-permute-done.3.refs_1_.refs_3_ = f32[2,4,8,128]{3,2,1,0:T(8,128)S(1)} collective-permute-done((f32[2,4,8,128]{3,2,1,0:T(8,128)S(1)}, f32[2,4,8,128]{3,2,1,0:T(8,128)S(1)}, u32[]{:S(2)}, u32[]{:S(2)}) %collective-permute-start.3) | collective-permute-done | bytes 32800 | tf_op jit(solution)/shard_map/ppermute | solution.py:54
  16.2 1.6 %collective-permute-start.4 = (f32[2,4,4,8,128]{4,3,2,1,0:T(8,128)S(1)}, f32[2,4,4,8,128]{4,3,2,1,0:T(8,128)S(1)}, u32[]{:S(2)}, u32[]{:S(2)}) collective-permute-start(f32[2,4,4,8,128]{4,3,2,1,0:T(8,128)S(1)} %pack_x.1), channel_id=1, source_target_pairs={{0,16},{16,0},{1,17},{17,1},{2,18},{18,2},{3,19},{19,3},{4,20},{20... | collective-permute-start | bytes 393224 | tf_op jit(solution)/shard_map/ppermute | solution.py:52
  17.7 7.3 %density_own.1 = (bf16[8,1024,128]{2,1,0:T(8,128)(2,1)S(1)}, bf16[8,1024,128]{2,1,0:T(8,128)(2,1)S(1)}, f32[8,1024,128]{2,1,0:T(8,128)S(1)}, f32[8,32,128]{2,1,0...) custom-call(f32[2,2,2,8,128]{4,3,2,1,0:T(8,128)S(1)} %get-tuple-element.46.own_ref), custom_call_target="tpu_custom_call" | custom-call | tf_op jit(solution)/shard_map/density_own/pallas_call | solution.py:287
  25.0 5.7 %density_z.1 = (bf16[8,512,128]{2,1,0:T(8,128)(2,1)S(1)}, bf16[8,512,128]{2,1,0:T(8,128)(2,1)S(1)}, f32[8,512,128]{2,1,0:T(8,128)S(1)}, f32[8,32,128]{2,1,0:T(8,128)S(1)}, f32[8,8,128]{2,1,0:T(8,128)S(1)}) custom-call(f32[2,2,8,128]{3,2,1,0:T(8,128)S(1)} %collective-permute-done.refs_0_, f32[2,2,8,128]{3,2,1,0:T(8,128)S(1)} %collective-permute-done.1.refs_1_, ...), custom_call_target="tpu_custom_call" | custom-call | tf_op jit(solution)/shard_map/density_z/pallas_call | solution.py:287
  30.7 8.5 %density_y.1 = (bf16[8,768,128]{2,1,0:T(8,128)(2,1)S(1)}, bf16[8,768,128]{2,1,0:T(8,128)(2,1)S(1)}, f32[8,768,128]{2,1,0:T(8,128)S(1)}, f32[8,32,128]{2,1,0:T(8,128)S(1)}, f32[8,8,128]{2,1,0:T(8,128)S(1)}) custom-call(f32[2,4,8,128]{3,2,1,0:T(8,128)S(1)} %collective-permute-done.2.refs_0_.refs_2_, ...), custom_call_target="tpu_custom_call" | custom-call | tf_op jit(solution)/shard_map/density_y/pallas_call | solution.py:287
  39.2 13.6 %density_x.1 = (bf16[8,1152,128]{2,1,0:T(8,128)(2,1)S(1)}, bf16[8,1152,128]{2,1,0:T(8,128)(2,1)S(1)}, f32[8,1152,128]{2,1,0:T(8,128)S(1)}, f32[8,32,128]{2,1,0:T(8,128)S(1)}, f32[8,8,128]{2,1,0:T(8,128)S(1)}) custom-call(f32[2,4,4,8,128]{4,3,2,1,0:T(8,128)S(1)} %collective-permute-done.4.refs_0_, bf16[8,64,256]{2,1,0:T(8,128)(2,1)S(1)} %get-tuple-element.51.refs_2_.refs_1_), custom_call_target="tpu_custom_call" | custom-call | tf_op jit(solution)/shard_map/density_x/pallas_call | solution.py:287
  54.2 1.3 %pressure.1 = (f32[2,2,2,2,128]{4,3,2,1,0:T(2,128)S(1)}, f32[2,2,2,128]{3,2,1,0:T(2,128)}, f32[8,8,128]{2,1,0:T(8,128)S(1)}, f32[2,2,2,128]{3,2,1,0:T(2,128)S(1)}, f32[2,2,2,128]{3,2,1,0:T(2,128)S(1)}) custom-call(s32[2,2,2]{2,1,0:T(2,128)S(1)} %copy-done.1, f32[2,2,2,128]{3,2,1,0:T(2,128)S(1)} %copy-done.5, ...), custom_call_target="tpu_custom_call" | custom-call | tf_op jit(solution)/shard_map/pressure/pallas_call | solution.py:287
  55.5 2.5 %collective-permute-start.6 = (f32[2,2,2,128]{3,2,1,0:T(2,128)S(1)}, f32[2,2,2,128]{3,2,1,0:T(2,128)S(1)}, u32[]{:S(2)}, u32[]{:S(2)}) collective-permute-start(f32[2,2,2,128]{3,2,1,0:T(2,128)S(1)} %get-tuple-element.69), channel_id=1, source_target_pairs={{0,3},{1,2},{2,1},{3,0},{4,7},{5,6},{6,5},{7,4},{8,11},{9,10},{10,... | collective-permute-start | bytes 12296 | tf_op jit(solution)/shard_map/ppermute | solution.py:54
  58.0 1.1 %collective-permute-done.5.refs_2_.refs_0_ = f32[2,2,2,128]{3,2,1,0:T(2,128)S(1)} collective-permute-done((f32[2,2,2,128]{3,2,1,0:T(2,128)S(1)}, f32[2,2,2,128]{3,2,1,0:T(2,128)S(1)}, u32[]{:S(2)}, u32[]{:S(2)}) %collective-permute-start.5) | collective-permute-done | bytes 4128 | tf_op jit(solution)/shard_map/ppermute | solution.py:54
  59.1 1.8 %collective-permute-done.6.refs_3_.refs_1_ = f32[2,2,2,128]{3,2,1,0:T(2,128)S(1)} collective-permute-done((f32[2,2,2,128]{3,2,1,0:T(2,128)S(1)}, f32[2,2,2,128]{3,2,1,0:T(2,128)S(1)}, u32[]{:S(2)}, u32[]{:S(2)}) %collective-permute-start.6) | collective-permute-done | bytes 4128 | tf_op jit(solution)/shard_map/ppermute | solution.py:54
  61.0 1.6 %collective-permute-start.8 = (f32[2,4,2,128]{3,2,1,0:T(2,128)S(1)}, f32[2,4,2,128]{3,2,1,0:T(2,128)S(1)}, u32[]{:S(2)}, u32[]{:S(2)}) collective-permute-start(f32[2,4,2,128]{3,2,1,0:T(2,128)S(1)} %get-tuple-element.76), channel_id=1, source_target_pairs={{0,12},{4,8},{8,4},{12,0},{1,13},{5,9},{9,5},{13,1},{2,14},{6,10},... | collective-permute-start | bytes 24584 | tf_op jit(solution)/shard_map/ppermute | solution.py:54
  62.6 1.5 %collective-permute-done.8.refs_3_ = f32[2,4,2,128]{3,2,1,0:T(2,128)S(1)} collective-permute-done((f32[2,4,2,128]{3,2,1,0:T(2,128)S(1)}, f32[2,4,2,128]{3,2,1,0:T(2,128)S(1)}, u32[]{:S(2)}, u32[]{:S(2)}) %collective-permute-start.8) | collective-permute-done | bytes 8224 | tf_op jit(solution)/shard_map/ppermute | solution.py:54
  64.8 5.1 %force_own.1 = (f32[8,48,128]{2,1,0:T(8,128)S(1)}, f32[8,16,128]{2,1,0:T(8,128)S(1)}) custom-call(f32[2,2,2,8,128]{4,3,2,1,0:T(8,128)S(1)} %get-tuple-element.46.own_ref, f32[2,2,2,2,128]{4,3,2,1,0:T(2,128)S(1)} %get-tuple-element.61.press_ref.refs_4_.own_ref.refs_2_, bf16[8,1024,128]{2,1,0:T(8,128)(2,1)S(1)} %get-tuple-element.63.ghi, ...), custom_call_target="tpu_custom_call" | custom-call | tf_op jit(solution)/shard_map/force_own/pallas_call | solution.py:287
  70.0 4.1 %force_z.1 = (f32[8,48,128]{2,1,0:T(8,128)S(1)}, f32[8,16,128]{2,1,0:T(8,128)S(1)}) custom-call(f32[2,2,8,128]{3,2,1,0:T(8,128)S(1)} %collective-permute-done.refs_0_, f32[2,2,8,128]{3,2,1,0:T(8,128)S(1)} %collective-permute-done.1.refs_1_, f32[2,2,2,128]{3,2,1,0:T(2,128)S(1)} %collective-permute-done.5.refs_2_.refs_0_, ...), custom_call_target="tpu_custom_call" | custom-call | tf_op jit(solution)/shard_map/force_z/pallas_call | solution.py:287
  74.1 6.3 %force_y.1 = (f32[8,48,128]{2,1,0:T(8,128)S(1)}, f32[8,16,128]{2,1,0:T(8,128)S(1)}) custom-call(f32[2,4,8,128]{3,2,1,0:T(8,128)S(1)} %collective-permute-done.2.refs_0_.refs_2_, f32[2,4,8,128]{3,2,1,0:T(8,128)S(1)} %collective-permute-done.3.refs_1_.refs_3_, f32[2,4,2,128]{3,2,1,0:T(2,128)S(1)} %collective-permute-done.7.refs_2_, ...), custom_call_target="tpu_custom_call" | custom-call | tf_op jit(solution)/shard_map/force_y/pallas_call | solution.py:287
  80.4 10.8 %force_x.1 = (f32[8,48,128]{2,1,0:T(8,128)S(1)}, f32[8,16,128]{2,1,0:T(8,128)S(1)}) custom-call(f32[2,4,4,8,128]{4,3,2,1,0:T(8,128)S(1)} %collective-permute-done.4.refs_0_, f32[2,4,4,2,128]{4,3,2,1,0:T(2,128)S(1)} %collective-permute-done.9.refs_1_, f32[2,2,2,2,128]{4,3,2,1,0:T(2,128)S(1)} %get-tuple-element.61.press_ref.refs_4_.own_ref.refs_2_, ...), custom_call_target="tpu_custom_call" | custom-call | tf_op jit(solution)/shard_map/force_x/pallas_call | solution.py:287
  91.2 1.3 %finish.1 = (f32[3,2,2,2,128]{4,3,2,1,0:T(2,128)}, f32[2,2,2,128]{3,2,1,0:T(2,128)}) custom-call(s32[2,2,2]{2,1,0:T(2,128)S(1)} %copy-done.2, f32[2,2,2,8,128]{4,3,2,1,0:T(8,128)S(1)} %get-tuple-element.46.own_ref, f32[2,2,2,2,128]{4,3,2,1,0:T(2,128)S(1)} %get-tuple-element.61.press_ref.refs_4_.own_ref.refs_2_, ...), custom_call_target="tpu_custom_call" | custom-call | tf_op jit(solution)/shard_map/finish/pallas_call | solution.py:287
  (25 shorter events, 3.5 us)
Async XLA Ops:
  0.6 0.7 copy-start
  1.3 0.7 copy-start.3
  2.0 0.7 copy-start.4
  2.7 0.7 copy-start.6
  4.0 5.6 %collective-permute-start = (f32[2,2,8,128]{3,2,1,0:T(8,128)S(1)}, f32[2,2,8,128]{3,2,1,0:T(8,128)S(1)}, u32[]{:S(2)}, u32[]{:S(2)}) collective-permute-start(f32[2,2,8,128]{3,2,1,0:T(8,128)S(1)} %get-tuple-element.49), channel_id=1, source_target_pairs={{0,1},{1,0},{2,3},{3,2},{4,5},{5,4},{6,7},{7,6},{8,9},{9,8},{10,11... | collective-permute-start | bytes 49160 | tf_op jit(solution)/shard_map/ppermute | solution.py:54
  7.1 5.5 %collective-permute-start.1 = (f32[2,2,8,128]{3,2,1,0:T(8,128)S(1)}, f32[2,2,8,128]{3,2,1,0:T(8,128)S(1)}, u32[]{:S(2)}, u32[]{:S(2)}) collective-permute-start(f32[2,2,8,128]{3,2,1,0:T(8,128)S(1)} %get-tuple-element.50), channel_id=1, source_target_pairs={{0,3},{1,2},{2,1},{3,0},{4,7},{5,6},{6,5},{7,4},{8,11},{9,10},{10,... | collective-permute-start | bytes 49160 | tf_op jit(solution)/shard_map/ppermute | solution.py:54
  12.7 1.7 %collective-permute-start.2 = (f32[2,4,8,128]{3,2,1,0:T(8,128)S(1)}, f32[2,4,8,128]{3,2,1,0:T(8,128)S(1)}, u32[]{:S(2)}, u32[]{:S(2)}) collective-permute-start(f32[2,4,8,128]{3,2,1,0:T(8,128)S(1)} %get-tuple-element.54), channel_id=1, source_target_pairs={{0,4},{4,0},{8,12},{12,8},{1,5},{5,1},{9,13},{13,9},{2,6},{6,2},{1... | collective-permute-start | bytes 98312 | tf_op jit(solution)/shard_map/ppermute | solution.py:54
  12.8 3.4 %collective-permute-start.3 = (f32[2,4,8,128]{3,2,1,0:T(8,128)S(1)}, f32[2,4,8,128]{3,2,1,0:T(8,128)S(1)}, u32[]{:S(2)}, u32[]{:S(2)}) collective-permute-start(f32[2,4,8,128]{3,2,1,0:T(8,128)S(1)} %get-tuple-element.55), channel_id=1, source_target_pairs={{0,12},{4,8},{8,4},{12,0},{1,13},{5,9},{9,5},{13,1},{2,14},{6,10},... | collective-permute-start | bytes 98312 | tf_op jit(solution)/shard_map/ppermute | solution.py:54
  16.2 23.0 %collective-permute-start.4 = (f32[2,4,4,8,128]{4,3,2,1,0:T(8,128)S(1)}, f32[2,4,4,8,128]{4,3,2,1,0:T(8,128)S(1)}, u32[]{:S(2)}, u32[]{:S(2)}) collective-permute-start(f32[2,4,4,8,128]{4,3,2,1,0:T(8,128)S(1)} %pack_x.1), channel_id=1, source_target_pairs={{0,16},{16,0},{1,17},{17,1},{2,18},{18,2},{3,19},{19,3},{4,20},{20... | collective-permute-start | bytes 393224 | tf_op jit(solution)/shard_map/ppermute | solution.py:52
  52.9 0.7 copy-start.1
  53.6 0.7 copy-start.5
  55.5 3.6 %collective-permute-start.5 = (f32[2,2,2,128]{3,2,1,0:T(2,128)S(1)}, f32[2,2,2,128]{3,2,1,0:T(2,128)S(1)}, u32[]{:S(2)}, u32[]{:S(2)}) collective-permute-start(f32[2,2,2,128]{3,2,1,0:T(2,128)S(1)} %get-tuple-element.68), channel_id=1, source_target_pairs={{0,1},{1,0},{2,3},{3,2},{4,5},{5,4},{6,7},{7,6},{8,9},{9,8},{10,11... | collective-permute-start | bytes 12296 | tf_op jit(solution)/shard_map/ppermute | solution.py:54
  55.5 5.4 %collective-permute-start.6 = (f32[2,2,2,128]{3,2,1,0:T(2,128)S(1)}, f32[2,2,2,128]{3,2,1,0:T(2,128)S(1)}, u32[]{:S(2)}, u32[]{:S(2)}) collective-permute-start(f32[2,2,2,128]{3,2,1,0:T(2,128)S(1)} %get-tuple-element.69), channel_id=1, source_target_pairs={{0,3},{1,2},{2,1},{3,0},{4,7},{5,6},{6,5},{7,4},{8,11},{9,10},{10,... | collective-permute-start | bytes 12296 | tf_op jit(solution)/shard_map/ppermute | solution.py:54
  60.9 1.7 %collective-permute-start.7 = (f32[2,4,2,128]{3,2,1,0:T(2,128)S(1)}, f32[2,4,2,128]{3,2,1,0:T(2,128)S(1)}, u32[]{:S(2)}, u32[]{:S(2)}) collective-permute-start(f32[2,4,2,128]{3,2,1,0:T(2,128)S(1)} %get-tuple-element.75), channel_id=1, source_target_pairs={{0,4},{4,0},{8,12},{12,8},{1,5},{5,1},{9,13},{13,9},{2,6},{6,2},{1... | collective-permute-start | bytes 24584 | tf_op jit(solution)/shard_map/ppermute | solution.py:54
  61.0 3.1 %collective-permute-start.8 = (f32[2,4,2,128]{3,2,1,0:T(2,128)S(1)}, f32[2,4,2,128]{3,2,1,0:T(2,128)S(1)}, u32[]{:S(2)}, u32[]{:S(2)}) collective-permute-start(f32[2,4,2,128]{3,2,1,0:T(2,128)S(1)} %get-tuple-element.76), channel_id=1, source_target_pairs={{0,12},{4,8},{8,4},{12,0},{1,13},{5,9},{9,5},{13,1},{2,14},{6,10},... | collective-permute-start | bytes 24584 | tf_op jit(solution)/shard_map/ppermute | solution.py:54
  64.2 16.2 %collective-permute-start.9 = (f32[2,4,4,2,128]{4,3,2,1,0:T(2,128)S(1)}, f32[2,4,4,2,128]{4,3,2,1,0:T(2,128)S(1)}, u32[]{:S(2)}, u32[]{:S(2)}) collective-permute-start(f32[2,4,4,2,128]{4,3,2,1,0:T(2,128)S(1)} %pack_press_x.1), channel_id=1, source_target_pairs={{0,16},{16,0},{1,17},{17,1},{2,18},{18,2},{3,19},{19,3},{4,20},{20... | collective-permute-start | bytes 98312 | tf_op jit(solution)/shard_map/ppermute | solution.py:52
  80.4 10.8 %copy-start.2 = (s32[2,2,2]{2,1,0:T(2,128)S(1)}, s32[2,2,2]{2,1,0:T(2,128)}, u32[]{:S(2)}) copy-start(s32[2,2,2]{2,1,0:T(2,128)} %counts_ref.5) | copy-start | bytes 100
where the time goes:
time: 92.9 us; the launch traced here: 92.5 us
  Pallas kernels  64.6 us (70%)
  starting transfers between devices  13.6 us (15%)
  waiting for transfers between devices  9.31 us (10%)
  local copies, waits for them, and re-layouts  4.15 us (4%)
    pallas_call x15, Pallas kernels, call(): pl.pallas_call(body, out_shape=tuple(outs), in_specs=specs or [vmem] * le...  64.6 us
    ppermute x4, starting transfers between devices, exchanged(): lax.ppermute(sends[1], axis, second)  8.18 us
    ppermute x4, waiting for transfers between devices, exchanged(): lax.ppermute(sends[1], axis, second)  8.16 us
    unnamed x14, local copies, waits for them, and re-layouts  4.15 us
    ppermute x4, starting transfers between devices, exchanged(): lax.ppermute(sends[0], axis, first)  3.26 us
    ppermute x2, starting transfers between devices, exchanged(): both = lax.ppermute(sends, axis, first)  2.19 us
  transfers between devices with their start and end apart: 10, of which 5 were waited for; matrix products, arithmetic and copies ran while one was open for 0% of the time, Pallas kernels for 40%

commit v1 on v0

--- a/solution.py
+++ b/solution.py
@@ -14,6 +14,7 @@
 tile_rows = 8
 feature_rows = 64
 tiny = 1e-12
+together = 2
 
 vmem = pl.BlockSpec(memory_space=pltpu.VMEM)
 smem = pl.BlockSpec(memory_space=pltpu.SMEM)
@@ -116,7 +117,8 @@
     w1, w2, _ = split3(weighted)
     m1, m2, _ = split3(mass)
     extra = rows_of(m1, m2)
-    return jnp.concatenate([w1, w2, extra, jnp.zeros_like(extra)], 0).astype(bf16)
+    left = jnp.concatenate([w1, w2, extra, jnp.zeros_like(extra)], 0).astype(bf16)
+    return jnp.concatenate([left, left], 1)
 
 
 def picker(first_row):
@@ -132,33 +134,55 @@
     columns[at] = mass_columns(table, mass)
 
 
-def density_pairs(own, cells, near, feats, masses, columns, ghi, glo, visc, sums, weighted):
-    def one(c, _):
-        right = own[c]
-        total = jnp.zeros((tile_rows, 128), f32)
-        picks = near(c)
-        for k, n in enumerate(picks):
-            both = jnp.dot(feats[n], right, preferred_element_type=f32)
+def pipelined(tiles, stages):
+    for step in range(len(tiles) + len(stages) - 1):
+        for lag, stage in enumerate(stages):
+            if 0 <= step - lag < len(tiles):
+                stage(*tiles[step - lag])
+
+
+def over_cells(cells, body):
+    lax.fori_loop(0, cells // together, lambda i, _: body([i * together + j for j in range(together)]), 0)
+
+
+def density_pairs(own, cells, near, feats, masses, columns, slopes, visc, sums, weighted):
+    def some(group):
+        both, total, sofar = {}, {}, {}
+        tiles = [(j, k) for j, c in enumerate(group) for k in range(len(near(c)))]
+        picks = [near(c) for c in group]
+
+        def geometry(j, k):
+            both[j, k] = jnp.dot(feats[picks[j][k]], own[group[j]], preferred_element_type=f32)
+
+        def terms(j, k):
+            c, n = group[j], picks[j][k]
+            pair = both.pop((j, k))
             for r in range(0, 128, 16):
-                dist = jnp.maximum(both[r : r + 16, :128], tiny)
-                run = both[r : r + 16, 128:]
+                dist = jnp.maximum(pair[r : r + 16, :128], tiny)
+                run = pair[r : r + 16, 128:]
                 q = dist * lax.rsqrt(dist)
                 fall = jnp.maximum(1.0 - q, 0.0)
                 g = fall * fall * fall
                 part = g * q * masses[n, r : r + 16]
-                total = total + part[:8] + part[8:]
+                part = part[:8] + part[8:]
+                total[j] = part if j not in total else total[j] + part
                 high = g.astype(bf16)
-                ghi[c, k * 128 + r : k * 128 + r + 16] = high
-                glo[c, k * 128 + r : k * 128 + r + 16] = (g - high.astype(f32)).astype(bf16)
-                visc[c, k * 128 + r : k * 128 + r + 16] = g * jnp.minimum(run, 0.0) * (1.0 / (dist + 0.01))
-        left = jnp.concatenate([columns[n] for n in picks], 1)
-        sums[c] = jnp.dot(left, ghi[c], preferred_element_type=f32) + jnp.dot(
-            left, glo[c], preferred_element_type=f32
-        )
-        weighted[c] = total
+                slopes[c, k, r : r + 16] = high
+                slopes[c, k, 128 + r : 128 + r + 16] = (g - high.astype(f32)).astype(bf16)
+                visc[c, k, r : r + 16] = g * jnp.minimum(run, 0.0) * (1.0 / (dist + 0.01))
+
+        def reduce(j, k):
+            c, n = group[j], picks[j][k]
+            part = jnp.dot(columns[n], slopes[c, k], preferred_element_type=f32)
+            sofar[j] = part if j not in sofar else sofar[j] + part
+            if k == len(picks[j]) - 1:
+                sums[c] = sofar[j]
+                weighted[c] = total[j]
+
+        pipelined(tiles, (geometry, terms, reduce))
         return 0
 
-    lax.fori_loop(0, cells, one, 0)
+    over_cells(cells, some)
 
 
 def prepare_force(tile, offsets, press, at, rhos, columns, gradients):
@@ -171,38 +195,49 @@
     m1, m2, _ = split3(mass)
     w1, w2, _ = split3(weight * mass)
     extra = rows_of(m1, m2, w1, w2)
-    columns[at] = jnp.concatenate([h1, h2, s1, s2, extra, jnp.zeros_like(extra)], 0).astype(bf16)
+    left = jnp.concatenate([h1, h2, s1, s2, extra, jnp.zeros_like(extra)], 0).astype(bf16)
+    columns[at] = jnp.concatenate([left, left], 1)
     light = (mass / rho) * jnp.where(row_ids() < 3, table, 1.0)
     l1, l2, _ = split3(light)
-    gradients[at] = jnp.concatenate([l1, l2], 0).astype(bf16)
+    left = jnp.concatenate([l1, l2], 0).astype(bf16)
+    gradients[at] = jnp.concatenate([left, left], 1)
     r1, r2, r3 = split3(rho)
     lanes = jnp.concatenate([rows_of(r1, r2, r3), jnp.zeros((tile_rows, 128), f32)], 0).T.astype(bf16)
     ids = lax.broadcasted_iota(jnp.int32, (16, 128), 0)
     rhos[at] = jnp.dot(lanes, jnp.where(ids < 3, 1.0, 0.0).astype(bf16), preferred_element_type=f32)
 
 
-def force_pairs(cells, near, press_row, rhos, columns, gradients, ghi, glo, visc, thi, tlo, sums, slopes):
-    def one(c, _):
-        picks = near(c)
-        mine = press_row(c)
-        for k, n in enumerate(picks):
+def force_pairs(cells, near, press_row, rhos, columns, gradients, slopes, visc, sums, pulls):
+    def some(group):
+        mixed, sofar, pulled = {}, {}, {}
+        picks = [near(c) for c in group]
+        mine = [press_row(c) for c in group]
+        tiles = [(j, k) for j, c in enumerate(group) for k in range(len(near(c)))]
+
+        def terms(j, k):
+            c, n = group[j], picks[j][k]
+            highs, lows = [], []
             for r in range(0, 128, 16):
-                at = slice(k * 128 + r, k * 128 + r + 16)
-                t = visc[c, at] * (1.0 / (rhos[n, r : r + 16] + mine))
+                t = visc[c, k, r : r + 16] * (1.0 / (rhos[n, r : r + 16] + mine[j]))
                 high = t.astype(bf16)
-                thi[at] = high
-                tlo[at] = (t - high.astype(f32)).astype(bf16)
-        left = jnp.concatenate([columns[n] for n in picks], 1)
-        sums[c] = jnp.dot(left, thi[...], preferred_element_type=f32) + jnp.dot(
-            left, tlo[...], preferred_element_type=f32
-        )
-        left = jnp.concatenate([gradients[n] for n in picks], 1)
-        slopes[c] = jnp.dot(left, ghi[c], preferred_element_type=f32) + jnp.dot(
-            left, glo[c], preferred_element_type=f32
-        )
+                highs.append(high)
+                lows.append((t - high.astype(f32)).astype(bf16))
+            mixed[j, k] = jnp.concatenate(highs + lows, 0)
+
+        def reduce(j, k):
+            c, n = group[j], picks[j][k]
+            part = jnp.dot(columns[n], mixed.pop((j, k)), preferred_element_type=f32)
+            pull = jnp.dot(gradients[n], slopes[c, k], preferred_element_type=f32)
+            sofar[j] = part if j not in sofar else sofar[j] + part
+            pulled[j] = pull if j not in pulled else pulled[j] + pull
+            if k == len(picks[j]) - 1:
+                sums[c] = sofar[j]
+                pulls[c] = pulled[j]
+
+        pipelined(tiles, (terms, reduce))
         return 0
 
-    lax.fori_loop(0, cells, one, 0)
+    over_cells(cells, some)
 
 
 def parts_of(c):
@@ -269,15 +304,14 @@
     return [
         pltpu.VMEM((entries, 128, feature_rows), bf16),
         pltpu.VMEM((entries, 128, 128), f32),
-        pltpu.VMEM((entries, 32, 128), bf16),
+        pltpu.VMEM((entries, 32, 256), bf16),
     ]
 
 
 def pair_outputs(count):
     return [
-        shaped(8, count * 128, 128, kind=bf16),
-        shaped(8, count * 128, 128, kind=bf16),
-        shaped(8, count * 128, 128),
+        shaped(8, count, 256, 128, kind=bf16),
+        shaped(8, count, 128, 128),
         shaped(8, 32, 128),
         shaped(8, tile_rows, 128),
     ]
@@ -382,7 +416,7 @@
 def density_own(own):
     entries, near, place, count = groups["own"]
 
-    def body(own_ref, ghi, glo, visc, sums, weighted, table_ref, feats, masses, columns):
+    def body(own_ref, slopes, visc, sums, weighted, table_ref, feats, masses, columns):
         def one(c, _):
             x, y, z = parts_of(c)
             tile = own_ref[x, y, z]
@@ -392,8 +426,8 @@
             table_ref[c] = own_features(table)
             return 0
 
-        lax.fori_loop(0, 8, one, 0)
-        density_pairs(table_ref, 8, near, feats, masses, columns, ghi, glo, visc, sums, weighted)
+        lax.fori_loop(0, 8, one, 0, unroll=4)
+        density_pairs(table_ref, 8, near, feats, masses, columns, slopes, visc, sums, weighted)
 
     outs = pair_outputs(count) + [shaped(8, feature_rows, 256, kind=bf16)]
     return call(body, outs, (own,), scratch=scratch_density(entries), name="density_own")
@@ -406,7 +440,7 @@
 
     def body(*refs):
         got, own_ref = refs[:n], refs[n]
-        ghi, glo, visc, sums, weighted, feats, masses, columns = refs[n + 1 :]
+        slopes, visc, sums, weighted, feats, masses, columns = refs[n + 1 :]
         before = first_gives_before(axis)
         for side in range(2):
 
@@ -416,8 +450,8 @@
                 prepare(tile, offsets_of(place(at)), at, feats, masses, columns)
                 return 0
 
-            lax.fori_loop(0, half, one, 0)
-        density_pairs(own_ref, 8, near, feats, masses, columns, ghi, glo, visc, sums, weighted)
+            lax.fori_loop(0, half, one, 0, unroll=4)
+        density_pairs(own_ref, 8, near, feats, masses, columns, slopes, visc, sums, weighted)
 
     return call(
         body,
@@ -470,13 +504,11 @@
     return call(body, outs, operands, specs=specs, name="pressure", limit=8)
 
 
-def scratch_force(entries, count):
+def scratch_force(entries):
     return [
         pltpu.VMEM((entries, 128, 128), f32),
-        pltpu.VMEM((entries, 48, 128), bf16),
-        pltpu.VMEM((entries, 16, 128), bf16),
-        pltpu.VMEM((count * 128, 128), bf16),
-        pltpu.VMEM((count * 128, 128), bf16),
+        pltpu.VMEM((entries, 48, 256), bf16),
+        pltpu.VMEM((entries, 16, 256), bf16),
     ]
 
 
@@ -487,7 +519,7 @@
 def force_own(own, press, kept):
     entries, near, place, count = groups["own"]
 
-    def body(own_ref, press_ref, ghi, glo, visc, sums, slopes, rhos, columns, gradients, thi, tlo):
+    def body(own_ref, press_ref, slopes, visc, sums, pulls, rhos, columns, gradients):
         def one(c, _):
             x, y, z = parts_of(c)
             prepare_force(
@@ -495,19 +527,19 @@
             )
             return 0
 
-        lax.fori_loop(0, 8, one, 0)
+        lax.fori_loop(0, 8, one, 0, unroll=4)
 
         def mine(c):
             x, y, z = parts_of(c)
             return press_ref[x, y, z, 0:1]
 
-        force_pairs(8, near, mine, rhos, columns, gradients, ghi, glo, visc, thi, tlo, sums, slopes)
+        force_pairs(8, near, mine, rhos, columns, gradients, slopes, visc, sums, pulls)
 
     return call(
         body,
         force_outputs(),
         (own, press, *kept),
-        scratch=scratch_force(entries, count),
+        scratch=scratch_force(entries),
         name="force_own",
     )
 
@@ -519,7 +551,7 @@
 
     def body(*refs):
         got, got_press, press_ref = refs[:n], refs[n : 2 * n], refs[2 * n]
-        ghi, glo, visc, sums, slopes, rhos, columns, gradients, thi, tlo = refs[2 * n + 1 :]
+        slopes, visc, sums, pulls, rhos, columns, gradients = refs[2 * n + 1 :]
         before = first_gives_before(axis)
         for side in range(2):
 
@@ -530,19 +562,19 @@
                 prepare_force(tile, offsets_of(place(at)), fields, at, rhos, columns, gradients)
                 return 0
 
-            lax.fori_loop(0, half, one, 0)
+            lax.fori_loop(0, half, one, 0, unroll=4)
 
         def mine(c):
             x, y, z = parts_of(c)
             return press_ref[x, y, z, 0:1]
 
-        force_pairs(8, near, mine, rhos, columns, gradients, ghi, glo, visc, thi, tlo, sums, slopes)
+        force_pairs(8, near, mine, rhos, columns, gradients, slopes, visc, sums, pulls)
 
     return call(
         body,
         force_outputs(),
         (*received, *press_received, press, *kept),
-        scratch=scratch_force(entries, count),
+        scratch=scratch_force(entries),
         name="force_" + group,
     )
 

time: 92.9 us -> 65.7 us (0.71)
  Pallas kernels: 64.6 us -> 37.5 us
    pallas_call x15, Pallas kernels: 64.6 us -> 37.5 us  [call(): pl.pallas_call(body, out_shape=tuple(outs), in_specs=specs or [vmem] * le...]
  transfers between devices with their start and end apart: 10 -> 10, of which waited for: 5 -> 5; matrix products, arithmetic and copies ran while one was open for 0% -> 0% of each run, Pallas kernels for 40% -> 33%
where the time goes in v1:
time: 65.7 us; the launch traced here: 65.3 us
  Pallas kernels  37.5 us (57%)
  starting transfers between devices  13.6 us (21%)
  waiting for transfers between devices  9.31 us (14%)
  local copies, waits for them, and re-layouts  4.16 us (6%)
  between operations  0.76 us (1%)
    pallas_call x15, Pallas kernels, call(): pl.pallas_call(body, out_shape=tuple(outs), in_specs=specs or [vmem] * le...  37.5 us
    ppermute x4, starting transfers between devices, exchanged(): lax.ppermute(sends[1], axis, second)  8.18 us
    ppermute x4, waiting for transfers between devices, exchanged(): lax.ppermute(sends[1], axis, second)  8.17 us
    unnamed x14, local copies, waits for them, and re-layouts  4.16 us
    ppermute x4, starting transfers between devices, exchanged(): lax.ppermute(sends[0], axis, first)  3.26 us
    ppermute x2, starting transfers between devices, exchanged(): both = lax.ppermute(sends, axis, first)  2.15 us
  transfers between devices with their start and end apart: 10, of which 5 were waited for; matrix products, arithmetic and copies ran while one was open for 0% of the time, Pallas kernels for 33%

profile of v1, /device:TPU:0, one launch (start us, length us, event | category | flops | bytes accessed | tf_op | source)
XLA Modules:
  0.0 65.3 jit_solution(18111437228612120964)
XLA Ops:
  1.3 0.7 %copy-done.3 = f32[3,2,2,2,128]{4,3,2,1,0:T(2,128)S(1)} copy-done((f32[3,2,2,2,128]{4,3,2,1,0:T(2,128)S(1)}, f32[3,2,2,2,128]{4,3,2,1,0:T(2,128)}, u32[]{:S(2)}) %copy-start.3) | copy-done | bytes 12312
  2.0 0.7 %copy-done.4 = f32[3,2,2,2,128]{4,3,2,1,0:T(2,128)S(1)} copy-done((f32[3,2,2,2,128]{4,3,2,1,0:T(2,128)S(1)}, f32[3,2,2,2,128]{4,3,2,1,0:T(2,128)}, u32[]{:S(2)}) %copy-start.4) | copy-done | bytes 12312
  4.0 3.1 %collective-permute-start = (f32[2,2,8,128]{3,2,1,0:T(8,128)S(1)}, f32[2,2,8,128]{3,2,1,0:T(8,128)S(1)}, u32[]{:S(2)}, u32[]{:S(2)}) collective-permute-start(f32[2,2,8,128]{3,2,1,0:T(8,128)S(1)} %get-tuple-element.45), channel_id=1, source_target_pairs={{0,1},{1,0},{2,3},{3,2},{4,5},{5,4},{6,7},{7,6},{8,9},{9,8},{10,11... | collective-permute-start | bytes 49160 | tf_op jit(solution)/shard_map/ppermute | solution.py:55
  7.1 2.5 %collective-permute-start.1 = (f32[2,2,8,128]{3,2,1,0:T(8,128)S(1)}, f32[2,2,8,128]{3,2,1,0:T(8,128)S(1)}, u32[]{:S(2)}, u32[]{:S(2)}) collective-permute-start(f32[2,2,8,128]{3,2,1,0:T(8,128)S(1)} %get-tuple-element.46), channel_id=1, source_target_pairs={{0,3},{1,2},{2,1},{3,0},{4,7},{5,6},{6,5},{7,4},{8,11},{9,10},{10,... | collective-permute-start | bytes 49160 | tf_op jit(solution)/shard_map/ppermute | solution.py:55
  9.6 3.1 %collective-permute-done.1.refs_1_ = f32[2,2,8,128]{3,2,1,0:T(8,128)S(1)} collective-permute-done((f32[2,2,8,128]{3,2,1,0:T(8,128)S(1)}, f32[2,2,8,128]{3,2,1,0:T(8,128)S(1)}, u32[]{:S(2)}, u32[]{:S(2)}) %collective-permute-start.1) | collective-permute-done | bytes 16416 | tf_op jit(solution)/shard_map/ppermute | solution.py:55
  12.8 1.6 %collective-permute-start.3 = (f32[2,4,8,128]{3,2,1,0:T(8,128)S(1)}, f32[2,4,8,128]{3,2,1,0:T(8,128)S(1)}, u32[]{:S(2)}, u32[]{:S(2)}) collective-permute-start(f32[2,4,8,128]{3,2,1,0:T(8,128)S(1)} %get-tuple-element.51), channel_id=1, source_target_pairs={{0,12},{4,8},{8,4},{12,0},{1,13},{5,9},{9,5},{13,1},{2,14},{6,10},... | collective-permute-start | bytes 98312 | tf_op jit(solution)/shard_map/ppermute | solution.py:55
  14.4 1.8 %collective-permute-done.3.refs_1_.refs_3_ = f32[2,4,8,128]{3,2,1,0:T(8,128)S(1)} collective-permute-done((f32[2,4,8,128]{3,2,1,0:T(8,128)S(1)}, f32[2,4,8,128]{3,2,1,0:T(8,128)S(1)}, u32[]{:S(2)}, u32[]{:S(2)}) %collective-permute-start.3) | collective-permute-done | bytes 32800 | tf_op jit(solution)/shard_map/ppermute | solution.py:55
  16.2 1.6 %collective-permute-start.4 = (f32[2,4,4,8,128]{4,3,2,1,0:T(8,128)S(1)}, f32[2,4,4,8,128]{4,3,2,1,0:T(8,128)S(1)}, u32[]{:S(2)}, u32[]{:S(2)}) collective-permute-start(f32[2,4,4,8,128]{4,3,2,1,0:T(8,128)S(1)} %pack_x.1), channel_id=1, source_target_pairs={{0,16},{16,0},{1,17},{17,1},{2,18},{18,2},{3,19},{19,3},{4,20},{20... | collective-permute-start | bytes 393224 | tf_op jit(solution)/shard_map/ppermute | solution.py:53
  17.7 6.2 %density_own.1 = (bf16[8,8,256,128]{3,2,1,0:T(8,128)(2,1)S(1)}, f32[8,8,128,128]{3,2,1,0:T(8,128)S(1)}, f32[8,32,128]{2,1,0:T(8,128)S(1)}, f32[8,8,128]{2,1,0:T(8,128)S(1)}, bf16[8,64,256]{2,1,0:T(8,128)(2,1)S(1)}) custom-call(f32[2,2,2,8,128]{4,3,2,1,0:T(8,128)S(1)} %get-tuple-element.42.own_ref), custom_call_target="tpu_custom_call" | custom-call | tf_op jit(solution)/shard_map/density_own/pallas_call | solution.py:321
  24.0 3.3 %density_z.1 = (bf16[8,4,256,128]{3,2,1,0:T(8,128)(2,1)S(1)}, f32[8,4,128,128]{3,2,1,0:T(8,128)S(1)}, f32[8,32,128]{2,1,0:T(8,128)S(1)}, f32[8,8,128]{2,1,0:T(8,128)S(1)}) custom-call(f32[2,2,8,128]{3,2,1,0:T(8,128)S(1)} %collective-permute-done.refs_0_, f32[2,2,8,128]{3,2,1,0:T(8,128)S(1)} %collective-permute-done.1.refs_1_, ...), custom_call_target="tpu_custom_call" | custom-call | tf_op jit(solution)/shard_map/density_z/pallas_call | solution.py:321
  27.3 5.5 %density_y.1 = (bf16[8,6,256,128]{3,2,1,0:T(8,128)(2,1)S(1)}, f32[8,6,128,128]{3,2,1,0:T(8,128)S(1)}, f32[8,32,128]{2,1,0:T(8,128)S(1)}, f32[8,8,128]{2,1,0:T(8,128)S(1)}) custom-call(f32[2,4,8,128]{3,2,1,0:T(8,128)S(1)} %collective-permute-done.2.refs_0_.refs_2_, f32[2,4,8,128]{3,2,1,0:T(8,128)S(1)} %collective-permute-done.3.refs_1_.refs_3_, ...), custom_call_target="tpu_custom_call" | custom-call | tf_op jit(solution)/shard_map/density_y/pallas_call | solution.py:321
  32.8 8.7 %density_x.1 = (bf16[8,9,256,128]{3,2,1,0:T(8,128)(2,1)S(1)}, f32[8,9,128,128]{3,2,1,0:T(8,128)S(1)}, f32[8,32,128]{2,1,0:T(8,128)S(1)}, f32[8,8,128]{2,1,0:T(8,128)S(1)}) custom-call(f32[2,4,4,8,128]{4,3,2,1,0:T(8,128)S(1)} %collective-permute-done.4.refs_0_, bf16[8,64,256]{2,1,0:T(8,128)(2,1)S(1)} %get-tuple-element.47.refs_2_.refs_1_), custom_call_target="tpu_custom_call" | custom-call | tf_op jit(solution)/shard_map/density_x/pallas_call | solution.py:321
  41.5 0.7 %copy-done.1 = s32[2,2,2]{2,1,0:T(2,128)S(1)} copy-done((s32[2,2,2]{2,1,0:T(2,128)S(1)}, s32[2,2,2]{2,1,0:T(2,128)}, u32[]{:S(2)}) %copy-start.1) | copy-done | bytes 56
  42.9 1.3 %pressure.1 = (f32[2,2,2,2,128]{4,3,2,1,0:T(2,128)S(1)}, f32[2,2,2,128]{3,2,1,0:T(2,128)}, f32[8,8,128]{2,1,0:T(8,128)S(1)}, f32[2,2,2,128]{3,2,1,0:T(2,128)S(1)}, f32[2,2,2,128]{3,2,1,0:T(2,128)S(1)}) custom-call(s32[2,2,2]{2,1,0:T(2,128)S(1)} %copy-done.1, f32[2,2,2,128]{3,2,1,0:T(2,128)S(1)} %copy-done.5, ...), custom_call_target="tpu_custom_call" | custom-call | tf_op jit(solution)/shard_map/pressure/pallas_call | solution.py:321
  44.2 2.5 %collective-permute-start.6 = (f32[2,2,2,128]{3,2,1,0:T(2,128)S(1)}, f32[2,2,2,128]{3,2,1,0:T(2,128)S(1)}, u32[]{:S(2)}, u32[]{:S(2)}) collective-permute-start(f32[2,2,2,128]{3,2,1,0:T(2,128)S(1)} %get-tuple-element.64), channel_id=1, source_target_pairs={{0,3},{1,2},{2,1},{3,0},{4,7},{5,6},{6,5},{7,4},{8,11},{9,10},{10,... | collective-permute-start | bytes 12296 | tf_op jit(solution)/shard_map/ppermute | solution.py:55
  46.6 1.1 %collective-permute-done.5.refs_2_.refs_0_ = f32[2,2,2,128]{3,2,1,0:T(2,128)S(1)} collective-permute-done((f32[2,2,2,128]{3,2,1,0:T(2,128)S(1)}, f32[2,2,2,128]{3,2,1,0:T(2,128)S(1)}, u32[]{:S(2)}, u32[]{:S(2)}) %collective-permute-start.5) | collective-permute-done | bytes 4128 | tf_op jit(solution)/shard_map/ppermute | solution.py:55
  47.8 1.8 %collective-permute-done.6.refs_3_.refs_1_ = f32[2,2,2,128]{3,2,1,0:T(2,128)S(1)} collective-permute-done((f32[2,2,2,128]{3,2,1,0:T(2,128)S(1)}, f32[2,2,2,128]{3,2,1,0:T(2,128)S(1)}, u32[]{:S(2)}, u32[]{:S(2)}) %collective-permute-start.6) | collective-permute-done | bytes 4128 | tf_op jit(solution)/shard_map/ppermute | solution.py:55
  49.7 1.6 %collective-permute-start.8 = (f32[2,4,2,128]{3,2,1,0:T(2,128)S(1)}, f32[2,4,2,128]{3,2,1,0:T(2,128)S(1)}, u32[]{:S(2)}, u32[]{:S(2)}) collective-permute-start(f32[2,4,2,128]{3,2,1,0:T(2,128)S(1)} %get-tuple-element.70), channel_id=1, source_target_pairs={{0,12},{4,8},{8,4},{12,0},{1,13},{5,9},{9,5},{13,1},{2,14},{6,10},... | collective-permute-start | bytes 24584 | tf_op jit(solution)/shard_map/ppermute | solution.py:55
  51.3 1.5 %collective-permute-done.8.refs_3_ = f32[2,4,2,128]{3,2,1,0:T(2,128)S(1)} collective-permute-done((f32[2,4,2,128]{3,2,1,0:T(2,128)S(1)}, f32[2,4,2,128]{3,2,1,0:T(2,128)S(1)}, u32[]{:S(2)}, u32[]{:S(2)}) %collective-permute-start.8) | collective-permute-done | bytes 8224 | tf_op jit(solution)/shard_map/ppermute | solution.py:55
  53.4 2.3 %force_own.1 = (f32[8,48,128]{2,1,0:T(8,128)S(1)}, f32[8,16,128]{2,1,0:T(8,128)S(1)}) custom-call(f32[2,2,2,8,128]{4,3,2,1,0:T(8,128)S(1)} %get-tuple-element.42.own_ref, f32[2,2,2,2,128]{4,3,2,1,0:T(2,128)S(1)} %get-tuple-element.57.press_ref.refs_4_.own_ref.refs_2_, bf16[8,8,256,128]{3,2,1,0:T(8,128)(2,1)S(1)} %get-tuple-element.59.slopes, ...), custom_call_target="tpu_custom_call" | custom-call | tf_op jit(solution)/shard_map/force_own/pallas_call | solution.py:321
  55.7 1.5 %force_z.1 = (f32[8,48,128]{2,1,0:T(8,128)S(1)}, f32[8,16,128]{2,1,0:T(8,128)S(1)}) custom-call(f32[2,2,8,128]{3,2,1,0:T(8,128)S(1)} %collective-permute-done.refs_0_, f32[2,2,8,128]{3,2,1,0:T(8,128)S(1)} %collective-permute-done.1.refs_1_, f32[2,2,2,128]{3,2,1,0:T(2,128)S(1)} %collective-permute-done.5.refs_2_.refs_0_, ...), custom_call_target="tpu_custom_call" | custom-call | tf_op jit(solution)/shard_map/force_z/pallas_call | solution.py:321
  57.2 2.6 %force_y.1 = (f32[8,48,128]{2,1,0:T(8,128)S(1)}, f32[8,16,128]{2,1,0:T(8,128)S(1)}) custom-call(f32[2,4,8,128]{3,2,1,0:T(8,128)S(1)} %collective-permute-done.2.refs_0_.refs_2_, f32[2,4,8,128]{3,2,1,0:T(8,128)S(1)} %collective-permute-done.3.refs_1_.refs_3_, f32[2,4,2,128]{3,2,1,0:T(2,128)S(1)} %collective-permute-done.7.refs_2_, ...), custom_call_target="tpu_custom_call" | custom-call | tf_op jit(solution)/shard_map/force_y/pallas_call | solution.py:321
  59.8 4.2 %force_x.1 = (f32[8,48,128]{2,1,0:T(8,128)S(1)}, f32[8,16,128]{2,1,0:T(8,128)S(1)}) custom-call(f32[2,4,4,8,128]{4,3,2,1,0:T(8,128)S(1)} %collective-permute-done.4.refs_0_, f32[2,4,4,2,128]{4,3,2,1,0:T(2,128)S(1)} %collective-permute-done.9.refs_1_, f32[2,2,2,2,128]{4,3,2,1,0:T(2,128)S(1)} %get-tuple-element.57.press_ref.refs_4_.own_ref.refs_2_, ...), custom_call_target="tpu_custom_call" | custom-call | tf_op jit(solution)/shard_map/force_x/pallas_call | solution.py:321
  64.0 1.3 %finish.1 = (f32[3,2,2,2,128]{4,3,2,1,0:T(2,128)}, f32[2,2,2,128]{3,2,1,0:T(2,128)}) custom-call(s32[2,2,2]{2,1,0:T(2,128)S(1)} %copy-done.2, f32[2,2,2,8,128]{4,3,2,1,0:T(8,128)S(1)} %get-tuple-element.42.own_ref, f32[2,2,2,2,128]{4,3,2,1,0:T(2,128)S(1)} %get-tuple-element.57.press_ref.refs_4_.own_ref.refs_2_, ...), custom_call_target="tpu_custom_call" | custom-call | tf_op jit(solution)/shard_map/finish/pallas_call | solution.py:321
  (25 shorter events, 3.5 us)
Async XLA Ops:
  0.6 0.7 %copy-start = (s32[2,2,2]{2,1,0:T(2,128)S(1)}, s32[2,2,2]{2,1,0:T(2,128)}, u32[]{:S(2)}) copy-start(s32[2,2,2]{2,1,0:T(2,128)} %counts_ref.5) | copy-start | bytes 100
  1.3 0.7 %copy-start.3 = (f32[3,2,2,2,128]{4,3,2,1,0:T(2,128)S(1)}, f32[3,2,2,2,128]{4,3,2,1,0:T(2,128)}, u32[]{:S(2)}) copy-start(f32[3,2,2,2,128]{4,3,2,1,0:T(2,128)} %pos.1) | copy-start | bytes 36868
  2.0 0.7 %copy-start.4 = (f32[3,2,2,2,128]{4,3,2,1,0:T(2,128)S(1)}, f32[3,2,2,2,128]{4,3,2,1,0:T(2,128)}, u32[]{:S(2)}) copy-start(f32[3,2,2,2,128]{4,3,2,1,0:T(2,128)} %vel.1) | copy-start | bytes 36868
  2.7 0.7 %copy-start.6 = (f32[2,2,2,128]{3,2,1,0:T(2,128)S(1)}, f32[2,2,2,128]{3,2,1,0:T(2,128)}, u32[]{:S(2)}) copy-start(f32[2,2,2,128]{3,2,1,0:T(2,128)} %mass.1) | copy-start | bytes 12292
  4.0 5.6 %collective-permute-start = (f32[2,2,8,128]{3,2,1,0:T(8,128)S(1)}, f32[2,2,8,128]{3,2,1,0:T(8,128)S(1)}, u32[]{:S(2)}, u32[]{:S(2)}) collective-permute-start(f32[2,2,8,128]{3,2,1,0:T(8,128)S(1)} %get-tuple-element.45), channel_id=1, source_target_pairs={{0,1},{1,0},{2,3},{3,2},{4,5},{5,4},{6,7},{7,6},{8,9},{9,8},{10,11... | collective-permute-start | bytes 49160 | tf_op jit(solution)/shard_map/ppermute | solution.py:55
  7.1 5.5 %collective-permute-start.1 = (f32[2,2,8,128]{3,2,1,0:T(8,128)S(1)}, f32[2,2,8,128]{3,2,1,0:T(8,128)S(1)}, u32[]{:S(2)}, u32[]{:S(2)}) collective-permute-start(f32[2,2,8,128]{3,2,1,0:T(8,128)S(1)} %get-tuple-element.46), channel_id=1, source_target_pairs={{0,3},{1,2},{2,1},{3,0},{4,7},{5,6},{6,5},{7,4},{8,11},{9,10},{10,... | collective-permute-start | bytes 49160 | tf_op jit(solution)/shard_map/ppermute | solution.py:55
  12.7 1.7 %collective-permute-start.2 = (f32[2,4,8,128]{3,2,1,0:T(8,128)S(1)}, f32[2,4,8,128]{3,2,1,0:T(8,128)S(1)}, u32[]{:S(2)}, u32[]{:S(2)}) collective-permute-start(f32[2,4,8,128]{3,2,1,0:T(8,128)S(1)} %get-tuple-element.50), channel_id=1, source_target_pairs={{0,4},{4,0},{8,12},{12,8},{1,5},{5,1},{9,13},{13,9},{2,6},{6,2},{1... | collective-permute-start | bytes 98312 | tf_op jit(solution)/shard_map/ppermute | solution.py:55
  12.8 3.4 %collective-permute-start.3 = (f32[2,4,8,128]{3,2,1,0:T(8,128)S(1)}, f32[2,4,8,128]{3,2,1,0:T(8,128)S(1)}, u32[]{:S(2)}, u32[]{:S(2)}) collective-permute-start(f32[2,4,8,128]{3,2,1,0:T(8,128)S(1)} %get-tuple-element.51), channel_id=1, source_target_pairs={{0,12},{4,8},{8,4},{12,0},{1,13},{5,9},{9,5},{13,1},{2,14},{6,10},... | collective-permute-start | bytes 98312 | tf_op jit(solution)/shard_map/ppermute | solution.py:55
  16.2 16.6 %collective-permute-start.4 = (f32[2,4,4,8,128]{4,3,2,1,0:T(8,128)S(1)}, f32[2,4,4,8,128]{4,3,2,1,0:T(8,128)S(1)}, u32[]{:S(2)}, u32[]{:S(2)}) collective-permute-start(f32[2,4,4,8,128]{4,3,2,1,0:T(8,128)S(1)} %pack_x.1), channel_id=1, source_target_pairs={{0,16},{16,0},{1,17},{17,1},{2,18},{18,2},{3,19},{19,3},{4,20},{20... | collective-permute-start | bytes 393224 | tf_op jit(solution)/shard_map/ppermute | solution.py:53
  41.5 0.7 %copy-start.1 = (s32[2,2,2]{2,1,0:T(2,128)S(1)}, s32[2,2,2]{2,1,0:T(2,128)}, u32[]{:S(2)}) copy-start(s32[2,2,2]{2,1,0:T(2,128)} %counts_ref.5) | copy-start | bytes 100
  42.2 0.7 %copy-start.5 = (f32[2,2,2,128]{3,2,1,0:T(2,128)S(1)}, f32[2,2,2,128]{3,2,1,0:T(2,128)}, u32[]{:S(2)}) copy-start(f32[2,2,2,128]{3,2,1,0:T(2,128)} %alphas_ref.1) | copy-start | bytes 12292
  44.1 3.6 %collective-permute-start.5 = (f32[2,2,2,128]{3,2,1,0:T(2,128)S(1)}, f32[2,2,2,128]{3,2,1,0:T(2,128)S(1)}, u32[]{:S(2)}, u32[]{:S(2)}) collective-permute-start(f32[2,2,2,128]{3,2,1,0:T(2,128)S(1)} %get-tuple-element.63), channel_id=1, source_target_pairs={{0,1},{1,0},{2,3},{3,2},{4,5},{5,4},{6,7},{7,6},{8,9},{9,8},{10,11... | collective-permute-start | bytes 12296 | tf_op jit(solution)/shard_map/ppermute | solution.py:55
  44.2 5.4 %collective-permute-start.6 = (f32[2,2,2,128]{3,2,1,0:T(2,128)S(1)}, f32[2,2,2,128]{3,2,1,0:T(2,128)S(1)}, u32[]{:S(2)}, u32[]{:S(2)}) collective-permute-start(f32[2,2,2,128]{3,2,1,0:T(2,128)S(1)} %get-tuple-element.64), channel_id=1, source_target_pairs={{0,3},{1,2},{2,1},{3,0},{4,7},{5,6},{6,5},{7,4},{8,11},{9,10},{10,... | collective-permute-start | bytes 12296 | tf_op jit(solution)/shard_map/ppermute | solution.py:55
  49.6 1.7 %collective-permute-start.7 = (f32[2,4,2,128]{3,2,1,0:T(2,128)S(1)}, f32[2,4,2,128]{3,2,1,0:T(2,128)S(1)}, u32[]{:S(2)}, u32[]{:S(2)}) collective-permute-start(f32[2,4,2,128]{3,2,1,0:T(2,128)S(1)} %get-tuple-element.69), channel_id=1, source_target_pairs={{0,4},{4,0},{8,12},{12,8},{1,5},{5,1},{9,13},{13,9},{2,6},{6,2},{1... | collective-permute-start | bytes 24584 | tf_op jit(solution)/shard_map/ppermute | solution.py:55
  49.7 3.1 %collective-permute-start.8 = (f32[2,4,2,128]{3,2,1,0:T(2,128)S(1)}, f32[2,4,2,128]{3,2,1,0:T(2,128)S(1)}, u32[]{:S(2)}, u32[]{:S(2)}) collective-permute-start(f32[2,4,2,128]{3,2,1,0:T(2,128)S(1)} %get-tuple-element.70), channel_id=1, source_target_pairs={{0,12},{4,8},{8,4},{12,0},{1,13},{5,9},{9,5},{13,1},{2,14},{6,10},... | collective-permute-start | bytes 24584 | tf_op jit(solution)/shard_map/ppermute | solution.py:55
  52.8 7.0 %collective-permute-start.9 = (f32[2,4,4,2,128]{4,3,2,1,0:T(2,128)S(1)}, f32[2,4,4,2,128]{4,3,2,1,0:T(2,128)S(1)}, u32[]{:S(2)}, u32[]{:S(2)}) collective-permute-start(f32[2,4,4,2,128]{4,3,2,1,0:T(2,128)S(1)} %pack_press_x.1), channel_id=1, source_target_pairs={{0,16},{16,0},{1,17},{17,1},{2,18},{18,2},{3,19},{19,3},{4,20},{20... | collective-permute-start | bytes 98312 | tf_op jit(solution)/shard_map/ppermute | solution.py:53
  59.8 4.2 %copy-start.2 = (s32[2,2,2]{2,1,0:T(2,128)S(1)}, s32[2,2,2]{2,1,0:T(2,128)}, u32[]{:S(2)}) copy-start(s32[2,2,2]{2,1,0:T(2,128)} %counts_ref.5) | copy-start | bytes 100

commit v2 on v1

--- a/solution.py
+++ b/solution.py
@@ -7,17 +7,17 @@
 from jax.experimental.pallas import tpu as pltpu
 from jax.sharding import PartitionSpec as P
 
+
 f32 = jnp.float32
 bf16 = jnp.bfloat16
 kernel_norm = 21.0 / (2.0 * math.pi)
-axes = ("gx", "gy", "gz")
 tile_rows = 8
 feature_rows = 64
 tiny = 1e-12
-together = 2
+together = 4
+strip = 128
 
 vmem = pl.BlockSpec(memory_space=pltpu.VMEM)
-smem = pl.BlockSpec(memory_space=pltpu.SMEM)
 
 
 def shaped(*dims, kind=f32):
@@ -45,18 +45,6 @@
         first = [(i, (i + 1) % peers) for i in range(peers)]
         second = [(i, (i - 1) % peers) for i in range(peers)]
     return first, second
-
-
-def exchanged(axis, sends):
-    first, second = routes(axis)
-    if first == second:
-        both = lax.ppermute(sends, axis, first)
-        return (both,)
-    return lax.ppermute(sends[0], axis, first), lax.ppermute(sends[1], axis, second)
-
-
-def merged(axis, mesh_shape):
-    return mesh_shape[axis] == 2
 
 
 def split3(value):
@@ -141,6 +129,10 @@
                 stage(*tiles[step - lag])
 
 
+def idle(*tile):
+    pass
+
+
 def over_cells(cells, body):
     lax.fori_loop(0, cells // together, lambda i, _: body([i * together + j for j in range(together)]), 0)
 
@@ -148,18 +140,22 @@
 def density_pairs(own, cells, near, feats, masses, columns, slopes, visc, sums, weighted):
     def some(group):
         both, total, sofar = {}, {}, {}
-        tiles = [(j, k) for j, c in enumerate(group) for k in range(len(near(c)))]
         picks = [near(c) for c in group]
-
-        def geometry(j, k):
-            both[j, k] = jnp.dot(feats[picks[j][k]], own[group[j]], preferred_element_type=f32)
-
-        def terms(j, k):
+        tiles = [
+            (j, k, h) for j in range(len(group)) for k in range(len(picks[j])) for h in range(0, 128, strip)
+        ]
+
+        def geometry(j, k, h):
+            left = feats[picks[j][k], h : h + strip]
+            both[j, k, h] = jnp.dot(left, own[group[j]], preferred_element_type=f32)
+
+        def terms(j, k, h):
             c, n = group[j], picks[j][k]
-            pair = both.pop((j, k))
-            for r in range(0, 128, 16):
-                dist = jnp.maximum(pair[r : r + 16, :128], tiny)
-                run = pair[r : r + 16, 128:]
+            pair = both.pop((j, k, h))
+            for low in range(0, strip, 16):
+                r = h + low
+                dist = jnp.maximum(pair[low : low + 16, :128], tiny)
+                run = pair[low : low + 16, 128:]
                 q = dist * lax.rsqrt(dist)
                 fall = jnp.maximum(1.0 - q, 0.0)
                 g = fall * fall * fall
@@ -171,7 +167,9 @@
                 slopes[c, k, 128 + r : 128 + r + 16] = (g - high.astype(f32)).astype(bf16)
                 visc[c, k, r : r + 16] = g * jnp.minimum(run, 0.0) * (1.0 / (dist + 0.01))
 
-        def reduce(j, k):
+        def reduce(j, k, h):
+            if h + strip < 128:
+                return
             c, n = group[j], picks[j][k]
             part = jnp.dot(columns[n], slopes[c, k], preferred_element_type=f32)
             sofar[j] = part if j not in sofar else sofar[j] + part
@@ -179,7 +177,7 @@
                 sums[c] = sofar[j]
                 weighted[c] = total[j]
 
-        pipelined(tiles, (geometry, terms, reduce))
+        pipelined(tiles, (geometry, idle, terms, idle, reduce))
         return 0
 
     over_cells(cells, some)
@@ -256,12 +254,12 @@
 
 
 def near_z(c):
-    cx, cy, cz = parts_of(c)
+    _, _, cz = parts_of(c)
     return [flat((2, cz), (2, x), (2, y)) for x in range(2) for y in range(2)]
 
 
 def near_y(c):
-    cx, cy, cz = parts_of(c)
+    _, cy, cz = parts_of(c)
     return [flat((2, cy), (2, x), (4, cz + dz)) for x in range(2) for dz in range(3)]
 
 
@@ -317,7 +315,7 @@
     ]
 
 
-def call(body, outs, operands, specs=None, scratch=(), limit=24, name=None):
+def call(body, outs, operands, specs=None, scratch=(), limit=24):
     return pl.pallas_call(
         body,
         out_shape=tuple(outs),
@@ -325,7 +323,6 @@
         out_specs=tuple([vmem] * len(outs)),
         scratch_shapes=list(scratch),
         compiler_params=pltpu.CompilerParams(vmem_limit_bytes=limit << 20),
-        name=name,
     )(*operands)
 
 
@@ -343,7 +340,7 @@
     return [shaped(*plane), shaped(*plane)]
 
 
-def put_sends(axis, refs, high, tile_at, rest):
+def put_sends(refs, high, tile_at, rest):
     top, bottom = tile_at(1), tile_at(0)
     one, two = jnp.where(high, top, bottom), jnp.where(high, bottom, top)
     if len(refs) == 1:
@@ -355,12 +352,15 @@
 
 
 def receive(axis, sends):
-    if len(sends) == 1:
-        return exchanged(axis, sends[0])
-    return exchanged(axis, sends)
-
-
-def pack_y(own, from_z, rows, name):
+    first, second = routes(axis)
+    ways = (first,) if len(sends) == 1 else (first, second)
+    got = []
+    for send, way in zip(sends, ways):
+        got.append(lax.ppermute(send, axis, way))
+    return tuple(got)
+
+
+def pack_y(own, from_z, rows):
     sends = send_shapes("gy", (2, 4, rows, 128))
     n = len(from_z)
 
@@ -376,12 +376,12 @@
                         return own_ref[x, y, e - 1]
                     return take_side(before, got, 0 if e == 0 else 1, (x, y))
 
-                put_sends("gy", out, high, tile_at, (x, e))
-
-    return call(body, sends, (own, *from_z), name=name, limit=4)
-
-
-def pack_x(own, from_z, from_y, rows, name):
+                put_sends(out, high, tile_at, (x, e))
+
+    return call(body, sends, (own, *from_z), limit=4)
+
+
+def pack_x(own, from_z, from_y, rows):
     sends = send_shapes("gx", (4, 4, rows, 128))
     n, m = len(from_z), len(from_y)
 
@@ -400,16 +400,16 @@
                         return own_ref[x, a - 1, e - 1]
                     return take_side(before_z, got_z, 0 if e == 0 else 1, (x, a - 1))
 
-                put_sends("gx", out, high, tile_at, (a, e))
-
-    return call(body, sends, (own, *from_z, *from_y), name=name, limit=4)
+                put_sends(out, high, tile_at, (a, e))
+
+    return call(body, sends, (own, *from_z, *from_y), limit=4)
 
 
 inner_dims = {"z": (2, 2), "y": (2, 4), "x": (4, 4)}
 
 
 def entry_tile(group, before, refs, e, sides):
-    a, b = inner_dims[group]
+    _, b = inner_dims[group]
     return take_side(before, refs, sides, (e // b, e % b))
 
 
@@ -422,7 +422,7 @@
             tile = own_ref[x, y, z]
             offsets = offsets_of(place(c))
             prepare(tile, offsets, c, feats, masses, columns)
-            table, _mass = moments(tile, offsets)
+            table, _ = moments(tile, offsets)
             table_ref[c] = own_features(table)
             return 0
 
@@ -430,7 +430,7 @@
         density_pairs(table_ref, 8, near, feats, masses, columns, slopes, visc, sums, weighted)
 
     outs = pair_outputs(count) + [shaped(8, feature_rows, 256, kind=bf16)]
-    return call(body, outs, (own,), scratch=scratch_density(entries), name="density_own")
+    return call(body, outs, (own,), scratch=scratch_density(entries))
 
 
 def density_halo(group, axis, received, own_feats):
@@ -453,29 +453,22 @@
             lax.fori_loop(0, half, one, 0, unroll=4)
         density_pairs(own_ref, 8, near, feats, masses, columns, slopes, visc, sums, weighted)
 
-    return call(
-        body,
-        pair_outputs(count),
-        (*received, own_feats),
-        scratch=scratch_density(entries),
-        name="density_" + group,
-    )
-
-
-def pressure(own, alphas, counts, partials):
+    return call(body, pair_outputs(count), (*received, own_feats), scratch=scratch_density(entries))
+
+
+def pressure(own, partials):
     sends = send_shapes("gz", (2, 2, 2, 128))
-    outs = [shaped(2, 2, 2, 2, 128), shaped(2, 2, 2, 128), shaped(8, tile_rows, 128)] + sends
+    outs = [shaped(2, 2, 2, 2, 128), shaped(8, tile_rows, 128)] + sends
     n = len(partials)
 
-    def body(counts_ref, alphas_ref, own_ref, *refs):
-        pieces, (press, density, first), out = refs[:n], refs[n : n + 3], refs[n + 3 :]
+    def body(own_ref, *refs):
+        pieces, (press, first), out = refs[:n], refs[n : n + 2], refs[n + 2 :]
         high = first_sends_high("gz")
-        lanes = lax.broadcasted_iota(jnp.int32, (1, 128), 1)
         for x in range(2):
             for y in range(2):
                 for z in range(2):
                     c = 4 * x + 2 * y + z
-                    table, _mass = moments(own_ref[x, y, z], [float(v - 1) for v in (x, y, z)])
+                    table, mass = moments(own_ref[x, y, z], [float(v - 1) for v in (x, y, z)])
                     s = sum(p[c] for p in pieces[0::2])
                     gq = jnp.sum(sum(p[c] for p in pieces[1::2]), 0, keepdims=True)
                     t = s[0:8] + s[8:16]
@@ -487,21 +480,18 @@
                     gr2 = t[6:7] + table[6:7] * m0 - 2.0 * x_mx
                     rho = kernel_norm * (m0 + 3.0 * gq - 4.0 * gr2)
                     div = -20.0 * kernel_norm * (t[7:8] + table[7:8] * m0 - x_mv - v_mx)
-                    rho = jnp.where(lanes < counts_ref[x, y, z], rho, 1.0)
+                    rho = jnp.where(mass > 0.0, rho, 1.0)
                     compress = jnp.maximum(div / rho, 0.0)
-                    weight = alphas_ref[x, y, z : z + 1, :] * compress / (compress + 1.0)
+                    weight = own_ref[x, y, z, 7:8] * compress / (compress + 1.0)
                     press[x, y, z] = jnp.concatenate([rho, weight], 0)
-                    density[x, y, z : z + 1, :] = rho
                     first[c] = jnp.concatenate(
                         [pos * m0 - t[0:3], div, jnp.zeros((tile_rows - 4, 128), f32)], 0
                     )
         for x in range(2):
             for y in range(2):
-                put_sends("gz", out, high, lambda z, x=x, y=y: press[x, y, z], (x, y))
-
-    operands = (counts, alphas, own, *partials)
-    specs = [smem] + [vmem] * (len(operands) - 1)
-    return call(body, outs, operands, specs=specs, name="pressure", limit=8)
+                put_sends(out, high, lambda z, x=x, y=y: press[x, y, z], (x, y))
+
+    return call(body, outs, (own, *partials), limit=8)
 
 
 def scratch_force(entries):
@@ -517,7 +507,7 @@
 
 
 def force_own(own, press, kept):
-    entries, near, place, count = groups["own"]
+    entries, near, place, _ = groups["own"]
 
     def body(own_ref, press_ref, slopes, visc, sums, pulls, rhos, columns, gradients):
         def one(c, _):
@@ -535,17 +525,11 @@
 
         force_pairs(8, near, mine, rhos, columns, gradients, slopes, visc, sums, pulls)
 
-    return call(
-        body,
-        force_outputs(),
-        (own, press, *kept),
-        scratch=scratch_force(entries),
-        name="force_own",
-    )
+    return call(body, force_outputs(), (own, press, *kept), scratch=scratch_force(entries))
 
 
 def force_halo(group, axis, received, press_received, press, kept):
-    entries, near, place, count = groups[group]
+    entries, near, place, _ = groups[group]
     n = len(received)
     half = entries // 2
 
@@ -575,22 +559,20 @@
         force_outputs(),
         (*received, *press_received, press, *kept),
         scratch=scratch_force(entries),
-        name="force_" + group,
-    )
-
-
-def finish(own, press, first, counts, partials):
-    outs = [shaped(3, 2, 2, 2, 128), shaped(2, 2, 2, 128)]
+    )
+
+
+def finish(own, press, first, partials):
+    outs = [shaped(2, 2, 2, 128), shaped(3, 2, 2, 2, 128), shaped(2, 2, 2, 128)]
     n = len(partials)
 
-    def body(counts_ref, own_ref, press_ref, first_ref, *refs):
-        pieces, (accel, heating) = refs[:n], refs[n:]
-        lanes = lax.broadcasted_iota(jnp.int32, (1, 128), 1)
+    def body(own_ref, press_ref, first_ref, *refs):
+        pieces, (density, accel, heating) = refs[:n], refs[n:]
         for x in range(2):
             for y in range(2):
                 for z in range(2):
                     c = 4 * x + 2 * y + z
-                    table, _mass = moments(own_ref[x, y, z], [float(v - 1) for v in (x, y, z)])
+                    table, mass = moments(own_ref[x, y, z], [float(v - 1) for v in (x, y, z)])
                     u = sum(p[c] for p in pieces[0::2])
                     v = sum(p[c] for p in pieces[1::2])
                     plain, scaled = u[0:8] + u[8:16], u[16:24] + u[24:32]
@@ -606,7 +588,7 @@
                         + (pos * g[3:4] - g[0:3])
                         - (pos * zero - mixed[0:3])
                     )
-                    live = jnp.where(lanes < counts_ref[x, y, z], 1.0, 0.0)
+                    live = jnp.where(mass > 0.0, 1.0, 0.0)
                     push = (20.0 * kernel_norm) * live * total
                     work = (
                         mixed[7:8]
@@ -615,59 +597,51 @@
                         - jnp.sum(vel * mixed[0:3], 0, keepdims=True)
                     )
                     warm = live * (first_ref[c, 3:4] * inverse + (10.0 * kernel_norm) * work)
+                    density[x, y, z : z + 1, :] = rho
                     for i in range(3):
                         accel[i, x, y, z : z + 1, :] = push[i : i + 1]
                     heating[x, y, z : z + 1, :] = warm
 
-    operands = (counts, own, press, first, *partials)
-    specs = [smem] + [vmem] * (len(operands) - 1)
-    return call(body, outs, operands, specs=specs, name="finish", limit=8)
-
-
-def gather_own(positions, velocities, masses, counts):
+    return call(body, outs, (own, press, first, *partials), limit=8)
+
+
+def gather_own(fields):
     sends = send_shapes("gz", (2, 2, tile_rows, 128))
 
-    def body(counts_ref, pos, vel, mass, own, *out):
+    def body(fields_ref, own, *out):
         high = first_sends_high("gz")
-        lanes = lax.broadcasted_iota(jnp.int32, (1, 128), 1)
         for x in range(2):
             for y in range(2):
                 for z in range(2):
-                    here = mass[x, y, z : z + 1, :] * jnp.where(lanes < counts_ref[x, y, z], 1.0, 0.0)
-                    own[x, y, z] = rows_of(
-                        *(pos[i, x, y, z : z + 1, :] for i in range(3)),
-                        *(vel[i, x, y, z : z + 1, :] for i in range(3)),
-                        here,
-                    )
+                    own[x, y, z] = rows_of(*(fields_ref[i, x, y, z : z + 1, :] for i in range(tile_rows)))
         for x in range(2):
             for y in range(2):
-                put_sends("gz", out, high, lambda z, x=x, y=y: own[x, y, z], (x, y))
-
-    outs = [shaped(2, 2, 2, tile_rows, 128)] + sends
-    operands = (counts, positions, velocities, masses)
-    return call(body, outs, operands, specs=[smem] + [vmem] * 3, name="gather_own", limit=4)
+                put_sends(out, high, lambda z, x=x, y=y: own[x, y, z], (x, y))
+
+    return call(body, [shaped(2, 2, 2, tile_rows, 128)] + sends, (fields,), limit=4)
 
 
 def per_block(positions, velocities, masses, alphas, counts):
-    own, *sends = gather_own(positions, velocities, masses, counts)
+    slots = lax.broadcasted_iota(jnp.int32, masses.shape, 3)
+    live_mass = jnp.where(slots < counts[..., None], masses, 0.0)
+    own, *sends = gather_own(jnp.concatenate([positions, velocities, live_mass[None], alphas[None]], 0))
     from_z = receive("gz", sends)
     *kept_own, sums_own, weighted_own, own_feats = density_own(own)
-    from_y = receive("gy", pack_y(own, from_z, tile_rows, "pack_y"))
+    from_y = receive("gy", pack_y(own, from_z, tile_rows))
     *kept_z, sums_z, weighted_z = density_halo("z", "gz", from_z, own_feats)
-    from_x = receive("gx", pack_x(own, from_z, from_y, tile_rows, "pack_x"))
+    from_x = receive("gx", pack_x(own, from_z, from_y, tile_rows))
     *kept_y, sums_y, weighted_y = density_halo("y", "gy", from_y, own_feats)
     *kept_x, sums_x, weighted_x = density_halo("x", "gx", from_x, own_feats)
     partials = (sums_own, weighted_own, sums_z, weighted_z, sums_y, weighted_y, sums_x, weighted_x)
-    press, density, first, *sends = pressure(own, alphas, counts, partials)
+    press, first, *sends = pressure(own, partials)
     press_z = receive("gz", sends)
     forces = list(force_own(own, press, kept_own))
-    press_y = receive("gy", pack_y(press, press_z, 2, "pack_press_y"))
+    press_y = receive("gy", pack_y(press, press_z, 2))
     forces += force_halo("z", "gz", from_z, press_z, press, kept_z)
-    press_x = receive("gx", pack_x(press, press_z, press_y, 2, "pack_press_x"))
+    press_x = receive("gx", pack_x(press, press_z, press_y, 2))
     forces += force_halo("y", "gy", from_y, press_y, press, kept_y)
     forces += force_halo("x", "gx", from_x, press_x, press, kept_x)
-    accel, heating = finish(own, press, first, counts, forces)
-    return density, accel, heating
+    return finish(own, press, first, forces)
 
 
 neighbour_shifts = [
@@ -716,9 +690,7 @@
 
 
 def density_terms(own_rows, neighbour, cell_shift):
-    offset_parts, dist_sq, kernel_value, kernel_slope, approach = pair_geometry(
-        own_rows, neighbour, cell_shift
-    )
+    _, _, kernel_value, kernel_slope, approach = pair_geometry(own_rows, neighbour, cell_shift)
     other_mass = neighbour[6][:, None, :]
     return (
         jnp.sum(other_mass * kernel_value, -1),
@@ -727,7 +699,7 @@
 
 
 def force_terms(own_rows, neighbour, cell_shift):
-    offset_parts, dist_sq, kernel_value, kernel_slope, approach = pair_geometry(
+    offset_parts, dist_sq, _, kernel_slope, approach = pair_geometry(
         own_rows, neighbour, cell_shift
     )
     rho_own = own_rows[7][:, :, None]

time: 65.7 us -> 53.7 us (0.82)
  Pallas kernels: 37.5 us -> 28.2 us
  local copies, waits for them, and re-layouts: 4.16 us -> 0 us
  other arithmetic: 0 us -> 1.53 us
    pallas_call x15, Pallas kernels: 37.5 us -> 28.2 us  [call(): pl.pallas_call(body, out_shape=tuple(outs), in_specs=specs or [vmem] * le...]
    unnamed x14 -> x0, local copies, waits for them, and re-layouts: 4.16 us -> none
    broadcast_in_dim x0 -> x1, other arithmetic: none -> 0.77 us  [per_block(): live_mass[None]]
    concatenate x0 -> x1, other arithmetic: none -> 0.76 us  [per_block(): jnp.concatenate([positions, velocities, live_mass[None], alphas[None]], 0)]
  transfers between devices with their start and end apart: 10 -> 10, of which waited for: 5 -> 5; matrix products, arithmetic and copies ran while one was open for 0% -> 0% of each run, Pallas kernels for 33% -> 31%
where the time goes in v2:
time: 53.7 us; the launch traced here: 53.5 us
  Pallas kernels  28.2 us (53%)
  starting transfers between devices  13.7 us (26%)
  waiting for transfers between devices  9.3 us (17%)
  other arithmetic  1.53 us (3%)
  between operations  0.74 us (1%)
    pallas_call x15, Pallas kernels, call(): pl.pallas_call(body, out_shape=tuple(outs), in_specs=specs or [vmem] * le...  28.2 us
    ppermute x10, starting transfers between devices, receive(): got.append(lax.ppermute(send, axis, way))  13.7 us
    ppermute x10, waiting for transfers between devices, receive(): got.append(lax.ppermute(send, axis, way))  9.3 us
  transfers between devices with their start and end apart: 10, of which 5 were waited for; matrix products, arithmetic and copies ran while one was open for 0% of the time, Pallas kernels for 31%

profile of v2, /device:TPU:0, one launch (start us, length us, event | category | flops | bytes accessed | tf_op | source)
XLA Modules:
  0.0 53.5 jit_solution(2687957382228138946)
XLA Ops:
  0.6 0.8 %fusion = f32[1,2,2,2,128]{4,3,2,1,0:T(2,128)S(1)} fusion(f32[2,2,2,128]{3,2,1,0:T(2,128)} %param.7, s32[2,2,2]{2,1,0:T(2,128)} %param.9), kind=kLoop, calls=%fused_computation.2 | loop fusion | flops 2048 | bytes 8224 | tf_op jit(solution)/shard_map/broadcast_in_dim | solution.py:627
  1.4 0.8 %pad_maximum_fusion.fields_ref = f32[8,2,2,2,128]{4,3,2,1,0:T(2,128)S(1)} fusion(f32[1,2,2,2,128]{4,3,2,1,0:T(2,128)} %bitcast.3, f32[1,2,2,2,128]{4,3,2,1,0:T(2,128)S(1)} %fusion, f32[3,2,2,2,128]{4,3,2,1,0:T(2,128)} %param.6, f32[3,2,2,2,128]{4,3,2,1,0:T(2,128)} %param.5), kind=kLoop, calls=%fused_computation | loop fusion | flops 24576 | bytes 65536 | tf_op jit(solution)/shard_map/concatenate | solution.py:627
  2.2 3.1 %collective-permute-start = (f32[2,2,8,128]{3,2,1,0:T(8,128)S(1)}, f32[2,2,8,128]{3,2,1,0:T(8,128)S(1)}, u32[]{:S(2)}, u32[]{:S(2)}) collective-permute-start(f32[2,2,8,128]{3,2,1,0:T(8,128)S(1)} %get-tuple-element.42), channel_id=1, source_target_pairs={{0,1},{1,0},{2,3},{3,2},{4,5},{5,4},{6,7},{7,6},{8,9},{9,8},{10,11... | collective-permute-start | bytes 49160 | tf_op jit(solution)/shard_map/ppermute | solution.py:359
  5.3 2.5 %collective-permute-start.1 = (f32[2,2,8,128]{3,2,1,0:T(8,128)S(1)}, f32[2,2,8,128]{3,2,1,0:T(8,128)S(1)}, u32[]{:S(2)}, u32[]{:S(2)}) collective-permute-start(f32[2,2,8,128]{3,2,1,0:T(8,128)S(1)} %get-tuple-element.43), channel_id=1, source_target_pairs={{0,3},{1,2},{2,1},{3,0},{4,7},{5,6},{6,5},{7,4},{8,11},{9,10},{10,... | collective-permute-start | bytes 49160 | tf_op jit(solution)/shard_map/ppermute | solution.py:359
  7.8 3.1 %collective-permute-done.1.refs_1_ = f32[2,2,8,128]{3,2,1,0:T(8,128)S(1)} collective-permute-done((f32[2,2,8,128]{3,2,1,0:T(8,128)S(1)}, f32[2,2,8,128]{3,2,1,0:T(8,128)S(1)}, u32[]{:S(2)}, u32[]{:S(2)}) %collective-permute-start.1) | collective-permute-done | bytes 16416 | tf_op jit(solution)/shard_map/ppermute | solution.py:359
  10.9 1.6 %collective-permute-start.3 = (f32[2,4,8,128]{3,2,1,0:T(8,128)S(1)}, f32[2,4,8,128]{3,2,1,0:T(8,128)S(1)}, u32[]{:S(2)}, u32[]{:S(2)}) collective-permute-start(f32[2,4,8,128]{3,2,1,0:T(8,128)S(1)} %get-tuple-element.48), channel_id=1, source_target_pairs={{0,12},{4,8},{8,4},{12,0},{1,13},{5,9},{9,5},{13,1},{2,14},{6,10},... | collective-permute-start | bytes 98312 | tf_op jit(solution)/shard_map/ppermute | solution.py:359
  12.6 1.8 %collective-permute-done.3.refs_1_.refs_3_ = f32[2,4,8,128]{3,2,1,0:T(8,128)S(1)} collective-permute-done((f32[2,4,8,128]{3,2,1,0:T(8,128)S(1)}, f32[2,4,8,128]{3,2,1,0:T(8,128)S(1)}, u32[]{:S(2)}, u32[]{:S(2)}) %collective-permute-start.3) | collective-permute-done | bytes 32800 | tf_op jit(solution)/shard_map/ppermute | solution.py:359
  14.4 1.6 %collective-permute-start.4 = (f32[2,4,4,8,128]{4,3,2,1,0:T(8,128)S(1)}, f32[2,4,4,8,128]{4,3,2,1,0:T(8,128)S(1)}, u32[]{:S(2)}, u32[]{:S(2)}) collective-permute-start(f32[2,4,4,8,128]{4,3,2,1,0:T(8,128)S(1)} %shard_map.81), channel_id=1, source_target_pairs={{0,16},{16,0},{1,17},{17,1},{2,18},{18,2},{3,19},{19,3},{4,20},{20... | collective-permute-start | bytes 393224 | tf_op jit(solution)/shard_map/ppermute | solution.py:359
  15.9 4.4 %shard_map.77 = (bf16[8,8,256,128]{3,2,1,0:T(8,128)(2,1)S(1)}, f32[8,8,128,128]{3,2,1,0:T(8,128)S(1)}, f32[8,32,128]{2,1,0:T(8,128)S(1)}, f32[8,8,128]{2,1,0:T(8,128)S(1)}, bf16[8,64,256]{2,1,0:T(8,128)(2,1)S(1)}) custom-call(f32[2,2,2,8,128]{4,3,2,1,0:T(8,128)S(1)} %get-tuple-element.39.own_ref), custom_call_target="tpu_custom_call" | custom-call | tf_op jit(solution)/shard_map/pallas_call | solution.py:319
  20.4 2.5 %shard_map.78 = (bf16[8,4,256,128]{3,2,1,0:T(8,128)(2,1)S(1)}, f32[8,4,128,128]{3,2,1,0:T(8,128)S(1)}, f32[8,32,128]{2,1,0:T(8,128)S(1)}, f32[8,8,128]{2,1,0:T(8,128)S(1)}) custom-call(f32[2,2,8,128]{3,2,1,0:T(8,128)S(1)} %collective-permute-done.refs_0_, f32[2,2,8,128]{3,2,1,0:T(8,128)S(1)} %collective-permute-done.1.refs_1_, ...), custom_call_target="tpu_custom_call" | custom-call | tf_op jit(solution)/shard_map/pallas_call | solution.py:319
  22.8 4.2 %shard_map.80 = (bf16[8,6,256,128]{3,2,1,0:T(8,128)(2,1)S(1)}, f32[8,6,128,128]{3,2,1,0:T(8,128)S(1)}, f32[8,32,128]{2,1,0:T(8,128)S(1)}, f32[8,8,128]{2,1,0:T(8,128)S(1)}) custom-call(f32[2,4,8,128]{3,2,1,0:T(8,128)S(1)} %collective-permute-done.2.refs_0_.refs_2_, f32[2,4,8,128]{3,2,1,0:T(8,128)S(1)} %collective-permute-done.3.refs_1_.refs_3_, ...), custom_call_target="tpu_custom_call" | custom-call | tf_op jit(solution)/shard_map/pallas_call | solution.py:319
  27.0 6.8 %shard_map.82 = (bf16[8,9,256,128]{3,2,1,0:T(8,128)(2,1)S(1)}, f32[8,9,128,128]{3,2,1,0:T(8,128)S(1)}, f32[8,32,128]{2,1,0:T(8,128)S(1)}, f32[8,8,128]{2,1,0:T(8,128)S(1)}) custom-call(f32[2,4,4,8,128]{4,3,2,1,0:T(8,128)S(1)} %collective-permute-done.4.refs_0_, bf16[8,64,256]{2,1,0:T(8,128)(2,1)S(1)} %get-tuple-element.44.refs_2_.refs_1_), custom_call_target="tpu_custom_call" | custom-call | tf_op jit(solution)/shard_map/pallas_call | solution.py:319
  33.8 0.1 shard_map.83
  34.1 2.5 %collective-permute-start.6 = (f32[2,2,2,128]{3,2,1,0:T(2,128)S(1)}, f32[2,2,2,128]{3,2,1,0:T(2,128)S(1)}, u32[]{:S(2)}, u32[]{:S(2)}) collective-permute-start(f32[2,2,2,128]{3,2,1,0:T(2,128)S(1)} %get-tuple-element.60), channel_id=1, source_target_pairs={{0,3},{1,2},{2,1},{3,0},{4,7},{5,6},{6,5},{7,4},{8,11},{9,10},{10,... | collective-permute-start | bytes 12296 | tf_op jit(solution)/shard_map/ppermute | solution.py:359
  36.6 1.1 %collective-permute-done.5.refs_2_.refs_0_ = f32[2,2,2,128]{3,2,1,0:T(2,128)S(1)} collective-permute-done((f32[2,2,2,128]{3,2,1,0:T(2,128)S(1)}, f32[2,2,2,128]{3,2,1,0:T(2,128)S(1)}, u32[]{:S(2)}, u32[]{:S(2)}) %collective-permute-start.5) | collective-permute-done | bytes 4128 | tf_op jit(solution)/shard_map/ppermute | solution.py:359
  37.7 1.9 %collective-permute-done.6.refs_3_.refs_1_ = f32[2,2,2,128]{3,2,1,0:T(2,128)S(1)} collective-permute-done((f32[2,2,2,128]{3,2,1,0:T(2,128)S(1)}, f32[2,2,2,128]{3,2,1,0:T(2,128)S(1)}, u32[]{:S(2)}, u32[]{:S(2)}) %collective-permute-start.6) | collective-permute-done | bytes 4128 | tf_op jit(solution)/shard_map/ppermute | solution.py:359
  39.6 1.6 %collective-permute-start.8 = (f32[2,4,2,128]{3,2,1,0:T(2,128)S(1)}, f32[2,4,2,128]{3,2,1,0:T(2,128)S(1)}, u32[]{:S(2)}, u32[]{:S(2)}) collective-permute-start(f32[2,4,2,128]{3,2,1,0:T(2,128)S(1)} %get-tuple-element.66), channel_id=1, source_target_pairs={{0,12},{4,8},{8,4},{12,0},{1,13},{5,9},{9,5},{13,1},{2,14},{6,10},... | collective-permute-start | bytes 24584 | tf_op jit(solution)/shard_map/ppermute | solution.py:359
  41.2 1.5 %collective-permute-done.8.refs_3_ = f32[2,4,2,128]{3,2,1,0:T(2,128)S(1)} collective-permute-done((f32[2,4,2,128]{3,2,1,0:T(2,128)S(1)}, f32[2,4,2,128]{3,2,1,0:T(2,128)S(1)}, u32[]{:S(2)}, u32[]{:S(2)}) %collective-permute-start.8) | collective-permute-done | bytes 8224 | tf_op jit(solution)/shard_map/ppermute | solution.py:359
  42.8 0.6 %collective-permute-start.9 = (f32[2,4,4,2,128]{4,3,2,1,0:T(2,128)S(1)}, f32[2,4,4,2,128]{4,3,2,1,0:T(2,128)S(1)}, u32[]{:S(2)}, u32[]{:S(2)}) collective-permute-start(f32[2,4,4,2,128]{4,3,2,1,0:T(2,128)S(1)} %shard_map.88), channel_id=1, source_target_pairs={{0,16},{16,0},{1,17},{17,1},{2,18},{18,2},{3,19},{19,3},{4,20},{20... | collective-permute-start | bytes 98312 | tf_op jit(solution)/shard_map/ppermute | solution.py:359
  43.4 2.0 %shard_map.84 = (f32[8,48,128]{2,1,0:T(8,128)S(1)}, f32[8,16,128]{2,1,0:T(8,128)S(1)}) custom-call(f32[2,2,2,8,128]{4,3,2,1,0:T(8,128)S(1)} %get-tuple-element.39.own_ref, f32[2,2,2,2,128]{4,3,2,1,0:T(2,128)S(1)} %get-tuple-element.53.press_ref.refs_4_.own_ref.refs_2_, bf16[8,8,256,128]{3,2,1,0:T(8,128)(2,1)S(1)} %get-tuple-element.55.slopes, ...), custom_call_target="tpu_custom_call" | custom-call | tf_op jit(solution)/shard_map/pallas_call | solution.py:319
  45.4 1.2 %shard_map.85 = (f32[8,48,128]{2,1,0:T(8,128)S(1)}, f32[8,16,128]{2,1,0:T(8,128)S(1)}) custom-call(f32[2,2,8,128]{3,2,1,0:T(8,128)S(1)} %collective-permute-done.refs_0_, f32[2,2,8,128]{3,2,1,0:T(8,128)S(1)} %collective-permute-done.1.refs_1_, f32[2,2,2,128]{3,2,1,0:T(2,128)S(1)} %collective-permute-done.5.refs_2_.refs_0_, ...), custom_call_target="tpu_custom_call" | custom-call | tf_op jit(solution)/shard_map/pallas_call | solution.py:319
  46.6 2.3 %shard_map.87 = (f32[8,48,128]{2,1,0:T(8,128)S(1)}, f32[8,16,128]{2,1,0:T(8,128)S(1)}) custom-call(f32[2,4,8,128]{3,2,1,0:T(8,128)S(1)} %collective-permute-done.2.refs_0_.refs_2_, f32[2,4,8,128]{3,2,1,0:T(8,128)S(1)} %collective-permute-done.3.refs_1_.refs_3_, f32[2,4,2,128]{3,2,1,0:T(2,128)S(1)} %collective-permute-done.7.refs_2_, ...), custom_call_target="tpu_custom_call" | custom-call | tf_op jit(solution)/shard_map/pallas_call | solution.py:319
  48.9 3.9 %shard_map.89 = (f32[8,48,128]{2,1,0:T(8,128)S(1)}, f32[8,16,128]{2,1,0:T(8,128)S(1)}) custom-call(f32[2,4,4,8,128]{4,3,2,1,0:T(8,128)S(1)} %collective-permute-done.4.refs_0_, f32[2,4,4,2,128]{4,3,2,1,0:T(2,128)S(1)} %collective-permute-done.9.refs_1_, f32[2,2,2,2,128]{4,3,2,1,0:T(2,128)S(1)} %get-tuple-element.53.press_ref.refs_4_.own_ref.refs_2_, ...), custom_call_target="tpu_custom_call" | custom-call | tf_op jit(solution)/shard_map/pallas_call | solution.py:319
  52.8 0.7 %shard_map.90 = (f32[2,2,2,128]{3,2,1,0:T(2,128)}, f32[3,2,2,2,128]{4,3,2,1,0:T(2,128)}, f32[2,2,2,128]{3,2,1,0:T(2,128)}) custom-call(f32[2,2,2,8,128]{4,3,2,1,0:T(8,128)S(1)} %get-tuple-element.39.own_ref, f32[2,2,2,2,128]{4,3,2,1,0:T(2,128)S(1)} %get-tuple-element.53.press_ref.refs_4_.own_ref.refs_2_, f32[8,8,128]{2,1,0:T(8,128)S(1)} %get-tuple-element.54.first_ref, ...), custom_call_target="tpu_custom_call" | custom-call | tf_op jit(solution)/shard_map/pallas_call | solution.py:319
  (13 shorter events, 0.3 us)
Async XLA Ops:
  2.2 5.6 %collective-permute-start = (f32[2,2,8,128]{3,2,1,0:T(8,128)S(1)}, f32[2,2,8,128]{3,2,1,0:T(8,128)S(1)}, u32[]{:S(2)}, u32[]{:S(2)}) collective-permute-start(f32[2,2,8,128]{3,2,1,0:T(8,128)S(1)} %get-tuple-element.42), channel_id=1, source_target_pairs={{0,1},{1,0},{2,3},{3,2},{4,5},{5,4},{6,7},{7,6},{8,9},{9,8},{10,11... | collective-permute-start | bytes 49160 | tf_op jit(solution)/shard_map/ppermute | solution.py:359
  5.3 5.5 %collective-permute-start.1 = (f32[2,2,8,128]{3,2,1,0:T(8,128)S(1)}, f32[2,2,8,128]{3,2,1,0:T(8,128)S(1)}, u32[]{:S(2)}, u32[]{:S(2)}) collective-permute-start(f32[2,2,8,128]{3,2,1,0:T(8,128)S(1)} %get-tuple-element.43), channel_id=1, source_target_pairs={{0,3},{1,2},{2,1},{3,0},{4,7},{5,6},{6,5},{7,4},{8,11},{9,10},{10,... | collective-permute-start | bytes 49160 | tf_op jit(solution)/shard_map/ppermute | solution.py:359
  10.9 1.7 %collective-permute-start.2 = (f32[2,4,8,128]{3,2,1,0:T(8,128)S(1)}, f32[2,4,8,128]{3,2,1,0:T(8,128)S(1)}, u32[]{:S(2)}, u32[]{:S(2)}) collective-permute-start(f32[2,4,8,128]{3,2,1,0:T(8,128)S(1)} %get-tuple-element.47), channel_id=1, source_target_pairs={{0,4},{4,0},{8,12},{12,8},{1,5},{5,1},{9,13},{13,9},{2,6},{6,2},{1... | collective-permute-start | bytes 98312 | tf_op jit(solution)/shard_map/ppermute | solution.py:359
  10.9 3.4 %collective-permute-start.3 = (f32[2,4,8,128]{3,2,1,0:T(8,128)S(1)}, f32[2,4,8,128]{3,2,1,0:T(8,128)S(1)}, u32[]{:S(2)}, u32[]{:S(2)}) collective-permute-start(f32[2,4,8,128]{3,2,1,0:T(8,128)S(1)} %get-tuple-element.48), channel_id=1, source_target_pairs={{0,12},{4,8},{8,4},{12,0},{1,13},{5,9},{9,5},{13,1},{2,14},{6,10},... | collective-permute-start | bytes 98312 | tf_op jit(solution)/shard_map/ppermute | solution.py:359
  14.4 12.6 %collective-permute-start.4 = (f32[2,4,4,8,128]{4,3,2,1,0:T(8,128)S(1)}, f32[2,4,4,8,128]{4,3,2,1,0:T(8,128)S(1)}, u32[]{:S(2)}, u32[]{:S(2)}) collective-permute-start(f32[2,4,4,8,128]{4,3,2,1,0:T(8,128)S(1)} %shard_map.81), channel_id=1, source_target_pairs={{0,16},{16,0},{1,17},{17,1},{2,18},{18,2},{3,19},{19,3},{4,20},{20... | collective-permute-start | bytes 393224 | tf_op jit(solution)/shard_map/ppermute | solution.py:359
  34.0 3.7 %collective-permute-start.5 = (f32[2,2,2,128]{3,2,1,0:T(2,128)S(1)}, f32[2,2,2,128]{3,2,1,0:T(2,128)S(1)}, u32[]{:S(2)}, u32[]{:S(2)}) collective-permute-start(f32[2,2,2,128]{3,2,1,0:T(2,128)S(1)} %get-tuple-element.59), channel_id=1, source_target_pairs={{0,1},{1,0},{2,3},{3,2},{4,5},{5,4},{6,7},{7,6},{8,9},{9,8},{10,11... | collective-permute-start | bytes 12296 | tf_op jit(solution)/shard_map/ppermute | solution.py:359
  34.1 5.5 %collective-permute-start.6 = (f32[2,2,2,128]{3,2,1,0:T(2,128)S(1)}, f32[2,2,2,128]{3,2,1,0:T(2,128)S(1)}, u32[]{:S(2)}, u32[]{:S(2)}) collective-permute-start(f32[2,2,2,128]{3,2,1,0:T(2,128)S(1)} %get-tuple-element.60), channel_id=1, source_target_pairs={{0,3},{1,2},{2,1},{3,0},{4,7},{5,6},{6,5},{7,4},{8,11},{9,10},{10,... | collective-permute-start | bytes 12296 | tf_op jit(solution)/shard_map/ppermute | solution.py:359
  39.5 1.7 %collective-permute-start.7 = (f32[2,4,2,128]{3,2,1,0:T(2,128)S(1)}, f32[2,4,2,128]{3,2,1,0:T(2,128)S(1)}, u32[]{:S(2)}, u32[]{:S(2)}) collective-permute-start(f32[2,4,2,128]{3,2,1,0:T(2,128)S(1)} %get-tuple-element.65), channel_id=1, source_target_pairs={{0,4},{4,0},{8,12},{12,8},{1,5},{5,1},{9,13},{13,9},{2,6},{6,2},{1... | collective-permute-start | bytes 24584 | tf_op jit(solution)/shard_map/ppermute | solution.py:359
  39.6 3.1 %collective-permute-start.8 = (f32[2,4,2,128]{3,2,1,0:T(2,128)S(1)}, f32[2,4,2,128]{3,2,1,0:T(2,128)S(1)}, u32[]{:S(2)}, u32[]{:S(2)}) collective-permute-start(f32[2,4,2,128]{3,2,1,0:T(2,128)S(1)} %get-tuple-element.66), channel_id=1, source_target_pairs={{0,12},{4,8},{8,4},{12,0},{1,13},{5,9},{9,5},{13,1},{2,14},{6,10},... | collective-permute-start | bytes 24584 | tf_op jit(solution)/shard_map/ppermute | solution.py:359
  42.8 6.1 %collective-permute-start.9 = (f32[2,4,4,2,128]{4,3,2,1,0:T(2,128)S(1)}, f32[2,4,4,2,128]{4,3,2,1,0:T(2,128)S(1)}, u32[]{:S(2)}, u32[]{:S(2)}) collective-permute-start(f32[2,4,4,2,128]{4,3,2,1,0:T(2,128)S(1)} %shard_map.88), channel_id=1, source_target_pairs={{0,16},{16,0},{1,17},{17,1},{2,18},{18,2},{3,19},{19,3},{4,20},{20... | collective-permute-start | bytes 98312 | tf_op jit(solution)/shard_map/ppermute | solution.py:359

commit v3 on v2

--- a/solution.py
+++ b/solution.py
@@ -12,7 +12,7 @@
 bf16 = jnp.bfloat16
 kernel_norm = 21.0 / (2.0 * math.pi)
 tile_rows = 8
-feature_rows = 64
+feature_rows = 48
 tiny = 1e-12
 together = 4
 strip = 128
@@ -69,7 +69,8 @@
 def moments(tile, offsets):
     ids = row_ids()
     shift = jnp.where(ids == 0, offsets[0], jnp.where(ids == 1, offsets[1], jnp.where(ids == 2, offsets[2], 0.0)))
-    moved = tile + shift
+    high, low, _ = split3(tile + shift)
+    moved = high + low.astype(bf16).astype(f32)
     x, y, z, vx, vy, vz = (moved[i : i + 1] for i in range(6))
     sq = x * x + y * y + z * z
     xv = x * vx + y * vy + z * vz
@@ -79,9 +80,9 @@
 def other_features(table, mass):
     p1, p2, p3 = split3(table)
     m1, m2, m3 = split3(mass)
-    extra = rows_of(1.0, 1.0, 1.0, m1, m2, m3)
-    lanes = jnp.concatenate([p1, p1, p1, p2, p2, p3, extra, jnp.zeros_like(extra)], 0)
-    return lanes.T.astype(bf16)
+    ids = row_ids()
+    extra = jnp.where(ids < 3, 1.0, jnp.where(ids >= 6, p3, jnp.where(ids == 3, m1, jnp.where(ids == 4, m2, m3))))
+    return jnp.concatenate([p1, p1, p2, p2, extra, jnp.zeros_like(extra)], 0).T.astype(bf16)
 
 
 def own_features(table):
@@ -94,9 +95,9 @@
     right = jnp.where(ids < 3, -up, jnp.where(ids < 6, -down, jnp.where(ids == 7, 1.0, 0.0)))
     halves = []
     for part, fixed in ((left, sq), (right, xv)):
-        q1, q2, q3 = split3(part)
-        extra = rows_of(*fixed)
-        halves.append(jnp.concatenate([q1, q2, q3, q1, q2, q1, extra, jnp.zeros_like(extra)], 0))
+        q1, q2, _ = split3(part)
+        extra = rows_of(*fixed) + jnp.where(ids >= 6, part, 0.0)
+        halves.append(jnp.concatenate([q1, q2, q1, q2, extra, jnp.zeros_like(extra)], 0))
     return jnp.concatenate(halves, 1).astype(bf16)
 
 
@@ -118,7 +119,7 @@
     table, mass = moments(tile, offsets)
     lanes = other_features(table, mass)
     feats[at] = lanes
-    masses[at] = jnp.dot(lanes, picker(51), preferred_element_type=f32)
+    masses[at] = jnp.dot(lanes, picker(35), preferred_element_type=f32)
     columns[at] = mass_columns(table, mass)
 
 
@@ -426,7 +427,7 @@
             table_ref[c] = own_features(table)
             return 0
 
-        lax.fori_loop(0, 8, one, 0, unroll=4)
+        lax.fori_loop(0, 8, one, 0, unroll=8)
         density_pairs(table_ref, 8, near, feats, masses, columns, slopes, visc, sums, weighted)
 
     outs = pair_outputs(count) + [shaped(8, feature_rows, 256, kind=bf16)]
@@ -450,7 +451,7 @@
                 prepare(tile, offsets_of(place(at)), at, feats, masses, columns)
                 return 0
 
-            lax.fori_loop(0, half, one, 0, unroll=4)
+            lax.fori_loop(0, half, one, 0, unroll=min(half, 8))
         density_pairs(own_ref, 8, near, feats, masses, columns, slopes, visc, sums, weighted)
 
     return call(body, pair_outputs(count), (*received, own_feats), scratch=scratch_density(entries))
@@ -517,7 +518,7 @@
             )
             return 0
 
-        lax.fori_loop(0, 8, one, 0, unroll=4)
+        lax.fori_loop(0, 8, one, 0, unroll=8)
 
         def mine(c):
             x, y, z = parts_of(c)
@@ -546,7 +547,7 @@
                 prepare_force(tile, offsets_of(place(at)), fields, at, rhos, columns, gradients)
                 return 0
 
-            lax.fori_loop(0, half, one, 0, unroll=4)
+            lax.fori_loop(0, half, one, 0, unroll=min(half, 8))
 
         def mine(c):
             x, y, z = parts_of(c)
@@ -605,26 +606,29 @@
     return call(body, outs, (own, press, first, *partials), limit=8)
 
 
-def gather_own(fields):
+def gather_own(fields, counts):
     sends = send_shapes("gz", (2, 2, tile_rows, 128))
 
-    def body(fields_ref, own, *out):
+    def body(fields_ref, counts_ref, own, *out):
         high = first_sends_high("gz")
+        alone = row_ids() == 6
+        lanes = lax.broadcasted_iota(jnp.int32, (tile_rows, 128), 1)
         for x in range(2):
             for y in range(2):
                 for z in range(2):
-                    own[x, y, z] = rows_of(*(fields_ref[i, x, y, z : z + 1, :] for i in range(tile_rows)))
+                    dead = lanes >= counts_ref[x, y : y + 1, z : z + 1]
+                    tile = rows_of(*(fields_ref[i, x, y, z : z + 1, :] for i in range(tile_rows)))
+                    own[x, y, z] = jnp.where(alone & dead, 0.0, tile)
         for x in range(2):
             for y in range(2):
                 put_sends(out, high, lambda z, x=x, y=y: own[x, y, z], (x, y))
 
-    return call(body, [shaped(2, 2, 2, tile_rows, 128)] + sends, (fields,), limit=4)
+    return call(body, [shaped(2, 2, 2, tile_rows, 128)] + sends, (fields, counts), limit=4)
 
 
 def per_block(positions, velocities, masses, alphas, counts):
-    slots = lax.broadcasted_iota(jnp.int32, masses.shape, 3)
-    live_mass = jnp.where(slots < counts[..., None], masses, 0.0)
-    own, *sends = gather_own(jnp.concatenate([positions, velocities, live_mass[None], alphas[None]], 0))
+    fields = jnp.concatenate([positions, velocities, masses[None], alphas[None]], 0)
+    own, *sends = gather_own(fields, counts)
     from_z = receive("gz", sends)
     *kept_own, sums_own, weighted_own, own_feats = density_own(own)
     from_y = receive("gy", pack_y(own, from_z, tile_rows))

time: 53.7 us -> 50.1 us (0.933)
  Pallas kernels: 28.2 us -> 24.6 us
  other arithmetic: 1.53 us -> 0.77 us
  local copies, waits for them, and re-layouts: 0 us -> 0.68 us
    pallas_call x15, Pallas kernels: 28.2 us -> 24.6 us  [call(): pl.pallas_call(body, out_shape=tuple(outs), in_specs=specs or [vmem] * le...]
    broadcast_in_dim x1 -> x0, other arithmetic: 0.77 us -> none  [per_block(): live_mass[None]]
    unnamed x0 -> x2, local copies, waits for them, and re-layouts: none -> 0.68 us
  transfers between devices with their start and end apart: 10 -> 10, of which waited for: 5 -> 5; matrix products, arithmetic and copies ran while one was open for 0% -> 0% of each run, Pallas kernels for 31% -> 29%
where the time goes in v3:
time: 50.1 us; the launch traced here: 49.8 us
  Pallas kernels  24.6 us (49%)
  starting transfers between devices  13.7 us (27%)
  waiting for transfers between devices  9.3 us (19%)
  other arithmetic  0.77 us (2%)
  between operations  0.75 us (1%)
  local copies, waits for them, and re-layouts  0.68 us (1%)
    pallas_call x15, Pallas kernels, call(): pl.pallas_call(body, out_shape=tuple(outs), in_specs=specs or [vmem] * le...  24.6 us
    ppermute x10, starting transfers between devices, receive(): got.append(lax.ppermute(send, axis, way))  13.7 us
    ppermute x10, waiting for transfers between devices, receive(): got.append(lax.ppermute(send, axis, way))  9.3 us
  transfers between devices with their start and end apart: 10, of which 5 were waited for; matrix products, arithmetic and copies ran while one was open for 0% of the time, Pallas kernels for 29%

profile of v3, /device:TPU:0, one launch (start us, length us, event | category | flops | bytes accessed | tf_op | source)
XLA Modules:
  0.0 49.8 jit_solution(9862014448791716208)
XLA Ops:
  0.6 0.8 %pad_maximum_fusion.fields_ref = f32[8,2,2,2,128]{4,3,2,1,0:T(2,128)S(1)} fusion(f32[1,2,2,2,128]{4,3,2,1,0:T(2,128)} %bitcast.2, f32[1,2,2,2,128]{4,3,2,1,0:T(2,128)} %bitcast.3, f32[3,2,2,2,128]{4,3,2,1,0:T(2,128)} %param.6, f32[3,2,2,2,128]{4,3,2,1,0:T(2,128)} %param.5), kind=kLoop, calls=%fused_computation | loop fusion | flops 24576 | bytes 65536 | tf_op jit(solution)/shard_map/concatenate | solution.py:630
  1.4 0.7 %copy-done = s32[2,2,2]{2,1,0:T(2,128)S(1)} copy-done((s32[2,2,2]{2,1,0:T(2,128)S(1)}, s32[2,2,2]{2,1,0:T(2,128)}, u32[]{:S(2)}) %copy-start) | copy-done | bytes 56
  2.2 3.1 %collective-permute-start = (f32[2,2,8,128]{3,2,1,0:T(8,128)S(1)}, f32[2,2,8,128]{3,2,1,0:T(8,128)S(1)}, u32[]{:S(2)}, u32[]{:S(2)}) collective-permute-start(f32[2,2,8,128]{3,2,1,0:T(8,128)S(1)} %get-tuple-element.42), channel_id=1, source_target_pairs={{0,1},{1,0},{2,3},{3,2},{4,5},{5,4},{6,7},{7,6},{8,9},{9,8},{10,11... | collective-permute-start | bytes 49160 | tf_op jit(solution)/shard_map/ppermute | solution.py:360
  5.3 2.5 %collective-permute-start.1 = (f32[2,2,8,128]{3,2,1,0:T(8,128)S(1)}, f32[2,2,8,128]{3,2,1,0:T(8,128)S(1)}, u32[]{:S(2)}, u32[]{:S(2)}) collective-permute-start(f32[2,2,8,128]{3,2,1,0:T(8,128)S(1)} %get-tuple-element.43), channel_id=1, source_target_pairs={{0,3},{1,2},{2,1},{3,0},{4,7},{5,6},{6,5},{7,4},{8,11},{9,10},{10,... | collective-permute-start | bytes 49160 | tf_op jit(solution)/shard_map/ppermute | solution.py:360
  7.8 3.1 %collective-permute-done.1.refs_1_ = f32[2,2,8,128]{3,2,1,0:T(8,128)S(1)} collective-permute-done((f32[2,2,8,128]{3,2,1,0:T(8,128)S(1)}, f32[2,2,8,128]{3,2,1,0:T(8,128)S(1)}, u32[]{:S(2)}, u32[]{:S(2)}) %collective-permute-start.1) | collective-permute-done | bytes 16416 | tf_op jit(solution)/shard_map/ppermute | solution.py:360
  11.0 1.6 %collective-permute-start.3 = (f32[2,4,8,128]{3,2,1,0:T(8,128)S(1)}, f32[2,4,8,128]{3,2,1,0:T(8,128)S(1)}, u32[]{:S(2)}, u32[]{:S(2)}) collective-permute-start(f32[2,4,8,128]{3,2,1,0:T(8,128)S(1)} %get-tuple-element.48), channel_id=1, source_target_pairs={{0,12},{4,8},{8,4},{12,0},{1,13},{5,9},{9,5},{13,1},{2,14},{6,10},... | collective-permute-start | bytes 98312 | tf_op jit(solution)/shard_map/ppermute | solution.py:360
  12.6 1.8 %collective-permute-done.3.refs_1_.refs_3_ = f32[2,4,8,128]{3,2,1,0:T(8,128)S(1)} collective-permute-done((f32[2,4,8,128]{3,2,1,0:T(8,128)S(1)}, f32[2,4,8,128]{3,2,1,0:T(8,128)S(1)}, u32[]{:S(2)}, u32[]{:S(2)}) %collective-permute-start.3) | collective-permute-done | bytes 32800 | tf_op jit(solution)/shard_map/ppermute | solution.py:360
  14.4 1.6 %collective-permute-start.4 = (f32[2,4,4,8,128]{4,3,2,1,0:T(8,128)S(1)}, f32[2,4,4,8,128]{4,3,2,1,0:T(8,128)S(1)}, u32[]{:S(2)}, u32[]{:S(2)}) collective-permute-start(f32[2,4,4,8,128]{4,3,2,1,0:T(8,128)S(1)} %shard_map.81), channel_id=1, source_target_pairs={{0,16},{16,0},{1,17},{17,1},{2,18},{18,2},{3,19},{19,3},{4,20},{20... | collective-permute-start | bytes 393224 | tf_op jit(solution)/shard_map/ppermute | solution.py:360
  15.9 4.1 %shard_map.77 = (bf16[8,8,256,128]{3,2,1,0:T(8,128)(2,1)S(1)}, f32[8,8,128,128]{3,2,1,0:T(8,128)S(1)}, f32[8,32,128]{2,1,0:T(8,128)S(1)}, f32[8,8,128]{2,1,0:T(8,128)S(1)}, bf16[8,48,256]{2,1,0:T(8,128)(2,1)S(1)}) custom-call(f32[2,2,2,8,128]{4,3,2,1,0:T(8,128)S(1)} %get-tuple-element.39.own_ref), custom_call_target="tpu_custom_call" | custom-call | tf_op jit(solution)/shard_map/pallas_call | solution.py:320
  20.1 2.5 %shard_map.78 = (bf16[8,4,256,128]{3,2,1,0:T(8,128)(2,1)S(1)}, f32[8,4,128,128]{3,2,1,0:T(8,128)S(1)}, f32[8,32,128]{2,1,0:T(8,128)S(1)}, f32[8,8,128]{2,1,0:T(8,128)S(1)}) custom-call(f32[2,2,8,128]{3,2,1,0:T(8,128)S(1)} %collective-permute-done.refs_0_, f32[2,2,8,128]{3,2,1,0:T(8,128)S(1)} %collective-permute-done.1.refs_1_, ...), custom_call_target="tpu_custom_call" | custom-call | tf_op jit(solution)/shard_map/pallas_call | solution.py:320
  22.5 3.3 %shard_map.80 = (bf16[8,6,256,128]{3,2,1,0:T(8,128)(2,1)S(1)}, f32[8,6,128,128]{3,2,1,0:T(8,128)S(1)}, f32[8,32,128]{2,1,0:T(8,128)S(1)}, f32[8,8,128]{2,1,0:T(8,128)S(1)}) custom-call(f32[2,4,8,128]{3,2,1,0:T(8,128)S(1)} %collective-permute-done.2.refs_0_.refs_2_, f32[2,4,8,128]{3,2,1,0:T(8,128)S(1)} %collective-permute-done.3.refs_1_.refs_3_, ...), custom_call_target="tpu_custom_call" | custom-call | tf_op jit(solution)/shard_map/pallas_call | solution.py:320
  25.9 5.9 %shard_map.82 = (bf16[8,9,256,128]{3,2,1,0:T(8,128)(2,1)S(1)}, f32[8,9,128,128]{3,2,1,0:T(8,128)S(1)}, f32[8,32,128]{2,1,0:T(8,128)S(1)}, f32[8,8,128]{2,1,0:T(8,128)S(1)}) custom-call(f32[2,4,4,8,128]{4,3,2,1,0:T(8,128)S(1)} %collective-permute-done.4.refs_0_, bf16[8,48,256]{2,1,0:T(8,128)(2,1)S(1)} %get-tuple-element.44.refs_2_.refs_1_), custom_call_target="tpu_custom_call" | custom-call | tf_op jit(solution)/shard_map/pallas_call | solution.py:320
  31.8 0.2 shard_map.83
  32.0 2.5 %collective-permute-start.6 = (f32[2,2,2,128]{3,2,1,0:T(2,128)S(1)}, f32[2,2,2,128]{3,2,1,0:T(2,128)S(1)}, u32[]{:S(2)}, u32[]{:S(2)}) collective-permute-start(f32[2,2,2,128]{3,2,1,0:T(2,128)S(1)} %get-tuple-element.60), channel_id=1, source_target_pairs={{0,3},{1,2},{2,1},{3,0},{4,7},{5,6},{6,5},{7,4},{8,11},{9,10},{10,... | collective-permute-start | bytes 12296 | tf_op jit(solution)/shard_map/ppermute | solution.py:360
  34.6 1.1 %collective-permute-done.5.refs_2_.refs_0_ = f32[2,2,2,128]{3,2,1,0:T(2,128)S(1)} collective-permute-done((f32[2,2,2,128]{3,2,1,0:T(2,128)S(1)}, f32[2,2,2,128]{3,2,1,0:T(2,128)S(1)}, u32[]{:S(2)}, u32[]{:S(2)}) %collective-permute-start.5) | collective-permute-done | bytes 4128 | tf_op jit(solution)/shard_map/ppermute | solution.py:360
  35.6 1.9 %collective-permute-done.6.refs_3_.refs_1_ = f32[2,2,2,128]{3,2,1,0:T(2,128)S(1)} collective-permute-done((f32[2,2,2,128]{3,2,1,0:T(2,128)S(1)}, f32[2,2,2,128]{3,2,1,0:T(2,128)S(1)}, u32[]{:S(2)}, u32[]{:S(2)}) %collective-permute-start.6) | collective-permute-done | bytes 4128 | tf_op jit(solution)/shard_map/ppermute | solution.py:360
  37.6 1.6 %collective-permute-start.8 = (f32[2,4,2,128]{3,2,1,0:T(2,128)S(1)}, f32[2,4,2,128]{3,2,1,0:T(2,128)S(1)}, u32[]{:S(2)}, u32[]{:S(2)}) collective-permute-start(f32[2,4,2,128]{3,2,1,0:T(2,128)S(1)} %get-tuple-element.66), channel_id=1, source_target_pairs={{0,12},{4,8},{8,4},{12,0},{1,13},{5,9},{9,5},{13,1},{2,14},{6,10},... | collective-permute-start | bytes 24584 | tf_op jit(solution)/shard_map/ppermute | solution.py:360
  39.2 1.5 %collective-permute-done.8.refs_3_ = f32[2,4,2,128]{3,2,1,0:T(2,128)S(1)} collective-permute-done((f32[2,4,2,128]{3,2,1,0:T(2,128)S(1)}, f32[2,4,2,128]{3,2,1,0:T(2,128)S(1)}, u32[]{:S(2)}, u32[]{:S(2)}) %collective-permute-start.8) | collective-permute-done | bytes 8224 | tf_op jit(solution)/shard_map/ppermute | solution.py:360
  40.8 0.6 %collective-permute-start.9 = (f32[2,4,4,2,128]{4,3,2,1,0:T(2,128)S(1)}, f32[2,4,4,2,128]{4,3,2,1,0:T(2,128)S(1)}, u32[]{:S(2)}, u32[]{:S(2)}) collective-permute-start(f32[2,4,4,2,128]{4,3,2,1,0:T(2,128)S(1)} %shard_map.88), channel_id=1, source_target_pairs={{0,16},{16,0},{1,17},{17,1},{2,18},{18,2},{3,19},{19,3},{4,20},{20... | collective-permute-start | bytes 98312 | tf_op jit(solution)/shard_map/ppermute | solution.py:360
  41.4 1.7 %shard_map.84 = (f32[8,48,128]{2,1,0:T(8,128)S(1)}, f32[8,16,128]{2,1,0:T(8,128)S(1)}) custom-call(f32[2,2,2,8,128]{4,3,2,1,0:T(8,128)S(1)} %get-tuple-element.39.own_ref, f32[2,2,2,2,128]{4,3,2,1,0:T(2,128)S(1)} %get-tuple-element.53.press_ref.refs_4_.own_ref.refs_2_, bf16[8,8,256,128]{3,2,1,0:T(8,128)(2,1)S(1)} %get-tuple-element.55.slopes, ...), custom_call_target="tpu_custom_call" | custom-call | tf_op jit(solution)/shard_map/pallas_call | solution.py:320
  43.1 1.2 %shard_map.85 = (f32[8,48,128]{2,1,0:T(8,128)S(1)}, f32[8,16,128]{2,1,0:T(8,128)S(1)}) custom-call(f32[2,2,8,128]{3,2,1,0:T(8,128)S(1)} %collective-permute-done.refs_0_, f32[2,2,8,128]{3,2,1,0:T(8,128)S(1)} %collective-permute-done.1.refs_1_, f32[2,2,2,128]{3,2,1,0:T(2,128)S(1)} %collective-permute-done.5.refs_2_.refs_0_, ...), custom_call_target="tpu_custom_call" | custom-call | tf_op jit(solution)/shard_map/pallas_call | solution.py:320
  44.3 1.6 %shard_map.87 = (f32[8,48,128]{2,1,0:T(8,128)S(1)}, f32[8,16,128]{2,1,0:T(8,128)S(1)}) custom-call(f32[2,4,8,128]{3,2,1,0:T(8,128)S(1)} %collective-permute-done.2.refs_0_.refs_2_, f32[2,4,8,128]{3,2,1,0:T(8,128)S(1)} %collective-permute-done.3.refs_1_.refs_3_, f32[2,4,2,128]{3,2,1,0:T(2,128)S(1)} %collective-permute-done.7.refs_2_, ...), custom_call_target="tpu_custom_call" | custom-call | tf_op jit(solution)/shard_map/pallas_call | solution.py:320
  45.9 3.2 %shard_map.89 = (f32[8,48,128]{2,1,0:T(8,128)S(1)}, f32[8,16,128]{2,1,0:T(8,128)S(1)}) custom-call(f32[2,4,4,8,128]{4,3,2,1,0:T(8,128)S(1)} %collective-permute-done.4.refs_0_, f32[2,4,4,2,128]{4,3,2,1,0:T(2,128)S(1)} %collective-permute-done.9.refs_1_, f32[2,2,2,2,128]{4,3,2,1,0:T(2,128)S(1)} %get-tuple-element.53.press_ref.refs_4_.own_ref.refs_2_, ...), custom_call_target="tpu_custom_call" | custom-call | tf_op jit(solution)/shard_map/pallas_call | solution.py:320
  49.1 0.7 %shard_map.90 = (f32[2,2,2,128]{3,2,1,0:T(2,128)}, f32[3,2,2,2,128]{4,3,2,1,0:T(2,128)}, f32[2,2,2,128]{3,2,1,0:T(2,128)}) custom-call(f32[2,2,2,8,128]{4,3,2,1,0:T(8,128)S(1)} %get-tuple-element.39.own_ref, f32[2,2,2,2,128]{4,3,2,1,0:T(2,128)S(1)} %get-tuple-element.53.press_ref.refs_4_.own_ref.refs_2_, f32[8,8,128]{2,1,0:T(8,128)S(1)} %get-tuple-element.54.first_ref, ...), custom_call_target="tpu_custom_call" | custom-call | tf_op jit(solution)/shard_map/pallas_call | solution.py:320
  (14 shorter events, 0.4 us)
Async XLA Ops:
  1.4 0.7 %copy-start = (s32[2,2,2]{2,1,0:T(2,128)S(1)}, s32[2,2,2]{2,1,0:T(2,128)}, u32[]{:S(2)}) copy-start(s32[2,2,2]{2,1,0:T(2,128)} %counts_ref.1) | copy-start | bytes 100
  2.2 5.6 %collective-permute-start = (f32[2,2,8,128]{3,2,1,0:T(8,128)S(1)}, f32[2,2,8,128]{3,2,1,0:T(8,128)S(1)}, u32[]{:S(2)}, u32[]{:S(2)}) collective-permute-start(f32[2,2,8,128]{3,2,1,0:T(8,128)S(1)} %get-tuple-element.42), channel_id=1, source_target_pairs={{0,1},{1,0},{2,3},{3,2},{4,5},{5,4},{6,7},{7,6},{8,9},{9,8},{10,11... | collective-permute-start | bytes 49160 | tf_op jit(solution)/shard_map/ppermute | solution.py:360
  5.3 5.5 %collective-permute-start.1 = (f32[2,2,8,128]{3,2,1,0:T(8,128)S(1)}, f32[2,2,8,128]{3,2,1,0:T(8,128)S(1)}, u32[]{:S(2)}, u32[]{:S(2)}) collective-permute-start(f32[2,2,8,128]{3,2,1,0:T(8,128)S(1)} %get-tuple-element.43), channel_id=1, source_target_pairs={{0,3},{1,2},{2,1},{3,0},{4,7},{5,6},{6,5},{7,4},{8,11},{9,10},{10,... | collective-permute-start | bytes 49160 | tf_op jit(solution)/shard_map/ppermute | solution.py:360
  10.9 1.7 %collective-permute-start.2 = (f32[2,4,8,128]{3,2,1,0:T(8,128)S(1)}, f32[2,4,8,128]{3,2,1,0:T(8,128)S(1)}, u32[]{:S(2)}, u32[]{:S(2)}) collective-permute-start(f32[2,4,8,128]{3,2,1,0:T(8,128)S(1)} %get-tuple-element.47), channel_id=1, source_target_pairs={{0,4},{4,0},{8,12},{12,8},{1,5},{5,1},{9,13},{13,9},{2,6},{6,2},{1... | collective-permute-start | bytes 98312 | tf_op jit(solution)/shard_map/ppermute | solution.py:360
  11.0 3.4 %collective-permute-start.3 = (f32[2,4,8,128]{3,2,1,0:T(8,128)S(1)}, f32[2,4,8,128]{3,2,1,0:T(8,128)S(1)}, u32[]{:S(2)}, u32[]{:S(2)}) collective-permute-start(f32[2,4,8,128]{3,2,1,0:T(8,128)S(1)} %get-tuple-element.48), channel_id=1, source_target_pairs={{0,12},{4,8},{8,4},{12,0},{1,13},{5,9},{9,5},{13,1},{2,14},{6,10},... | collective-permute-start | bytes 98312 | tf_op jit(solution)/shard_map/ppermute | solution.py:360
  14.4 11.5 %collective-permute-start.4 = (f32[2,4,4,8,128]{4,3,2,1,0:T(8,128)S(1)}, f32[2,4,4,8,128]{4,3,2,1,0:T(8,128)S(1)}, u32[]{:S(2)}, u32[]{:S(2)}) collective-permute-start(f32[2,4,4,8,128]{4,3,2,1,0:T(8,128)S(1)} %shard_map.81), channel_id=1, source_target_pairs={{0,16},{16,0},{1,17},{17,1},{2,18},{18,2},{3,19},{19,3},{4,20},{20... | collective-permute-start | bytes 393224 | tf_op jit(solution)/shard_map/ppermute | solution.py:360
  32.0 3.7 %collective-permute-start.5 = (f32[2,2,2,128]{3,2,1,0:T(2,128)S(1)}, f32[2,2,2,128]{3,2,1,0:T(2,128)S(1)}, u32[]{:S(2)}, u32[]{:S(2)}) collective-permute-start(f32[2,2,2,128]{3,2,1,0:T(2,128)S(1)} %get-tuple-element.59), channel_id=1, source_target_pairs={{0,1},{1,0},{2,3},{3,2},{4,5},{5,4},{6,7},{7,6},{8,9},{9,8},{10,11... | collective-permute-start | bytes 12296 | tf_op jit(solution)/shard_map/ppermute | solution.py:360
  32.0 5.5 %collective-permute-start.6 = (f32[2,2,2,128]{3,2,1,0:T(2,128)S(1)}, f32[2,2,2,128]{3,2,1,0:T(2,128)S(1)}, u32[]{:S(2)}, u32[]{:S(2)}) collective-permute-start(f32[2,2,2,128]{3,2,1,0:T(2,128)S(1)} %get-tuple-element.60), channel_id=1, source_target_pairs={{0,3},{1,2},{2,1},{3,0},{4,7},{5,6},{6,5},{7,4},{8,11},{9,10},{10,... | collective-permute-start | bytes 12296 | tf_op jit(solution)/shard_map/ppermute | solution.py:360
  37.5 1.7 %collective-permute-start.7 = (f32[2,4,2,128]{3,2,1,0:T(2,128)S(1)}, f32[2,4,2,128]{3,2,1,0:T(2,128)S(1)}, u32[]{:S(2)}, u32[]{:S(2)}) collective-permute-start(f32[2,4,2,128]{3,2,1,0:T(2,128)S(1)} %get-tuple-element.65), channel_id=1, source_target_pairs={{0,4},{4,0},{8,12},{12,8},{1,5},{5,1},{9,13},{13,9},{2,6},{6,2},{1... | collective-permute-start | bytes 24584 | tf_op jit(solution)/shard_map/ppermute | solution.py:360
  37.6 3.1 %collective-permute-start.8 = (f32[2,4,2,128]{3,2,1,0:T(2,128)S(1)}, f32[2,4,2,128]{3,2,1,0:T(2,128)S(1)}, u32[]{:S(2)}, u32[]{:S(2)}) collective-permute-start(f32[2,4,2,128]{3,2,1,0:T(2,128)S(1)} %get-tuple-element.66), channel_id=1, source_target_pairs={{0,12},{4,8},{8,4},{12,0},{1,13},{5,9},{9,5},{13,1},{2,14},{6,10},... | collective-permute-start | bytes 24584 | tf_op jit(solution)/shard_map/ppermute | solution.py:360
  40.8 5.2 %collective-permute-start.9 = (f32[2,4,4,2,128]{4,3,2,1,0:T(2,128)S(1)}, f32[2,4,4,2,128]{4,3,2,1,0:T(2,128)S(1)}, u32[]{:S(2)}, u32[]{:S(2)}) collective-permute-start(f32[2,4,4,2,128]{4,3,2,1,0:T(2,128)S(1)} %shard_map.88), channel_id=1, source_target_pairs={{0,16},{16,0},{1,17},{17,1},{2,18},{18,2},{3,19},{19,3},{4,20},{20... | collective-permute-start | bytes 98312 | tf_op jit(solution)/shard_map/ppermute | solution.py:360

commit v4 on v3

--- a/solution.py
+++ b/solution.py
@@ -15,7 +15,6 @@
 feature_rows = 48
 tiny = 1e-12
 together = 4
-strip = 128
 
 vmem = pl.BlockSpec(memory_space=pltpu.VMEM)
 
@@ -77,15 +76,14 @@
     return jnp.where(ids == 6, sq, jnp.where(ids == 7, xv, moved)), tile[6:7]
 
 
-def other_features(table, mass):
+def column_features(table):
     p1, p2, p3 = split3(table)
-    m1, m2, m3 = split3(mass)
     ids = row_ids()
-    extra = jnp.where(ids < 3, 1.0, jnp.where(ids >= 6, p3, jnp.where(ids == 3, m1, jnp.where(ids == 4, m2, m3))))
+    extra = jnp.where(ids < 3, 1.0, jnp.where(ids >= 6, p3, 0.0))
     return jnp.concatenate([p1, p1, p2, p2, extra, jnp.zeros_like(extra)], 0).T.astype(bf16)
 
 
-def own_features(table):
+def row_features(table):
     ids = row_ids()
     sq = split3(table[6:7])
     xv = split3(table[7:8])
@@ -110,17 +108,15 @@
     return jnp.concatenate([left, left], 1)
 
 
-def picker(first_row):
-    ids = lax.broadcasted_iota(jnp.int32, (feature_rows, 128), 0)
-    return jnp.where((ids >= first_row) & (ids < first_row + 3), 1.0, 0.0).astype(bf16)
-
-
 def prepare(tile, offsets, at, feats, masses, columns):
     table, mass = moments(tile, offsets)
-    lanes = other_features(table, mass)
-    feats[at] = lanes
-    masses[at] = jnp.dot(lanes, picker(35), preferred_element_type=f32)
+    feats[at] = row_features(table)
+    masses[at] = jnp.broadcast_to(mass, (16, 128))
     columns[at] = mass_columns(table, mass)
+
+
+def over_lanes(left, right):
+    return lax.dot_general(left, right, (((1,), (1,)), ((), ())), preferred_element_type=f32)
 
 
 def pipelined(tiles, stages):
@@ -134,99 +130,118 @@
     pass
 
 
-def over_cells(cells, body):
-    lax.fori_loop(0, cells // together, lambda i, _: body([i * together + j for j in range(together)]), 0)
-
-
-def density_pairs(own, cells, near, feats, masses, columns, slopes, visc, sums, weighted):
+def over_cells(start, stop, body):
+    lax.fori_loop(
+        start // together, stop // together, lambda i, _: body([i * together + j for j in range(together)]), 0
+    )
+
+
+def density_pairs(own, cells, near, feats, masses, columns, slopes, pairs, sums, weighted):
+    ones = jnp.ones((tile_rows, 256), bf16)
+
     def some(group):
-        both, total, sofar = {}, {}, {}
+        both, sofar = {}, {}
         picks = [near(c) for c in group]
-        tiles = [
-            (j, k, h) for j in range(len(group)) for k in range(len(picks[j])) for h in range(0, 128, strip)
-        ]
-
-        def geometry(j, k, h):
-            left = feats[picks[j][k], h : h + strip]
-            both[j, k, h] = jnp.dot(left, own[group[j]], preferred_element_type=f32)
-
-        def terms(j, k, h):
+        tiles = [(j, k) for j in range(len(group)) for k in range(len(picks[j]))]
+
+        def geometry(j, k):
+            pair = both[j, k] = jnp.dot(own[group[j]], feats[picks[j][k]], preferred_element_type=f32)
+            pairs[group[j], k] = pair
+
+        def terms(j, k):
             c, n = group[j], picks[j][k]
-            pair = both.pop((j, k, h))
-            for low in range(0, strip, 16):
-                r = h + low
-                dist = jnp.maximum(pair[low : low + 16, :128], tiny)
-                run = pair[low : low + 16, 128:]
+            pair = both.pop((j, k))
+            mass = masses[n]
+            for r in range(0, 128, 16):
+                at = slice(r, r + 16)
+                dist = jnp.maximum(pair[at, :128], tiny)
                 q = dist * lax.rsqrt(dist)
                 fall = jnp.maximum(1.0 - q, 0.0)
                 g = fall * fall * fall
-                part = g * q * masses[n, r : r + 16]
-                part = part[:8] + part[8:]
-                total[j] = part if j not in total else total[j] + part
+                part = g * q * mass
+                weighted[j, at] = part if k == 0 else weighted[j, at] + part
                 high = g.astype(bf16)
-                slopes[c, k, r : r + 16] = high
-                slopes[c, k, 128 + r : 128 + r + 16] = (g - high.astype(f32)).astype(bf16)
-                visc[c, k, r : r + 16] = g * jnp.minimum(run, 0.0) * (1.0 / (dist + 0.01))
-
-        def reduce(j, k, h):
-            if h + strip < 128:
-                return
+                slopes[c, k, at, :128] = high
+                slopes[c, k, at, 128:] = (g - high.astype(f32)).astype(bf16)
+
+        def reduce(j, k):
             c, n = group[j], picks[j][k]
-            part = jnp.dot(columns[n], slopes[c, k], preferred_element_type=f32)
+            part = over_lanes(columns[n], slopes[c, k])
             sofar[j] = part if j not in sofar else sofar[j] + part
             if k == len(picks[j]) - 1:
-                sums[c] = sofar[j]
-                weighted[c] = total[j]
+                sums[c, :32] = sofar[j]
+                high = weighted[j].astype(bf16)
+                low = (weighted[j] - high.astype(f32)).astype(bf16)
+                sums[c, 32:] = over_lanes(ones, jnp.concatenate([high, low], 1))
 
         pipelined(tiles, (geometry, idle, terms, idle, reduce))
         return 0
 
-    over_cells(cells, some)
+    over_cells(*cells, some)
+
+
+def viscous(group, slopes, pairs):
+    count = groups[group][3]
+
+    def body(slopes_ref, pairs_ref, visc):
+        def one(c, _):
+            for k in range(count):
+                for r in range(0, 128, 16):
+                    at = slice(r, r + 16)
+                    g = slopes_ref[c, k, at, :128].astype(f32) + slopes_ref[c, k, at, 128:].astype(f32)
+                    run = jnp.minimum(pairs_ref[c, k, at, 128:], 0.0)
+                    visc[c, k, at] = g * run * (1.0 / (pairs_ref[c, k, at, :128] + 0.01))
+            return 0
+
+        lax.fori_loop(0, 8, one, 0)
+
+    return call(body, [shaped(8, count, 128, 128)], (slopes, pairs), limit=4)[0]
 
 
 def prepare_force(tile, offsets, press, at, rhos, columns, gradients):
     table, mass = moments(tile, offsets)
     rho = press[0:1]
     weight = press[1:2]
-    heavy = mass * table
+    heavy = mass * jnp.where(row_ids() == 6, 1.0, table)
     h1, h2, _ = split3(heavy)
     s1, s2, _ = split3(weight * heavy)
-    m1, m2, _ = split3(mass)
-    w1, w2, _ = split3(weight * mass)
-    extra = rows_of(m1, m2, w1, w2)
-    left = jnp.concatenate([h1, h2, s1, s2, extra, jnp.zeros_like(extra)], 0).astype(bf16)
+    left = jnp.concatenate([h1, h2, s1, s2], 0).astype(bf16)
     columns[at] = jnp.concatenate([left, left], 1)
     light = (mass / rho) * jnp.where(row_ids() < 3, table, 1.0)
     l1, l2, _ = split3(light)
     left = jnp.concatenate([l1, l2], 0).astype(bf16)
     gradients[at] = jnp.concatenate([left, left], 1)
-    r1, r2, r3 = split3(rho)
-    lanes = jnp.concatenate([rows_of(r1, r2, r3), jnp.zeros((tile_rows, 128), f32)], 0).T.astype(bf16)
-    ids = lax.broadcasted_iota(jnp.int32, (16, 128), 0)
-    rhos[at] = jnp.dot(lanes, jnp.where(ids < 3, 1.0, 0.0).astype(bf16), preferred_element_type=f32)
-
-
-def force_pairs(cells, near, press_row, rhos, columns, gradients, slopes, visc, sums, pulls):
+    rhos[at] = jnp.broadcast_to(rho, (16, 128))
+
+
+def force_pairs(near, spread, rhos, columns, gradients, slopes, visc, sums, pulls, ready):
     def some(group):
         mixed, sofar, pulled = {}, {}, {}
         picks = [near(c) for c in group]
-        mine = [press_row(c) for c in group]
         tiles = [(j, k) for j, c in enumerate(group) for k in range(len(near(c)))]
 
         def terms(j, k):
             c, n = group[j], picks[j][k]
             highs, lows = [], []
+            theirs = rhos[n]
             for r in range(0, 128, 16):
-                t = visc[c, k, r : r + 16] * (1.0 / (rhos[n, r : r + 16] + mine[j]))
+                at = slice(r, r + 16)
+                below = theirs + spread[c, at]
+                if ready:
+                    t = visc[c, k, at] * (1.0 / below)
+                else:
+                    g = slopes[c, k, at, :128].astype(f32) + slopes[c, k, at, 128:].astype(f32)
+                    run = jnp.minimum(visc[c, k, at, 128:], 0.0)
+                    t = g * run * (1.0 / ((visc[c, k, at, :128] + 0.01) * below))
                 high = t.astype(bf16)
                 highs.append(high)
                 lows.append((t - high.astype(f32)).astype(bf16))
-            mixed[j, k] = jnp.concatenate(highs + lows, 0)
+            mixed[j, k] = jnp.concatenate([jnp.concatenate(highs, 0), jnp.concatenate(lows, 0)], 1)
 
         def reduce(j, k):
             c, n = group[j], picks[j][k]
-            part = jnp.dot(columns[n], mixed.pop((j, k)), preferred_element_type=f32)
-            pull = jnp.dot(gradients[n], slopes[c, k], preferred_element_type=f32)
+            part = over_lanes(columns[n], mixed.pop((j, k)))
+            pull = over_lanes(gradients[n], slopes[c, k])
             sofar[j] = part if j not in sofar else sofar[j] + part
             pulled[j] = pull if j not in pulled else pulled[j] + pull
             if k == len(picks[j]) - 1:
@@ -236,7 +251,7 @@
         pipelined(tiles, (terms, reduce))
         return 0
 
-    over_cells(cells, some)
+    over_cells(0, 8, some)
 
 
 def parts_of(c):
@@ -299,24 +314,27 @@
 }
 
 
+weights = pltpu.VMEM((together, 128, 128), f32)
+
+
 def scratch_density(entries):
     return [
-        pltpu.VMEM((entries, 128, feature_rows), bf16),
-        pltpu.VMEM((entries, 128, 128), f32),
+        pltpu.VMEM((entries, feature_rows, 256), bf16),
+        pltpu.VMEM((entries, 16, 128), f32),
         pltpu.VMEM((entries, 32, 256), bf16),
+        weights,
     ]
 
 
 def pair_outputs(count):
     return [
-        shaped(8, count, 256, 128, kind=bf16),
-        shaped(8, count, 128, 128),
-        shaped(8, 32, 128),
-        shaped(8, tile_rows, 128),
+        shaped(8, count, 128, 256, kind=bf16),
+        shaped(8, count, 128, 256),
+        shaped(8, 40, 128),
     ]
 
 
-def call(body, outs, operands, specs=None, scratch=(), limit=24):
+def call(body, outs, operands, specs=None, scratch=(), limit=12, aliases={}):
     return pl.pallas_call(
         body,
         out_shape=tuple(outs),
@@ -324,6 +342,7 @@
         out_specs=tuple([vmem] * len(outs)),
         scratch_shapes=list(scratch),
         compiler_params=pltpu.CompilerParams(vmem_limit_bytes=limit << 20),
+        input_output_aliases=aliases,
     )(*operands)
 
 
@@ -417,21 +436,42 @@
 def density_own(own):
     entries, near, place, count = groups["own"]
 
-    def body(own_ref, slopes, visc, sums, weighted, table_ref, feats, masses, columns):
+    def body(own_ref, slopes, pairs, sums, table_ref, feats, masses, columns, weighted):
         def one(c, _):
             x, y, z = parts_of(c)
             tile = own_ref[x, y, z]
             offsets = offsets_of(place(c))
             prepare(tile, offsets, c, feats, masses, columns)
             table, _ = moments(tile, offsets)
-            table_ref[c] = own_features(table)
+            table_ref[c] = column_features(table)
             return 0
 
         lax.fori_loop(0, 8, one, 0, unroll=8)
-        density_pairs(table_ref, 8, near, feats, masses, columns, slopes, visc, sums, weighted)
-
-    outs = pair_outputs(count) + [shaped(8, feature_rows, 256, kind=bf16)]
-    return call(body, outs, (own,), scratch=scratch_density(entries))
+        density_pairs(table_ref, (0, 4), near, feats, masses, columns, slopes, pairs, sums, weighted)
+
+    outs = pair_outputs(count) + [
+        shaped(8, 128, feature_rows, kind=bf16),
+        shaped(entries, feature_rows, 256, kind=bf16),
+        shaped(entries, 16, 128),
+        shaped(entries, 32, 256, kind=bf16),
+    ]
+    got = call(body, outs, (own,), scratch=[weights])
+    return got[:3], got[3:]
+
+
+def density_own_rest(kept, features):
+    _, near, _, count = groups["own"]
+
+    def body(table_ref, feats, masses, columns, _slopes, _pairs, _sums, slopes, pairs, sums, weighted):
+        density_pairs(table_ref, (4, 8), near, feats, masses, columns, slopes, pairs, sums, weighted)
+
+    return call(
+        body,
+        pair_outputs(count),
+        (*features, *kept),
+        scratch=[weights],
+        aliases={4 + i: i for i in range(3)},
+    )
 
 
 def density_halo(group, axis, received, own_feats):
@@ -441,7 +481,7 @@
 
     def body(*refs):
         got, own_ref = refs[:n], refs[n]
-        slopes, visc, sums, weighted, feats, masses, columns = refs[n + 1 :]
+        slopes, pairs, sums, feats, masses, columns, weighted = refs[n + 1 :]
         before = first_gives_before(axis)
         for side in range(2):
 
@@ -452,7 +492,7 @@
                 return 0
 
             lax.fori_loop(0, half, one, 0, unroll=min(half, 8))
-        density_pairs(own_ref, 8, near, feats, masses, columns, slopes, visc, sums, weighted)
+        density_pairs(own_ref, (0, 8), near, feats, masses, columns, slopes, pairs, sums, weighted)
 
     return call(body, pair_outputs(count), (*received, own_feats), scratch=scratch_density(entries))
 
@@ -470,8 +510,8 @@
                 for z in range(2):
                     c = 4 * x + 2 * y + z
                     table, mass = moments(own_ref[x, y, z], [float(v - 1) for v in (x, y, z)])
-                    s = sum(p[c] for p in pieces[0::2])
-                    gq = jnp.sum(sum(p[c] for p in pieces[1::2]), 0, keepdims=True)
+                    s = sum(p[c] for p in pieces)
+                    gq = s[32:33]
                     t = s[0:8] + s[8:16]
                     m0 = s[16:17] + s[17:18]
                     pos, vel = table[0:3], table[3:6]
@@ -495,22 +535,34 @@
     return call(body, outs, (own, *partials), limit=8)
 
 
+def spread_own(press):
+    def body(press_ref, spread):
+        chosen = jnp.where(lax.broadcasted_iota(jnp.int32, (16, 128), 0) < 3, 1.0, 0.0).astype(bf16)
+        for c in range(8):
+            x, y, z = parts_of(c)
+            parts = rows_of(*split3(press_ref[x, y, z, 0:1]))
+            parts = jnp.concatenate([parts, jnp.zeros_like(parts)], 0).T.astype(bf16)
+            spread[c] = jnp.dot(parts, chosen, preferred_element_type=f32)
+
+    return call(body, [shaped(8, 128, 128)], (press,), limit=4)[0]
+
+
 def scratch_force(entries):
     return [
-        pltpu.VMEM((entries, 128, 128), f32),
-        pltpu.VMEM((entries, 48, 256), bf16),
+        pltpu.VMEM((entries, 16, 128), f32),
+        pltpu.VMEM((entries, 32, 256), bf16),
         pltpu.VMEM((entries, 16, 256), bf16),
     ]
 
 
 def force_outputs():
-    return [shaped(8, 48, 128), shaped(8, 16, 128)]
-
-
-def force_own(own, press, kept):
+    return [shaped(8, 32, 128), shaped(8, 16, 128)]
+
+
+def force_own(own, press, spread, kept, ready=False):
     entries, near, place, _ = groups["own"]
 
-    def body(own_ref, press_ref, slopes, visc, sums, pulls, rhos, columns, gradients):
+    def body(own_ref, press_ref, spread_ref, slopes, visc, sums, pulls, rhos, columns, gradients):
         def one(c, _):
             x, y, z = parts_of(c)
             prepare_force(
@@ -520,22 +572,18 @@
 
         lax.fori_loop(0, 8, one, 0, unroll=8)
 
-        def mine(c):
-            x, y, z = parts_of(c)
-            return press_ref[x, y, z, 0:1]
-
-        force_pairs(8, near, mine, rhos, columns, gradients, slopes, visc, sums, pulls)
-
-    return call(body, force_outputs(), (own, press, *kept), scratch=scratch_force(entries))
-
-
-def force_halo(group, axis, received, press_received, press, kept):
+        force_pairs(near, spread_ref, rhos, columns, gradients, slopes, visc, sums, pulls, ready)
+
+    return call(body, force_outputs(), (own, press, spread, *kept), scratch=scratch_force(entries))
+
+
+def force_halo(group, axis, received, press_received, spread, kept, ready=False):
     entries, near, place, _ = groups[group]
     n = len(received)
     half = entries // 2
 
     def body(*refs):
-        got, got_press, press_ref = refs[:n], refs[n : 2 * n], refs[2 * n]
+        got, got_press, spread_ref = refs[:n], refs[n : 2 * n], refs[2 * n]
         slopes, visc, sums, pulls, rhos, columns, gradients = refs[2 * n + 1 :]
         before = first_gives_before(axis)
         for side in range(2):
@@ -549,16 +597,12 @@
 
             lax.fori_loop(0, half, one, 0, unroll=min(half, 8))
 
-        def mine(c):
-            x, y, z = parts_of(c)
-            return press_ref[x, y, z, 0:1]
-
-        force_pairs(8, near, mine, rhos, columns, gradients, slopes, visc, sums, pulls)
+        force_pairs(near, spread_ref, rhos, columns, gradients, slopes, visc, sums, pulls, ready)
 
     return call(
         body,
         force_outputs(),
-        (*received, *press_received, press, *kept),
+        (*received, *press_received, spread, *kept),
         scratch=scratch_force(entries),
     )
 
@@ -577,7 +621,7 @@
                     u = sum(p[c] for p in pieces[0::2])
                     v = sum(p[c] for p in pieces[1::2])
                     plain, scaled = u[0:8] + u[8:16], u[16:24] + u[24:32]
-                    a0, b0 = u[32:33] + u[33:34], u[34:35] + u[35:36]
+                    a0, b0 = plain[6:7], scaled[6:7]
                     g = v[0:8] + v[8:16]
                     rho, weight = press_ref[x, y, z, 0:1], press_ref[x, y, z, 1:2]
                     inverse = 1.0 / rho
@@ -630,21 +674,24 @@
     fields = jnp.concatenate([positions, velocities, masses[None], alphas[None]], 0)
     own, *sends = gather_own(fields, counts)
     from_z = receive("gz", sends)
-    *kept_own, sums_own, weighted_own, own_feats = density_own(own)
+    half, features = density_own(own)
+    own_feats = features[0]
     from_y = receive("gy", pack_y(own, from_z, tile_rows))
-    *kept_z, sums_z, weighted_z = density_halo("z", "gz", from_z, own_feats)
+    *kept_z, sums_z = density_halo("z", "gz", from_z, own_feats)
     from_x = receive("gx", pack_x(own, from_z, from_y, tile_rows))
-    *kept_y, sums_y, weighted_y = density_halo("y", "gy", from_y, own_feats)
-    *kept_x, sums_x, weighted_x = density_halo("x", "gx", from_x, own_feats)
-    partials = (sums_own, weighted_own, sums_z, weighted_z, sums_y, weighted_y, sums_x, weighted_x)
-    press, first, *sends = pressure(own, partials)
+    *kept_y, sums_y = density_halo("y", "gy", from_y, own_feats)
+    *kept_own, sums_own = density_own_rest(half, features)
+    *kept_x, sums_x = density_halo("x", "gx", from_x, own_feats)
+    press, first, *sends = pressure(own, (sums_own, sums_z, sums_y, sums_x))
     press_z = receive("gz", sends)
-    forces = list(force_own(own, press, kept_own))
+    spread = spread_own(press)
+    forces = list(force_own(own, press, spread, kept_own))
+    kept_x[1] = viscous("x", *kept_x)
     press_y = receive("gy", pack_y(press, press_z, 2))
-    forces += force_halo("z", "gz", from_z, press_z, press, kept_z)
+    forces += force_halo("z", "gz", from_z, press_z, spread, kept_z)
     press_x = receive("gx", pack_x(press, press_z, press_y, 2))
-    forces += force_halo("y", "gy", from_y, press_y, press, kept_y)
-    forces += force_halo("x", "gx", from_x, press_x, press, kept_x)
+    forces += force_halo("y", "gy", from_y, press_y, spread, kept_y)
+    forces += force_halo("x", "gx", from_x, press_x, spread, kept_x, ready=True)
     return finish(own, press, first, forces)
 
 

time: 50.1 us -> 49.9 us (level)
    pallas_call x15 -> x18, Pallas kernels: 24.6 us -> 24.4 us  [call(): pl.pallas_call(body, out_shape=tuple(outs), in_specs=specs or [vmem] * le...]
  transfers between devices with their start and end apart: 10 -> 10, of which waited for: 5 -> 5; matrix products, arithmetic and copies ran while one was open for 0% -> 0% of each run, Pallas kernels for 29% -> 32%
where the time goes in v4:
time: 49.9 us; the launch traced here: 49.6 us
  Pallas kernels  24.4 us (49%)
  starting transfers between devices  13.7 us (27%)
  waiting for transfers between devices  9.31 us (19%)
  other arithmetic  0.77 us (2%)
  between operations  0.73 us (1%)
  local copies, waits for them, and re-layouts  0.68 us (1%)
    pallas_call x18, Pallas kernels, call(): pl.pallas_call(body, out_shape=tuple(outs), in_specs=specs or [vmem] * le...  24.4 us
    ppermute x10, starting transfers between devices, receive(): got.append(lax.ppermute(send, axis, way))  13.7 us
    ppermute x10, waiting for transfers between devices, receive(): got.append(lax.ppermute(send, axis, way))  9.31 us
  transfers between devices with their start and end apart: 10, of which 5 were waited for; matrix products, arithmetic and copies ran while one was open for 0% of the time, Pallas kernels for 32%

profile of v4, /device:TPU:0, one launch (start us, length us, event | category | flops | bytes accessed | tf_op | source)
XLA Modules:
  0.0 49.6 jit_solution(1665561220827281630)
XLA Ops:
  0.6 0.8 %pad_maximum_fusion.fields_ref = f32[8,2,2,2,128]{4,3,2,1,0:T(2,128)S(1)} fusion(f32[1,2,2,2,128]{4,3,2,1,0:T(2,128)} %bitcast.2, f32[1,2,2,2,128]{4,3,2,1,0:T(2,128)} %bitcast.3, f32[3,2,2,2,128]{4,3,2,1,0:T(2,128)} %param.6, f32[3,2,2,2,128]{4,3,2,1,0:T(2,128)} %param.5), kind=kLoop, calls=%fused_computation | loop fusion | flops 24576 | bytes 65536 | tf_op jit(solution)/shard_map/concatenate | solution.py:674
  1.4 0.7 %copy-done = s32[2,2,2]{2,1,0:T(2,128)S(1)} copy-done((s32[2,2,2]{2,1,0:T(2,128)S(1)}, s32[2,2,2]{2,1,0:T(2,128)}, u32[]{:S(2)}) %copy-start) | copy-done | bytes 56
  2.2 3.1 %collective-permute-start = (f32[2,2,8,128]{3,2,1,0:T(8,128)S(1)}, f32[2,2,8,128]{3,2,1,0:T(8,128)S(1)}, u32[]{:S(2)}, u32[]{:S(2)}) collective-permute-start(f32[2,2,8,128]{3,2,1,0:T(8,128)S(1)} %get-tuple-element.50), channel_id=1, source_target_pairs={{0,1},{1,0},{2,3},{3,2},{4,5},{5,4},{6,7},{7,6},{8,9},{9,8},{10,11... | collective-permute-start | bytes 49160 | tf_op jit(solution)/shard_map/ppermute | solution.py:379
  5.3 2.5 %collective-permute-start.1 = (f32[2,2,8,128]{3,2,1,0:T(8,128)S(1)}, f32[2,2,8,128]{3,2,1,0:T(8,128)S(1)}, u32[]{:S(2)}, u32[]{:S(2)}) collective-permute-start(f32[2,2,8,128]{3,2,1,0:T(8,128)S(1)} %get-tuple-element.51), channel_id=1, source_target_pairs={{0,3},{1,2},{2,1},{3,0},{4,7},{5,6},{6,5},{7,4},{8,11},{9,10},{10,... | collective-permute-start | bytes 49160 | tf_op jit(solution)/shard_map/ppermute | solution.py:379
  7.8 3.1 %collective-permute-done.1.refs_1_ = f32[2,2,8,128]{3,2,1,0:T(8,128)S(1)} collective-permute-done((f32[2,2,8,128]{3,2,1,0:T(8,128)S(1)}, f32[2,2,8,128]{3,2,1,0:T(8,128)S(1)}, u32[]{:S(2)}, u32[]{:S(2)}) %collective-permute-start.1) | collective-permute-done | bytes 16416 | tf_op jit(solution)/shard_map/ppermute | solution.py:379
  11.0 1.6 %collective-permute-start.3 = (f32[2,4,8,128]{3,2,1,0:T(8,128)S(1)}, f32[2,4,8,128]{3,2,1,0:T(8,128)S(1)}, u32[]{:S(2)}, u32[]{:S(2)}) collective-permute-start(f32[2,4,8,128]{3,2,1,0:T(8,128)S(1)} %get-tuple-element.54), channel_id=1, source_target_pairs={{0,12},{4,8},{8,4},{12,0},{1,13},{5,9},{9,5},{13,1},{2,14},{6,10},... | collective-permute-start | bytes 98312 | tf_op jit(solution)/shard_map/ppermute | solution.py:379
  12.6 1.8 %collective-permute-done.3.refs_1_.refs_3_ = f32[2,4,8,128]{3,2,1,0:T(8,128)S(1)} collective-permute-done((f32[2,4,8,128]{3,2,1,0:T(8,128)S(1)}, f32[2,4,8,128]{3,2,1,0:T(8,128)S(1)}, u32[]{:S(2)}, u32[]{:S(2)}) %collective-permute-start.3) | collective-permute-done | bytes 32800 | tf_op jit(solution)/shard_map/ppermute | solution.py:379
  14.4 1.6 %collective-permute-start.4 = (f32[2,4,4,8,128]{4,3,2,1,0:T(8,128)S(1)}, f32[2,4,4,8,128]{4,3,2,1,0:T(8,128)S(1)}, u32[]{:S(2)}, u32[]{:S(2)}) collective-permute-start(f32[2,4,4,8,128]{4,3,2,1,0:T(8,128)S(1)} %shard_map.82), channel_id=1, source_target_pairs={{0,16},{16,0},{1,17},{17,1},{2,18},{18,2},{3,19},{19,3},{4,20},{20... | collective-permute-start | bytes 393224 | tf_op jit(solution)/shard_map/ppermute | solution.py:379
  15.9 1.7 %shard_map.77 = (bf16[8,8,128,256]{3,2,1,0:T(8,128)(2,1)S(1)}, f32[8,8,128,256]{3,2,1,0:T(8,128)S(1)}, f32[8,40,128]{2,1,0:T(8,128)S(1)}, bf16[8,128,48]{2,1,0:T...) custom-call(f32[2,2,2,8,128]{4,3,2,1,0:T(8,128)S(1)} %get-tuple-elemen, ...), custom_call_target="tpu_custom_call" | custom-call | tf_op jit(solution)/shard_map/pallas_call | solution.py:338
  17.6 1.5 %shard_map.78 = (bf16[8,8,128,256]{3,2,1,0:T(8,128)(2,1)S(1)}, f32[8,8,128,256]{3,2,1,0:T(8,128)S(1)}, f32[8,40,128]{2,1,0:T(8,128)S(1)}) custom-call(bf16[8,128,48]{2,1,0:T(8,128)(2,1)S(1)} %get-tuple-element.42.table_ref.refs_2_.refs_1_, ...), custom_call_target="tpu_custom_call", output_to_operand_aliasing={{0}: (4, {}), {1}: (5, {}), {2}: (6, {})} | custom-call | tf_op jit(solution)/shard_map/pallas_call | solution.py:338
  19.1 2.3 %shard_map.79 = (bf16[8,4,128,256]{3,2,1,0:T(8,128)(2,1)S(1)}, f32[8,4,128,256]{3,2,1,0:T(8,128)S(1)}, f32[8,40,128]{2,1,0:T(8,128)S(1)}) custom-call(f32[2,2,8,128]{3,2,1,0:T(8,128)S(1)} %collective-permute-done.refs_0_, f32[2,2,8,128]{3,2,1,0:T(8,128)S(1)} %collective-permute-done.1.refs_1_, bf16[8,128,48]{2,1,0:T(8,128)(2,1)S(1)} %get-tuple-element.42.table_ref.refs_2_.refs_1_), custom_call_target="tpu_custom_call" | custom-call | tf_op jit(solution)/shard_map/pallas_call | solution.py:338
  21.4 2.7 %shard_map.81 = (bf16[8,6,128,256]{3,2,1,0:T(8,128)(2,1)S(1)}, f32[8,6,128,256]{3,2,1,0:T(8,128)S(1)}, f32[8,40,128]{2,1,0:T(8,128)S(1)}) custom-call(f32[2,4,8,128]{3,2,1,0:T(8,128)S(1)} %collective-permute-done.2.refs_0_.refs_2_, f32[2,4,8,128]{3,2,1,0:T(8,128)S(1)} %collective-permute-done.3.refs_1_.refs_3_, ...), custom_call_target="tpu_custom_call" | custom-call | tf_op jit(solution)/shard_map/pallas_call | solution.py:338
  24.2 4.0 %shard_map.83 = (bf16[8,9,128,256]{3,2,1,0:T(8,128)(2,1)S(1)}, f32[8,9,128,256]{3,2,1,0:T(8,128)S(1)}, f32[8,40,128]{2,1,0:T(8,128)S(1)}) custom-call(f32[2,4,4,8,128]{4,3,2,1,0:T(8,128)S(1)} %collective-permute-done.4.refs_0_, bf16[8,128,48]{2,1,0:T(8,128)(2,1)S(1)} %get-tuple-element.42.table_ref.refs_2_.refs_1_), custom_call_target="tpu_custom_call" | custom-call | tf_op jit(solution)/shard_map/pallas_call | solution.py:338
  28.5 2.5 %collective-permute-start.6 = (f32[2,2,2,128]{3,2,1,0:T(2,128)S(1)}, f32[2,2,2,128]{3,2,1,0:T(2,128)S(1)}, u32[]{:S(2)}, u32[]{:S(2)}) collective-permute-start(f32[2,2,2,128]{3,2,1,0:T(2,128)S(1)} %get-tuple-element.64), channel_id=1, source_target_pairs={{0,3},{1,2},{2,1},{3,0},{4,7},{5,6},{6,5},{7,4},{8,11},{9,10},{10,... | collective-permute-start | bytes 12296 | tf_op jit(solution)/shard_map/ppermute | solution.py:379
  31.0 1.1 %collective-permute-done.5.refs_2_.refs_0_ = f32[2,2,2,128]{3,2,1,0:T(2,128)S(1)} collective-permute-done((f32[2,2,2,128]{3,2,1,0:T(2,128)S(1)}, f32[2,2,2,128]{3,2,1,0:T(2,128)S(1)}, u32[]{:S(2)}, u32[]{:S(2)}) %collective-permute-start.5) | collective-permute-done | bytes 4128 | tf_op jit(solution)/shard_map/ppermute | solution.py:379
  32.0 1.9 %collective-permute-done.6.refs_3_.refs_1_ = f32[2,2,2,128]{3,2,1,0:T(2,128)S(1)} collective-permute-done((f32[2,2,2,128]{3,2,1,0:T(2,128)S(1)}, f32[2,2,2,128]{3,2,1,0:T(2,128)S(1)}, u32[]{:S(2)}, u32[]{:S(2)}) %collective-permute-start.6) | collective-permute-done | bytes 4128 | tf_op jit(solution)/shard_map/ppermute | solution.py:379
  34.0 1.6 %collective-permute-start.8 = (f32[2,4,2,128]{3,2,1,0:T(2,128)S(1)}, f32[2,4,2,128]{3,2,1,0:T(2,128)S(1)}, u32[]{:S(2)}, u32[]{:S(2)}) collective-permute-start(f32[2,4,2,128]{3,2,1,0:T(2,128)S(1)} %get-tuple-element.70), channel_id=1, source_target_pairs={{0,12},{4,8},{8,4},{12,0},{1,13},{5,9},{9,5},{13,1},{2,14},{6,10},... | collective-permute-start | bytes 24584 | tf_op jit(solution)/shard_map/ppermute | solution.py:379
  35.6 1.5 %collective-permute-done.8.refs_3_ = f32[2,4,2,128]{3,2,1,0:T(2,128)S(1)} collective-permute-done((f32[2,4,2,128]{3,2,1,0:T(2,128)S(1)}, f32[2,4,2,128]{3,2,1,0:T(2,128)S(1)}, u32[]{:S(2)}, u32[]{:S(2)}) %collective-permute-start.8) | collective-permute-done | bytes 8224 | tf_op jit(solution)/shard_map/ppermute | solution.py:379
  38.1 1.3 %shard_map.91.refs_4_ = f32[8,9,128,128]{3,2,1,0:T(8,128)S(1)} custom-call(bf16[8,9,128,256]{3,2,1,0:T(8,128)(2,1)S(1)} %get-tuple-element.75.slopes_ref.refs_3_, f32[8,9,128,256]{3,2,1,0:T(8,128)S(1)} %get-tuple-element.76.pairs_ref), custom_call_target="tpu_custom_call" | custom-call | tf_op jit(solution)/shard_map/pallas_call | solution.py:338
  39.4 2.5 %shard_map.86 = (f32[8,32,128]{2,1,0:T(8,128)S(1)}, f32[8,16,128]{2,1,0:T(8,128)S(1)}) custom-call(f32[2,2,2,8,128]{4,3,2,1,0:T(8,128)S(1)} %get-tuple-element.41.own_ref, f32[2,2,2,2,128]{4,3,2,1,0:T(2,128)S(1)} %get-tuple-element.57.press_ref.own_ref, f32[8,128,128]{2,1,0:T(8,128)S(1)} %shard_map.85.spread_ref.refs_4_.refs_2_, ...), custom_call_target="tpu_custom_call" | custom-call | tf_op jit(solution)/shard_map/pallas_call | solution.py:338
  41.9 1.5 %shard_map.87 = (f32[8,32,128]{2,1,0:T(8,128)S(1)}, f32[8,16,128]{2,1,0:T(8,128)S(1)}) custom-call(f32[2,2,8,128]{3,2,1,0:T(8,128)S(1)} %collective-permute-done.refs_0_, f32[2,2,8,128]{3,2,1,0:T(8,128)S(1)} %collective-permute-done.1.refs_1_, f32[2,2,2,128]{3,2,1,0:T(2,128)S(1)} %collective-permute-done.5.refs_2_.refs_0_, ...), custom_call_target="tpu_custom_call" | custom-call | tf_op jit(solution)/shard_map/pallas_call | solution.py:338
  43.3 2.1 %shard_map.89 = (f32[8,32,128]{2,1,0:T(8,128)S(1)}, f32[8,16,128]{2,1,0:T(8,128)S(1)}) custom-call(f32[2,4,8,128]{3,2,1,0:T(8,128)S(1)} %collective-permute-done.2.refs_0_.refs_2_, f32[2,4,8,128]{3,2,1,0:T(8,128)S(1)} %collective-permute-done.3.refs_1_.refs_3_, f32[2,4,2,128]{3,2,1,0:T(2,128)S(1)} %collective-permute-done.7.refs_2_, ...), custom_call_target="tpu_custom_call" | custom-call | tf_op jit(solution)/shard_map/pallas_call | solution.py:338
  45.4 3.4 %shard_map.92 = (f32[8,32,128]{2,1,0:T(8,128)S(1)}, f32[8,16,128]{2,1,0:T(8,128)S(1)}) custom-call(f32[2,4,4,8,128]{4,3,2,1,0:T(8,128)S(1)} %collective-permute-done.4.refs_0_, f32[2,4,4,2,128]{4,3,2,1,0:T(2,128)S(1)} %collective-permute-done.9.refs_1_, f32[8,128,128]{2,1,0:T(8,128)S(1)} %shard_map.85.spread_ref.refs_4_.refs_2_, ...), custom_call_target="tpu_custom_call" | custom-call | tf_op jit(solution)/shard_map/pallas_call | solution.py:338
  48.8 0.7 %shard_map.93 = (f32[2,2,2,128]{3,2,1,0:T(2,128)}, f32[3,2,2,2,128]{4,3,2,1,0:T(2,128)}, f32[2,2,2,128]{3,2,1,0:T(2,128)}) custom-call(f32[2,2,2,8,128]{4,3,2,1,0:T(8,128)S(1)} %get-tuple-element.41.own_ref, f32[2,2,2,2,128]{4,3,2,1,0:T(2,128)S(1)} %get-tuple-element.57.press_ref.own_ref, f32[8,8,128]{2,1,0:T(8,128)S(1)} %get-tuple-element.58.first_ref, ...), custom_call_target="tpu_custom_call" | custom-call | tf_op jit(solution)/shard_map/pallas_call | solution.py:338
  (17 shorter events, 1.5 us)
Async XLA Ops:
  1.4 0.7 %copy-start = (s32[2,2,2]{2,1,0:T(2,128)S(1)}, s32[2,2,2]{2,1,0:T(2,128)}, u32[]{:S(2)}) copy-start(s32[2,2,2]{2,1,0:T(2,128)} %counts_ref.1) | copy-start | bytes 100
  2.2 5.6 %collective-permute-start = (f32[2,2,8,128]{3,2,1,0:T(8,128)S(1)}, f32[2,2,8,128]{3,2,1,0:T(8,128)S(1)}, u32[]{:S(2)}, u32[]{:S(2)}) collective-permute-start(f32[2,2,8,128]{3,2,1,0:T(8,128)S(1)} %get-tuple-element.50), channel_id=1, source_target_pairs={{0,1},{1,0},{2,3},{3,2},{4,5},{5,4},{6,7},{7,6},{8,9},{9,8},{10,11... | collective-permute-start | bytes 49160 | tf_op jit(solution)/shard_map/ppermute | solution.py:379
  5.3 5.5 %collective-permute-start.1 = (f32[2,2,8,128]{3,2,1,0:T(8,128)S(1)}, f32[2,2,8,128]{3,2,1,0:T(8,128)S(1)}, u32[]{:S(2)}, u32[]{:S(2)}) collective-permute-start(f32[2,2,8,128]{3,2,1,0:T(8,128)S(1)} %get-tuple-element.51), channel_id=1, source_target_pairs={{0,3},{1,2},{2,1},{3,0},{4,7},{5,6},{6,5},{7,4},{8,11},{9,10},{10,... | collective-permute-start | bytes 49160 | tf_op jit(solution)/shard_map/ppermute | solution.py:379
  10.9 1.7 %collective-permute-start.2 = (f32[2,4,8,128]{3,2,1,0:T(8,128)S(1)}, f32[2,4,8,128]{3,2,1,0:T(8,128)S(1)}, u32[]{:S(2)}, u32[]{:S(2)}) collective-permute-start(f32[2,4,8,128]{3,2,1,0:T(8,128)S(1)} %get-tuple-element.53), channel_id=1, source_target_pairs={{0,4},{4,0},{8,12},{12,8},{1,5},{5,1},{9,13},{13,9},{2,6},{6,2},{1... | collective-permute-start | bytes 98312 | tf_op jit(solution)/shard_map/ppermute | solution.py:379
  11.0 3.4 %collective-permute-start.3 = (f32[2,4,8,128]{3,2,1,0:T(8,128)S(1)}, f32[2,4,8,128]{3,2,1,0:T(8,128)S(1)}, u32[]{:S(2)}, u32[]{:S(2)}) collective-permute-start(f32[2,4,8,128]{3,2,1,0:T(8,128)S(1)} %get-tuple-element.54), channel_id=1, source_target_pairs={{0,12},{4,8},{8,4},{12,0},{1,13},{5,9},{9,5},{13,1},{2,14},{6,10},... | collective-permute-start | bytes 98312 | tf_op jit(solution)/shard_map/ppermute | solution.py:379
  14.4 9.8 %collective-permute-start.4 = (f32[2,4,4,8,128]{4,3,2,1,0:T(8,128)S(1)}, f32[2,4,4,8,128]{4,3,2,1,0:T(8,128)S(1)}, u32[]{:S(2)}, u32[]{:S(2)}) collective-permute-start(f32[2,4,4,8,128]{4,3,2,1,0:T(8,128)S(1)} %shard_map.82), channel_id=1, source_target_pairs={{0,16},{16,0},{1,17},{17,1},{2,18},{18,2},{3,19},{19,3},{4,20},{20... | collective-permute-start | bytes 393224 | tf_op jit(solution)/shard_map/ppermute | solution.py:379
  28.4 3.7 %collective-permute-start.5 = (f32[2,2,2,128]{3,2,1,0:T(2,128)S(1)}, f32[2,2,2,128]{3,2,1,0:T(2,128)S(1)}, u32[]{:S(2)}, u32[]{:S(2)}) collective-permute-start(f32[2,2,2,128]{3,2,1,0:T(2,128)S(1)} %get-tuple-element.63), channel_id=1, source_target_pairs={{0,1},{1,0},{2,3},{3,2},{4,5},{5,4},{6,7},{7,6},{8,9},{9,8},{10,11... | collective-permute-start | bytes 12296 | tf_op jit(solution)/shard_map/ppermute | solution.py:379
  28.5 5.5 %collective-permute-start.6 = (f32[2,2,2,128]{3,2,1,0:T(2,128)S(1)}, f32[2,2,2,128]{3,2,1,0:T(2,128)S(1)}, u32[]{:S(2)}, u32[]{:S(2)}) collective-permute-start(f32[2,2,2,128]{3,2,1,0:T(2,128)S(1)} %get-tuple-element.64), channel_id=1, source_target_pairs={{0,3},{1,2},{2,1},{3,0},{4,7},{5,6},{6,5},{7,4},{8,11},{9,10},{10,... | collective-permute-start | bytes 12296 | tf_op jit(solution)/shard_map/ppermute | solution.py:379
  33.9 1.7 %collective-permute-start.7 = (f32[2,4,2,128]{3,2,1,0:T(2,128)S(1)}, f32[2,4,2,128]{3,2,1,0:T(2,128)S(1)}, u32[]{:S(2)}, u32[]{:S(2)}) collective-permute-start(f32[2,4,2,128]{3,2,1,0:T(2,128)S(1)} %get-tuple-element.69), channel_id=1, source_target_pairs={{0,4},{4,0},{8,12},{12,8},{1,5},{5,1},{9,13},{13,9},{2,6},{6,2},{1... | collective-permute-start | bytes 24584 | tf_op jit(solution)/shard_map/ppermute | solution.py:379
  34.0 3.1 %collective-permute-start.8 = (f32[2,4,2,128]{3,2,1,0:T(2,128)S(1)}, f32[2,4,2,128]{3,2,1,0:T(2,128)S(1)}, u32[]{:S(2)}, u32[]{:S(2)}) collective-permute-start(f32[2,4,2,128]{3,2,1,0:T(2,128)S(1)} %get-tuple-element.70), channel_id=1, source_target_pairs={{0,12},{4,8},{8,4},{12,0},{1,13},{5,9},{9,5},{13,1},{2,14},{6,10},... | collective-permute-start | bytes 24584 | tf_op jit(solution)/shard_map/ppermute | solution.py:379
  37.2 8.2 %collective-permute-start.9 = (f32[2,4,4,2,128]{4,3,2,1,0:T(2,128)S(1)}, f32[2,4,4,2,128]{4,3,2,1,0:T(2,128)S(1)}, u32[]{:S(2)}, u32[]{:S(2)}) collective-permute-start(f32[2,4,4,2,128]{4,3,2,1,0:T(2,128)S(1)} %shard_map.90), channel_id=1, source_target_pairs={{0,16},{16,0},{1,17},{17,1},{2,18},{18,2},{3,19},{19,3},{4,20},{20... | collective-permute-start | bytes 98312 | tf_op jit(solution)/shard_map/ppermute | solution.py:379

commit v5 on v4

--- a/solution.py
+++ b/solution.py
@@ -130,13 +130,11 @@
     pass
 
 
-def over_cells(start, stop, body):
-    lax.fori_loop(
-        start // together, stop // together, lambda i, _: body([i * together + j for j in range(together)]), 0
-    )
-
-
-def density_pairs(own, cells, near, feats, masses, columns, slopes, pairs, sums, weighted):
+def over_cells(body):
+    lax.fori_loop(0, 8 // together, lambda i, _: body([i * together + j for j in range(together)]), 0)
+
+
+def density_pairs(own, near, feats, masses, columns, slopes, pairs, sums, weighted):
     ones = jnp.ones((tile_rows, 256), bf16)
 
     def some(group):
@@ -177,25 +175,7 @@
         pipelined(tiles, (geometry, idle, terms, idle, reduce))
         return 0
 
-    over_cells(*cells, some)
-
-
-def viscous(group, slopes, pairs):
-    count = groups[group][3]
-
-    def body(slopes_ref, pairs_ref, visc):
-        def one(c, _):
-            for k in range(count):
-                for r in range(0, 128, 16):
-                    at = slice(r, r + 16)
-                    g = slopes_ref[c, k, at, :128].astype(f32) + slopes_ref[c, k, at, 128:].astype(f32)
-                    run = jnp.minimum(pairs_ref[c, k, at, 128:], 0.0)
-                    visc[c, k, at] = g * run * (1.0 / (pairs_ref[c, k, at, :128] + 0.01))
-            return 0
-
-        lax.fori_loop(0, 8, one, 0)
-
-    return call(body, [shaped(8, count, 128, 128)], (slopes, pairs), limit=4)[0]
+    over_cells(some)
 
 
 def prepare_force(tile, offsets, press, at, rhos, columns, gradients):
@@ -214,7 +194,7 @@
     rhos[at] = jnp.broadcast_to(rho, (16, 128))
 
 
-def force_pairs(near, spread, rhos, columns, gradients, slopes, visc, sums, pulls, ready):
+def force_pairs(near, spread, rhos, columns, gradients, slopes, pairs, sums, pulls):
     def some(group):
         mixed, sofar, pulled = {}, {}, {}
         picks = [near(c) for c in group]
@@ -227,12 +207,9 @@
             for r in range(0, 128, 16):
                 at = slice(r, r + 16)
                 below = theirs + spread[c, at]
-                if ready:
-                    t = visc[c, k, at] * (1.0 / below)
-                else:
-                    g = slopes[c, k, at, :128].astype(f32) + slopes[c, k, at, 128:].astype(f32)
-                    run = jnp.minimum(visc[c, k, at, 128:], 0.0)
-                    t = g * run * (1.0 / ((visc[c, k, at, :128] + 0.01) * below))
+                g = slopes[c, k, at, :128].astype(f32) + slopes[c, k, at, 128:].astype(f32)
+                run = jnp.minimum(pairs[c, k, at, 128:], 0.0)
+                t = g * run * (1.0 / ((pairs[c, k, at, :128] + 0.01) * below))
                 high = t.astype(bf16)
                 highs.append(high)
                 lows.append((t - high.astype(f32)).astype(bf16))
@@ -251,7 +228,7 @@
         pipelined(tiles, (terms, reduce))
         return 0
 
-    over_cells(0, 8, some)
+    over_cells(some)
 
 
 def parts_of(c):
@@ -274,14 +251,14 @@
     return [flat((2, cz), (2, x), (2, y)) for x in range(2) for y in range(2)]
 
 
+def near_x(c):
+    cx, _, cz = parts_of(c)
+    return [flat((2, cx), (2, y), (4, cz + dz)) for y in range(2) for dz in range(3)]
+
+
 def near_y(c):
-    _, cy, cz = parts_of(c)
-    return [flat((2, cy), (2, x), (4, cz + dz)) for x in range(2) for dz in range(3)]
-
-
-def near_x(c):
     cx, cy, cz = parts_of(c)
-    return [flat((2, cx), (4, cy + dy), (4, cz + dz)) for dy in range(3) for dz in range(3)]
+    return [flat((2, cy), (4, cx + dx), (4, cz + dz)) for dx in range(3) for dz in range(3)]
 
 
 def place_own(e):
@@ -294,12 +271,12 @@
     return x - 1, y - 1, 3 * side - 2
 
 
+def place_x(e):
+    return 3 * (e // 8) - 2, (e // 4) % 2 - 1, e % 4 - 2
+
+
 def place_y(e):
-    return (e // 4) % 2 - 1, 3 * (e // 8) - 2, e % 4 - 2
-
-
-def place_x(e):
-    return 3 * (e // 16) - 2, (e // 4) % 4 - 2, e % 4 - 2
+    return (e // 4) % 4 - 2, 3 * (e // 16) - 2, e % 4 - 2
 
 
 def offsets_of(place):
@@ -309,8 +286,8 @@
 groups = {
     "own": (8, near_own, place_own, 8),
     "z": (8, near_z, place_z, 4),
-    "y": (16, near_y, place_y, 6),
-    "x": (32, near_x, place_x, 9),
+    "x": (16, near_x, place_x, 6),
+    "y": (32, near_y, place_y, 9),
 }
 
 
@@ -334,7 +311,7 @@
     ]
 
 
-def call(body, outs, operands, specs=None, scratch=(), limit=12, aliases={}):
+def call(body, outs, operands, specs=None, scratch=(), limit=12):
     return pl.pallas_call(
         body,
         out_shape=tuple(outs),
@@ -342,7 +319,6 @@
         out_specs=tuple([vmem] * len(outs)),
         scratch_shapes=list(scratch),
         compiler_params=pltpu.CompilerParams(vmem_limit_bytes=limit << 20),
-        input_output_aliases=aliases,
     )(*operands)
 
 
@@ -380,52 +356,52 @@
     return tuple(got)
 
 
-def pack_y(own, from_z, rows):
-    sends = send_shapes("gy", (2, 4, rows, 128))
+def pack_x(own, from_z, rows):
+    sends = send_shapes("gx", (2, 4, rows, 128))
     n = len(from_z)
 
     def body(own_ref, *refs):
         got, out = refs[:n], refs[n:]
-        high = first_sends_high("gy")
+        high = first_sends_high("gx")
         before = first_gives_before("gz")
-        for x in range(2):
+        for y in range(2):
             for e in range(4):
 
-                def tile_at(y, x=x, e=e):
+                def tile_at(x, y=y, e=e):
                     if 1 <= e <= 2:
                         return own_ref[x, y, e - 1]
                     return take_side(before, got, 0 if e == 0 else 1, (x, y))
 
-                put_sends(out, high, tile_at, (x, e))
+                put_sends(out, high, tile_at, (y, e))
 
     return call(body, sends, (own, *from_z), limit=4)
 
 
-def pack_x(own, from_z, from_y, rows):
-    sends = send_shapes("gx", (4, 4, rows, 128))
-    n, m = len(from_z), len(from_y)
+def pack_y(own, from_z, from_x, rows):
+    sends = send_shapes("gy", (4, 4, rows, 128))
+    n, m = len(from_z), len(from_x)
 
     def body(own_ref, *refs):
-        got_z, got_y, out = refs[:n], refs[n : n + m], refs[n + m :]
-        high = first_sends_high("gx")
+        got_z, got_x, out = refs[:n], refs[n : n + m], refs[n + m :]
+        high = first_sends_high("gy")
         before_z = first_gives_before("gz")
-        before_y = first_gives_before("gy")
+        before_x = first_gives_before("gx")
         for a in range(4):
             for e in range(4):
 
-                def tile_at(x, a=a, e=e):
+                def tile_at(y, a=a, e=e):
                     if not 1 <= a <= 2:
-                        return take_side(before_y, got_y, 0 if a == 0 else 1, (x, e))
+                        return take_side(before_x, got_x, 0 if a == 0 else 1, (y, e))
                     if 1 <= e <= 2:
-                        return own_ref[x, a - 1, e - 1]
-                    return take_side(before_z, got_z, 0 if e == 0 else 1, (x, a - 1))
+                        return own_ref[a - 1, y, e - 1]
+                    return take_side(before_z, got_z, 0 if e == 0 else 1, (a - 1, y))
 
                 put_sends(out, high, tile_at, (a, e))
 
-    return call(body, sends, (own, *from_z, *from_y), limit=4)
-
-
-inner_dims = {"z": (2, 2), "y": (2, 4), "x": (4, 4)}
+    return call(body, sends, (own, *from_z, *from_x), limit=4)
+
+
+inner_dims = {"z": (2, 2), "x": (2, 4), "y": (4, 4)}
 
 
 def entry_tile(group, before, refs, e, sides):
@@ -447,31 +423,10 @@
             return 0
 
         lax.fori_loop(0, 8, one, 0, unroll=8)
-        density_pairs(table_ref, (0, 4), near, feats, masses, columns, slopes, pairs, sums, weighted)
-
-    outs = pair_outputs(count) + [
-        shaped(8, 128, feature_rows, kind=bf16),
-        shaped(entries, feature_rows, 256, kind=bf16),
-        shaped(entries, 16, 128),
-        shaped(entries, 32, 256, kind=bf16),
-    ]
-    got = call(body, outs, (own,), scratch=[weights])
-    return got[:3], got[3:]
-
-
-def density_own_rest(kept, features):
-    _, near, _, count = groups["own"]
-
-    def body(table_ref, feats, masses, columns, _slopes, _pairs, _sums, slopes, pairs, sums, weighted):
-        density_pairs(table_ref, (4, 8), near, feats, masses, columns, slopes, pairs, sums, weighted)
-
-    return call(
-        body,
-        pair_outputs(count),
-        (*features, *kept),
-        scratch=[weights],
-        aliases={4 + i: i for i in range(3)},
-    )
+        density_pairs(table_ref, near, feats, masses, columns, slopes, pairs, sums, weighted)
+
+    outs = pair_outputs(count) + [shaped(8, 128, feature_rows, kind=bf16)]
+    return call(body, outs, (own,), scratch=scratch_density(entries))
 
 
 def density_halo(group, axis, received, own_feats):
@@ -492,7 +447,7 @@
                 return 0
 
             lax.fori_loop(0, half, one, 0, unroll=min(half, 8))
-        density_pairs(own_ref, (0, 8), near, feats, masses, columns, slopes, pairs, sums, weighted)
+        density_pairs(own_ref, near, feats, masses, columns, slopes, pairs, sums, weighted)
 
     return call(body, pair_outputs(count), (*received, own_feats), scratch=scratch_density(entries))
 
@@ -559,10 +514,10 @@
     return [shaped(8, 32, 128), shaped(8, 16, 128)]
 
 
-def force_own(own, press, spread, kept, ready=False):
+def force_own(own, press, spread, kept):
     entries, near, place, _ = groups["own"]
 
-    def body(own_ref, press_ref, spread_ref, slopes, visc, sums, pulls, rhos, columns, gradients):
+    def body(own_ref, press_ref, spread_ref, slopes, pairs, sums, pulls, rhos, columns, gradients):
         def one(c, _):
             x, y, z = parts_of(c)
             prepare_force(
@@ -572,19 +527,19 @@
 
         lax.fori_loop(0, 8, one, 0, unroll=8)
 
-        force_pairs(near, spread_ref, rhos, columns, gradients, slopes, visc, sums, pulls, ready)
+        force_pairs(near, spread_ref, rhos, columns, gradients, slopes, pairs, sums, pulls)
 
     return call(body, force_outputs(), (own, press, spread, *kept), scratch=scratch_force(entries))
 
 
-def force_halo(group, axis, received, press_received, spread, kept, ready=False):
+def force_halo(group, axis, received, press_received, spread, kept):
     entries, near, place, _ = groups[group]
     n = len(received)
     half = entries // 2
 
     def body(*refs):
         got, got_press, spread_ref = refs[:n], refs[n : 2 * n], refs[2 * n]
-        slopes, visc, sums, pulls, rhos, columns, gradients = refs[2 * n + 1 :]
+        slopes, pairs, sums, pulls, rhos, columns, gradients = refs[2 * n + 1 :]
         before = first_gives_before(axis)
         for side in range(2):
 
@@ -597,7 +552,7 @@
 
             lax.fori_loop(0, half, one, 0, unroll=min(half, 8))
 
-        force_pairs(near, spread_ref, rhos, columns, gradients, slopes, visc, sums, pulls, ready)
+        force_pairs(near, spread_ref, rhos, columns, gradients, slopes, pairs, sums, pulls)
 
     return call(
         body,
@@ -650,48 +605,63 @@
     return call(body, outs, (own, press, first, *partials), limit=8)
 
 
-def gather_own(fields, counts):
+def gather_own(*arguments):
     sends = send_shapes("gz", (2, 2, tile_rows, 128))
 
-    def body(fields_ref, counts_ref, own, *out):
+    def body(*refs):
+        sources, own, out = refs[:5], refs[5], refs[6 : 6 + len(sends)]
+        held, arrived = refs[6 + len(sends) : -1], refs[-1]
+        copies = [pltpu.make_async_copy(a, b, arrived.at[i]) for i, (a, b) in enumerate(zip(sources, held))]
+        for copy in copies:
+            copy.start()
+        for copy in copies:
+            copy.wait()
+        pos, vel, mass, alpha, count = held
         high = first_sends_high("gz")
-        alone = row_ids() == 6
-        lanes = lax.broadcasted_iota(jnp.int32, (tile_rows, 128), 1)
+        lanes = lax.broadcasted_iota(jnp.int32, (1, 128), 1)
         for x in range(2):
             for y in range(2):
                 for z in range(2):
-                    dead = lanes >= counts_ref[x, y : y + 1, z : z + 1]
-                    tile = rows_of(*(fields_ref[i, x, y, z : z + 1, :] for i in range(tile_rows)))
-                    own[x, y, z] = jnp.where(alone & dead, 0.0, tile)
+                    dead = lanes >= count[x, y : y + 1, z : z + 1]
+                    own[x, y, z] = rows_of(
+                        *(pos[i, x, y, z : z + 1, :] for i in range(3)),
+                        *(vel[i, x, y, z : z + 1, :] for i in range(3)),
+                        jnp.where(dead, 0.0, mass[x, y, z : z + 1, :]),
+                        alpha[x, y, z : z + 1, :],
+                    )
         for x in range(2):
             for y in range(2):
                 put_sends(out, high, lambda z, x=x, y=y: own[x, y, z], (x, y))
 
-    return call(body, [shaped(2, 2, 2, tile_rows, 128)] + sends, (fields, counts), limit=4)
+    scratch = [pltpu.VMEM(a.shape, a.dtype) for a in arguments] + [pltpu.SemaphoreType.DMA((5,))]
+    return call(
+        body,
+        [shaped(2, 2, 2, tile_rows, 128)] + sends,
+        [pltpu.with_memory_space_constraint(a, pltpu.HBM) for a in arguments],
+        specs=[pl.BlockSpec(memory_space=pltpu.HBM)] * 5,
+        scratch=scratch,
+        limit=4,
+    )
 
 
 def per_block(positions, velocities, masses, alphas, counts):
-    fields = jnp.concatenate([positions, velocities, masses[None], alphas[None]], 0)
-    own, *sends = gather_own(fields, counts)
+    own, *sends = gather_own(positions, velocities, masses, alphas, counts)
     from_z = receive("gz", sends)
-    half, features = density_own(own)
-    own_feats = features[0]
-    from_y = receive("gy", pack_y(own, from_z, tile_rows))
+    *kept_own, sums_own, own_feats = density_own(own)
+    from_x = receive("gx", pack_x(own, from_z, tile_rows))
     *kept_z, sums_z = density_halo("z", "gz", from_z, own_feats)
-    from_x = receive("gx", pack_x(own, from_z, from_y, tile_rows))
+    from_y = receive("gy", pack_y(own, from_z, from_x, tile_rows))
+    *kept_x, sums_x = density_halo("x", "gx", from_x, own_feats)
     *kept_y, sums_y = density_halo("y", "gy", from_y, own_feats)
-    *kept_own, sums_own = density_own_rest(half, features)
-    *kept_x, sums_x = density_halo("x", "gx", from_x, own_feats)
-    press, first, *sends = pressure(own, (sums_own, sums_z, sums_y, sums_x))
+    press, first, *sends = pressure(own, (sums_own, sums_z, sums_x, sums_y))
     press_z = receive("gz", sends)
     spread = spread_own(press)
     forces = list(force_own(own, press, spread, kept_own))
-    kept_x[1] = viscous("x", *kept_x)
-    press_y = receive("gy", pack_y(press, press_z, 2))
+    press_x = receive("gx", pack_x(press, press_z, 2))
     forces += force_halo("z", "gz", from_z, press_z, spread, kept_z)
-    press_x = receive("gx", pack_x(press, press_z, press_y, 2))
+    press_y = receive("gy", pack_y(press, press_z, press_x, 2))
+    forces += force_halo("x", "gx", from_x, press_x, spread, kept_x)
     forces += force_halo("y", "gy", from_y, press_y, spread, kept_y)
-    forces += force_halo("x", "gx", from_x, press_x, spread, kept_x, ready=True)
     return finish(own, press, first, forces)
 
 

time: 49.9 us -> 49.3 us (0.988)
  waiting for transfers between devices: 9.31 us -> 11 us
  Pallas kernels: 24.4 us -> 23.6 us
  other arithmetic: 0.77 us -> 0 us
  local copies, waits for them, and re-layouts: 0.68 us -> 0 us
    ppermute x10, waiting for transfers between devices: 9.31 us -> 11 us  [receive(): got.append(lax.ppermute(send, axis, way))]
    concatenate x1 -> x0, other arithmetic: 0.77 us -> none  [per_block(): jnp.concatenate([positions, velocities, masses[None], alphas[None]], 0)]
    pallas_call x18 -> x16, Pallas kernels: 24.4 us -> 23.6 us  [call(): pl.pallas_call(body, out_shape=tuple(outs), in_specs=specs or [vmem] * le...]
    unnamed x2 -> x0, local copies, waits for them, and re-layouts: 0.68 us -> none
  transfers between devices with their start and end apart: 10 -> 10, of which waited for: 5 -> 5; matrix products, arithmetic and copies ran while one was open for 0% -> 0% of each run, Pallas kernels for 32% -> 29%
where the time goes in v5:
time: 49.3 us; the launch traced here: 49.1 us
  Pallas kernels  23.6 us (48%)
  starting transfers between devices  13.7 us (28%)
  waiting for transfers between devices  11 us (22%)
  between operations  0.72 us (1%)
    pallas_call x16, Pallas kernels, call(): pl.pallas_call(body, out_shape=tuple(outs), in_specs=specs or [vmem] * le...  23.6 us
    ppermute x10, starting transfers between devices, receive(): got.append(lax.ppermute(send, axis, way))  13.7 us
    ppermute x10, waiting for transfers between devices, receive(): got.append(lax.ppermute(send, axis, way))  11 us
  transfers between devices with their start and end apart: 10, of which 5 were waited for; matrix products, arithmetic and copies ran while one was open for 0% of the time, Pallas kernels for 29%

profile of v5, /device:TPU:0, one launch (start us, length us, event | category | flops | bytes accessed | tf_op | source)
XLA Modules:
  0.0 49.1 jit_solution(13173659434586188761)
XLA Ops:
  0.6 0.9 %shard_map.76 = (f32[2,2,2,8,128]{4,3,2,1,0:T(8,128)S(1)}, f32[2,2,8,128]{3,2,1,0:T(8,128)S(1)}, f32[2,2,8,128]{3,2,1,0:T(8,128)S(1)}) custom-call(f32[3,2,2,2,128]{4,3,2,1,0:T(2,128)} %refs_0_.1, f32[3,2,2,2,128]{4,3,2,1,0:T(2,128)} %refs_1_.1, f32[2,2,2,128]{3,2,1,0:T(2,128)} %refs_2_.1, f32[2,2,2,128]{3,2,1,0:T(2,128)} %refs_3_.1, s32[2,2,2]{2,1,0:T(2,128)} %refs_4_.1), custom_call_target="tpu_custom_call" | custom-call | tf_op jit(solution)/shard_map/pallas_call | solution.py:315
  1.5 3.1 %collective-permute-start = (f32[2,2,8,128]{3,2,1,0:T(8,128)S(1)}, f32[2,2,8,128]{3,2,1,0:T(8,128)S(1)}, u32[]{:S(2)}, u32[]{:S(2)}) collective-permute-start(f32[2,2,8,128]{3,2,1,0:T(8,128)S(1)} %get-tuple-element.37), channel_id=1, source_target_pairs={{0,1},{1,0},{2,3},{3,2},{4,5},{5,4},{6,7},{7,6},{8,9},{9,8},{10,11... | collective-permute-start | bytes 49160 | tf_op jit(solution)/shard_map/ppermute | solution.py:355
  4.6 2.5 %collective-permute-start.1 = (f32[2,2,8,128]{3,2,1,0:T(8,128)S(1)}, f32[2,2,8,128]{3,2,1,0:T(8,128)S(1)}, u32[]{:S(2)}, u32[]{:S(2)}) collective-permute-start(f32[2,2,8,128]{3,2,1,0:T(8,128)S(1)} %get-tuple-element.38), channel_id=1, source_target_pairs={{0,3},{1,2},{2,1},{3,0},{4,7},{5,6},{6,5},{7,4},{8,11},{9,10},{10,... | collective-permute-start | bytes 49160 | tf_op jit(solution)/shard_map/ppermute | solution.py:355
  7.1 3.1 %collective-permute-done.1.refs_1_ = f32[2,2,8,128]{3,2,1,0:T(8,128)S(1)} collective-permute-done((f32[2,2,8,128]{3,2,1,0:T(8,128)S(1)}, f32[2,2,8,128]{3,2,1,0:T(8,128)S(1)}, u32[]{:S(2)}, u32[]{:S(2)}) %collective-permute-start.1) | collective-permute-done | bytes 16416 | tf_op jit(solution)/shard_map/ppermute | solution.py:355
  10.2 1.6 %collective-permute-start.2 = (f32[2,2,4,8,128]{4,3,2,1,0:T(8,128)S(1)}, f32[2,2,4,8,128]{4,3,2,1,0:T(8,128)S(1)}, u32[]{:S(2)}, u32[]{:S(2)}) collective-permute-start(f32[2,2,4,8,128]{4,3,2,1,0:T(8,128)S(1)} %shard_map.79), channel_id=1, source_target_pairs={{0,16},{16,0},{1,17},{17,1},{2,18},{18,2},{3,19},{19,3},{4,20},{20... | collective-permute-start | bytes 196616 | tf_op jit(solution)/shard_map/ppermute | solution.py:355
  11.7 2.8 %collective-permute-done.2.refs_0_.refs_2_ = f32[2,2,4,8,128]{4,3,2,1,0:T(8,128)S(1)} collective-permute-done((f32[2,2,4,8,128]{4,3,2,1,0:T(8,128)S(1)}, f32[2,2,4,8,128]{4,3,2,1,0:T(8,128)S(1)}, u32[]{:S(2)}, u32[]{:S(2)}) %collective-permute-start.2) | collective-permute-done | bytes 65568 | tf_op jit(solution)/shard_map/ppermute | solution.py:355
  14.6 1.6 %collective-permute-start.4 = (f32[4,4,8,128]{3,2,1,0:T(8,128)S(1)}, f32[4,4,8,128]{3,2,1,0:T(8,128)S(1)}, u32[]{:S(2)}, u32[]{:S(2)}) collective-permute-start(f32[4,4,8,128]{3,2,1,0:T(8,128)S(1)} %get-tuple-element.43), channel_id=1, source_target_pairs={{0,12},{4,8},{8,4},{12,0},{1,13},{5,9},{9,5},{13,1},{2,14},{6,10},... | collective-permute-start | bytes 196616 | tf_op jit(solution)/shard_map/ppermute | solution.py:355
  16.2 3.2 %shard_map.77 = (bf16[8,8,128,256]{3,2,1,0:T(8,128)(2,1)S(1)}, f32[8,8,128,256]{3,2,1,0:T(8,128)S(1)}, f32[8,40,128]{2,1,0:T(8,128)S(1)}, bf16[8,128,48]{2,1,0:T(8,128)(2,1)S(1)}) custom-call(f32[2,2,2,8,128]{4,3,2,1,0:T(8,128)S(1)} %get-tuple-element.35.own_ref), custom_call_target="tpu_custom_call" | custom-call | tf_op jit(solution)/shard_map/pallas_call | solution.py:315
  19.5 2.1 %shard_map.78 = (bf16[8,4,128,256]{3,2,1,0:T(8,128)(2,1)S(1)}, f32[8,4,128,256]{3,2,1,0:T(8,128)S(1)}, f32[8,40,128]{2,1,0:T(8,128)S(1)}) custom-call(f32[2,2,8,128]{3,2,1,0:T(8,128)S(1)} %collective-permute-done.refs_0_, f32[2,2,8,128]{3,2,1,0:T(8,128)S(1)} %collective-permute-done.1.refs_1_, bf16[8,128,48]{2,1,0:T(8,128)(2,1)S(1)} %get-tuple-element.39.refs_2_.refs_1_), custom_call_target="tpu_custom_call" | custom-call | tf_op jit(solution)/shard_map/pallas_call | solution.py:315
  21.6 2.7 %shard_map.80 = (bf16[8,6,128,256]{3,2,1,0:T(8,128)(2,1)S(1)}, f32[8,6,128,256]{3,2,1,0:T(8,128)S(1)}, f32[8,40,128]{2,1,0:T(8,128)S(1)}) custom-call(f32[2,2,4,8,128]{4,3,2,1,0:T(8,128)S(1)} %collective-permute-done.2.refs_0_.refs_2_, bf16[8,128,48]{2,1,0:T(8,128)(2,1)S(1)} %get-tuple-element.39.refs_2_.refs_1_), custom_call_target="tpu_custom_call" | custom-call | tf_op jit(solution)/shard_map/pallas_call | solution.py:315
  24.4 4.0 %shard_map.82 = (bf16[8,9,128,256]{3,2,1,0:T(8,128)(2,1)S(1)}, f32[8,9,128,256]{3,2,1,0:T(8,128)S(1)}, f32[8,40,128]{2,1,0:T(8,128)S(1)}) custom-call(f32[4,4,8,128]{3,2,1,0:T(8,128)S(1)} %collective-permute-done.3.refs_0_, f32[4,4,8,128]{3,2,1,0:T(8,128)S(1)} %collective-permute-done.4.refs_1_, bf16[8,128,48]{2,1,0:T(8,128)(2,1)S(1)} %get-tuple-element.39.refs_2_.refs_1_), custom_call_target="tpu_custom_call" | custom-call | tf_op jit(solution)/shard_map/pallas_call | solution.py:315
  28.4 0.2 shard_map.83
  28.6 2.5 %collective-permute-start.6 = (f32[2,2,2,128]{3,2,1,0:T(2,128)S(1)}, f32[2,2,2,128]{3,2,1,0:T(2,128)S(1)}, u32[]{:S(2)}, u32[]{:S(2)}) collective-permute-start(f32[2,2,2,128]{3,2,1,0:T(2,128)S(1)} %get-tuple-element.52), channel_id=1, source_target_pairs={{0,3},{1,2},{2,1},{3,0},{4,7},{5,6},{6,5},{7,4},{8,11},{9,10},{10,... | collective-permute-start | bytes 12296 | tf_op jit(solution)/shard_map/ppermute | solution.py:355
  31.2 1.0 %collective-permute-done.5.refs_2_.refs_0_ = f32[2,2,2,128]{3,2,1,0:T(2,128)S(1)} collective-permute-done((f32[2,2,2,128]{3,2,1,0:T(2,128)S(1)}, f32[2,2,2,128]{3,2,1,0:T(2,128)S(1)}, u32[]{:S(2)}, u32[]{:S(2)}) %collective-permute-start.5) | collective-permute-done | bytes 4128 | tf_op jit(solution)/shard_map/ppermute | solution.py:355
  32.2 1.9 %collective-permute-done.6.refs_3_.refs_1_ = f32[2,2,2,128]{3,2,1,0:T(2,128)S(1)} collective-permute-done((f32[2,2,2,128]{3,2,1,0:T(2,128)S(1)}, f32[2,2,2,128]{3,2,1,0:T(2,128)S(1)}, u32[]{:S(2)}, u32[]{:S(2)}) %collective-permute-start.6) | collective-permute-done | bytes 4128 | tf_op jit(solution)/shard_map/ppermute | solution.py:355
  34.1 1.6 %collective-permute-start.7 = (f32[2,2,4,2,128]{4,3,2,1,0:T(2,128)S(1)}, f32[2,2,4,2,128]{4,3,2,1,0:T(2,128)S(1)}, u32[]{:S(2)}, u32[]{:S(2)}) collective-permute-start(f32[2,2,4,2,128]{4,3,2,1,0:T(2,128)S(1)} %shard_map.87), channel_id=1, source_target_pairs={{0,16},{16,0},{1,17},{17,1},{2,18},{18,2},{3,19},{19,3},{4,20},{20... | collective-permute-start | bytes 49160 | tf_op jit(solution)/shard_map/ppermute | solution.py:355
  35.7 2.2 %collective-permute-done.7.refs_1_.refs_2_ = f32[2,2,4,2,128]{4,3,2,1,0:T(2,128)S(1)} collective-permute-done((f32[2,2,4,2,128]{4,3,2,1,0:T(2,128)S(1)}, f32[2,2,4,2,128]{4,3,2,1,0:T(2,128)S(1)}, u32[]{:S(2)}, u32[]{:S(2)}) %collective-permute-start.7) | collective-permute-done | bytes 16416 | tf_op jit(solution)/shard_map/ppermute | solution.py:355
  38.0 0.6 %collective-permute-start.9 = (f32[4,4,2,128]{3,2,1,0:T(2,128)S(1)}, f32[4,4,2,128]{3,2,1,0:T(2,128)S(1)}, u32[]{:S(2)}, u32[]{:S(2)}) collective-permute-start(f32[4,4,2,128]{3,2,1,0:T(2,128)S(1)} %get-tuple-element.62), channel_id=1, source_target_pairs={{0,12},{4,8},{8,4},{12,0},{1,13},{5,9},{9,5},{13,1},{2,14},{6,10},... | collective-permute-start | bytes 49160 | tf_op jit(solution)/shard_map/ppermute | solution.py:355
  38.7 0.3 shard_map.84.spread_ref.refs_4_.refs_2_
  39.0 2.5 %shard_map.85 = (f32[8,32,128]{2,1,0:T(8,128)S(1)}, f32[8,16,128]{2,1,0:T(8,128)S(1)}) custom-call(f32[2,2,2,8,128]{4,3,2,1,0:T(8,128)S(1)} %get-tuple-element.35.own_ref, f32[2,2,2,2,128]{4,3,2,1,0:T(2,128)S(1)} %get-tuple-element.45.press_ref.own_ref, f32[8,128,128]{2,1,0:T(8,128)S(1)} %shard_map.84.spread_ref.refs_4_.refs_2_, ...), custom_call_target="tpu_custom_call" | custom-call | tf_op jit(solution)/shard_map/pallas_call | solution.py:315
  41.4 1.4 %shard_map.86 = (f32[8,32,128]{2,1,0:T(8,128)S(1)}, f32[8,16,128]{2,1,0:T(8,128)S(1)}) custom-call(f32[2,2,8,128]{3,2,1,0:T(8,128)S(1)} %collective-permute-done.refs_0_, f32[2,2,8,128]{3,2,1,0:T(8,128)S(1)} %collective-permute-done.1.refs_1_, f32[2,2,2,128]{3,2,1,0:T(2,128)S(1)} %collective-permute-done.5.refs_2_.refs_0_, ...), custom_call_target="tpu_custom_call" | custom-call | tf_op jit(solution)/shard_map/pallas_call | solution.py:315
  42.9 2.0 %shard_map.88 = (f32[8,32,128]{2,1,0:T(8,128)S(1)}, f32[8,16,128]{2,1,0:T(8,128)S(1)}) custom-call(f32[2,2,4,8,128]{4,3,2,1,0:T(8,128)S(1)} %collective-permute-done.2.refs_0_.refs_2_, f32[2,2,4,2,128]{4,3,2,1,0:T(2,128)S(1)} %collective-permute-done.7.refs_1_.refs_2_, f32[8,128,128]{2,1,0:T(8,128)S(1)} %shard_map.84.spread_ref.refs_4_.refs_2_, ...), custom_call_target="tpu_custom_call" | custom-call | tf_op jit(solution)/shard_map/pallas_call | solution.py:315
  44.9 3.4 %shard_map.90 = (f32[8,32,128]{2,1,0:T(8,128)S(1)}, f32[8,16,128]{2,1,0:T(8,128)S(1)}) custom-call(f32[4,4,8,128]{3,2,1,0:T(8,128)S(1)} %collective-permute-done.3.refs_0_, f32[4,4,8,128]{3,2,1,0:T(8,128)S(1)} %collective-permute-done.4.refs_1_, f32[4,4,2,128]{3,2,1,0:T(2,128)S(1)} %collective-permute-done.8.refs_2_, ...), custom_call_target="tpu_custom_call" | custom-call | tf_op jit(solution)/shard_map/pallas_call | solution.py:315
  48.3 0.7 %shard_map.91 = (f32[2,2,2,128]{3,2,1,0:T(2,128)}, f32[3,2,2,2,128]{4,3,2,1,0:T(2,128)}, f32[2,2,2,128]{3,2,1,0:T(2,128)}) custom-call(f32[2,2,2,8,128]{4,3,2,1,0:T(8,128)S(1)} %get-tuple-element.35.own_ref, f32[2,2,2,2,128]{4,3,2,1,0:T(2,128)S(1)} %get-tuple-element.45.press_ref.own_ref, f32[8,8,128]{2,1,0:T(8,128)S(1)} %get-tuple-element.46.first_ref, ...), custom_call_target="tpu_custom_call" | custom-call | tf_op jit(solution)/shard_map/pallas_call | solution.py:315
  (12 shorter events, 0.3 us)
Async XLA Ops:
  1.5 5.6 %collective-permute-start = (f32[2,2,8,128]{3,2,1,0:T(8,128)S(1)}, f32[2,2,8,128]{3,2,1,0:T(8,128)S(1)}, u32[]{:S(2)}, u32[]{:S(2)}) collective-permute-start(f32[2,2,8,128]{3,2,1,0:T(8,128)S(1)} %get-tuple-element.37), channel_id=1, source_target_pairs={{0,1},{1,0},{2,3},{3,2},{4,5},{5,4},{6,7},{7,6},{8,9},{9,8},{10,11... | collective-permute-start | bytes 49160 | tf_op jit(solution)/shard_map/ppermute | solution.py:355
  4.6 5.5 %collective-permute-start.1 = (f32[2,2,8,128]{3,2,1,0:T(8,128)S(1)}, f32[2,2,8,128]{3,2,1,0:T(8,128)S(1)}, u32[]{:S(2)}, u32[]{:S(2)}) collective-permute-start(f32[2,2,8,128]{3,2,1,0:T(8,128)S(1)} %get-tuple-element.38), channel_id=1, source_target_pairs={{0,3},{1,2},{2,1},{3,0},{4,7},{5,6},{6,5},{7,4},{8,11},{9,10},{10,... | collective-permute-start | bytes 49160 | tf_op jit(solution)/shard_map/ppermute | solution.py:355
  10.2 4.3 %collective-permute-start.2 = (f32[2,2,4,8,128]{4,3,2,1,0:T(8,128)S(1)}, f32[2,2,4,8,128]{4,3,2,1,0:T(8,128)S(1)}, u32[]{:S(2)}, u32[]{:S(2)}) collective-permute-start(f32[2,2,4,8,128]{4,3,2,1,0:T(8,128)S(1)} %shard_map.79), channel_id=1, source_target_pairs={{0,16},{16,0},{1,17},{17,1},{2,18},{18,2},{3,19},{19,3},{4,20},{20... | collective-permute-start | bytes 196616 | tf_op jit(solution)/shard_map/ppermute | solution.py:355
  14.5 9.8 %collective-permute-start.3 = (f32[4,4,8,128]{3,2,1,0:T(8,128)S(1)}, f32[4,4,8,128]{3,2,1,0:T(8,128)S(1)}, u32[]{:S(2)}, u32[]{:S(2)}) collective-permute-start(f32[4,4,8,128]{3,2,1,0:T(8,128)S(1)} %get-tuple-element.42), channel_id=1, source_target_pairs={{0,4},{4,0},{8,12},{12,8},{1,5},{5,1},{9,13},{13,9},{2,6},{6,2},{1... | collective-permute-start | bytes 196616 | tf_op jit(solution)/shard_map/ppermute | solution.py:355
  14.6 9.7 %collective-permute-start.4 = (f32[4,4,8,128]{3,2,1,0:T(8,128)S(1)}, f32[4,4,8,128]{3,2,1,0:T(8,128)S(1)}, u32[]{:S(2)}, u32[]{:S(2)}) collective-permute-start(f32[4,4,8,128]{3,2,1,0:T(8,128)S(1)} %get-tuple-element.43), channel_id=1, source_target_pairs={{0,12},{4,8},{8,4},{12,0},{1,13},{5,9},{9,5},{13,1},{2,14},{6,10},... | collective-permute-start | bytes 196616 | tf_op jit(solution)/shard_map/ppermute | solution.py:355
  28.6 3.7 %collective-permute-start.5 = (f32[2,2,2,128]{3,2,1,0:T(2,128)S(1)}, f32[2,2,2,128]{3,2,1,0:T(2,128)S(1)}, u32[]{:S(2)}, u32[]{:S(2)}) collective-permute-start(f32[2,2,2,128]{3,2,1,0:T(2,128)S(1)} %get-tuple-element.51), channel_id=1, source_target_pairs={{0,1},{1,0},{2,3},{3,2},{4,5},{5,4},{6,7},{7,6},{8,9},{9,8},{10,11... | collective-permute-start | bytes 12296 | tf_op jit(solution)/shard_map/ppermute | solution.py:355
  28.6 5.5 %collective-permute-start.6 = (f32[2,2,2,128]{3,2,1,0:T(2,128)S(1)}, f32[2,2,2,128]{3,2,1,0:T(2,128)S(1)}, u32[]{:S(2)}, u32[]{:S(2)}) collective-permute-start(f32[2,2,2,128]{3,2,1,0:T(2,128)S(1)} %get-tuple-element.52), channel_id=1, source_target_pairs={{0,3},{1,2},{2,1},{3,0},{4,7},{5,6},{6,5},{7,4},{8,11},{9,10},{10,... | collective-permute-start | bytes 12296 | tf_op jit(solution)/shard_map/ppermute | solution.py:355
  34.1 3.8 %collective-permute-start.7 = (f32[2,2,4,2,128]{4,3,2,1,0:T(2,128)S(1)}, f32[2,2,4,2,128]{4,3,2,1,0:T(2,128)S(1)}, u32[]{:S(2)}, u32[]{:S(2)}) collective-permute-start(f32[2,2,4,2,128]{4,3,2,1,0:T(2,128)S(1)} %shard_map.87), channel_id=1, source_target_pairs={{0,16},{16,0},{1,17},{17,1},{2,18},{18,2},{3,19},{19,3},{4,20},{20... | collective-permute-start | bytes 49160 | tf_op jit(solution)/shard_map/ppermute | solution.py:355
  38.0 7.0 %collective-permute-start.8 = (f32[4,4,2,128]{3,2,1,0:T(2,128)S(1)}, f32[4,4,2,128]{3,2,1,0:T(2,128)S(1)}, u32[]{:S(2)}, u32[]{:S(2)}) collective-permute-start(f32[4,4,2,128]{3,2,1,0:T(2,128)S(1)} %get-tuple-element.61), channel_id=1, source_target_pairs={{0,4},{4,0},{8,12},{12,8},{1,5},{5,1},{9,13},{13,9},{2,6},{6,2},{1... | collective-permute-start | bytes 49160 | tf_op jit(solution)/shard_map/ppermute | solution.py:355
  38.0 6.9 %collective-permute-start.9 = (f32[4,4,2,128]{3,2,1,0:T(2,128)S(1)}, f32[4,4,2,128]{3,2,1,0:T(2,128)S(1)}, u32[]{:S(2)}, u32[]{:S(2)}) collective-permute-start(f32[4,4,2,128]{3,2,1,0:T(2,128)S(1)} %get-tuple-element.62), channel_id=1, source_target_pairs={{0,12},{4,8},{8,4},{12,0},{1,13},{5,9},{9,5},{13,1},{2,14},{6,10},... | collective-permute-start | bytes 49160 | tf_op jit(solution)/shard_map/ppermute | solution.py:355

commit v6 on v5

--- a/solution.py
+++ b/solution.py
@@ -225,7 +225,7 @@
                 sums[c] = sofar[j]
                 pulls[c] = pulled[j]
 
-        pipelined(tiles, (terms, reduce))
+        pipelined(tiles, (terms, idle, reduce))
         return 0
 
     over_cells(some)
@@ -446,7 +446,7 @@
                 prepare(tile, offsets_of(place(at)), at, feats, masses, columns)
                 return 0
 
-            lax.fori_loop(0, half, one, 0, unroll=min(half, 8))
+            lax.fori_loop(0, half, one, 0, unroll=half)
         density_pairs(own_ref, near, feats, masses, columns, slopes, pairs, sums, weighted)
 
     return call(body, pair_outputs(count), (*received, own_feats), scratch=scratch_density(entries))
@@ -550,7 +550,7 @@
                 prepare_force(tile, offsets_of(place(at)), fields, at, rhos, columns, gradients)
                 return 0
 
-            lax.fori_loop(0, half, one, 0, unroll=min(half, 8))
+            lax.fori_loop(0, half, one, 0, unroll=half)
 
         force_pairs(near, spread_ref, rhos, columns, gradients, slopes, pairs, sums, pulls)
 

time: 49.3 us -> 48.6 us (0.986)
  Pallas kernels: 23.6 us -> 22.9 us
    pallas_call x16, Pallas kernels: 23.6 us -> 22.9 us  [call(): pl.pallas_call(body, out_shape=tuple(outs), in_specs=specs or [vmem] * le...]
  transfers between devices with their start and end apart: 10 -> 10, of which waited for: 5 -> 5; matrix products, arithmetic and copies ran while one was open for 0% -> 0% of each run, Pallas kernels for 29% -> 30%
where the time goes in v6:
time: 48.6 us; the launch traced here: 48.4 us
  Pallas kernels  22.9 us (47%)
  starting transfers between devices  13.7 us (28%)
  waiting for transfers between devices  11 us (23%)
  between operations  0.72 us (1%)
    pallas_call x16, Pallas kernels, call(): pl.pallas_call(body, out_shape=tuple(outs), in_specs=specs or [vmem] * le...  22.9 us
    ppermute x10, starting transfers between devices, receive(): got.append(lax.ppermute(send, axis, way))  13.7 us
    ppermute x10, waiting for transfers between devices, receive(): got.append(lax.ppermute(send, axis, way))  11 us
  transfers between devices with their start and end apart: 10, of which 5 were waited for; matrix products, arithmetic and copies ran while one was open for 0% of the time, Pallas kernels for 30%

profile of v6, /device:TPU:0, one launch (start us, length us, event | category | flops | bytes accessed | tf_op | source)
XLA Modules:
  0.0 48.4 jit_solution(11579954241793972296)
XLA Ops:
  0.6 0.9 %shard_map.76 = (f32[2,2,2,8,128]{4,3,2,1,0:T(8,128)S(1)}, f32[2,2,8,128]{3,2,1,0:T(8,128)S(1)}, f32[2,2,8,128]{3,2,1,0:T(8,128)S(1)}) custom-call(f32[3,2,2,2,128]{4,3,2,1,0:T(2,128)} %refs_0_.1, f32[3,2,2,2,128]{4,3,2,1,0:T(2,128)} %refs_1_.1, f32[2,2,2,128]{3,2,1,0:T(2,128)} %refs_2_.1, f32[2,2,2,128]{3,2,1,0:T(2,128)} %refs_3_.1, s32[2,2,2]{2,1,0:T(2,128)} %refs_4_.1), custom_call_target="tpu_custom_call" | custom-call | tf_op jit(solution)/shard_map/pallas_call | solution.py:315
  1.5 3.1 %collective-permute-start = (f32[2,2,8,128]{3,2,1,0:T(8,128)S(1)}, f32[2,2,8,128]{3,2,1,0:T(8,128)S(1)}, u32[]{:S(2)}, u32[]{:S(2)}) collective-permute-start(f32[2,2,8,128]{3,2,1,0:T(8,128)S(1)} %get-tuple-element.37), channel_id=1, source_target_pairs={{0,1},{1,0},{2,3},{3,2},{4,5},{5,4},{6,7},{7,6},{8,9},{9,8},{10,11... | collective-permute-start | bytes 49160 | tf_op jit(solution)/shard_map/ppermute | solution.py:355
  4.6 2.5 %collective-permute-start.1 = (f32[2,2,8,128]{3,2,1,0:T(8,128)S(1)}, f32[2,2,8,128]{3,2,1,0:T(8,128)S(1)}, u32[]{:S(2)}, u32[]{:S(2)}) collective-permute-start(f32[2,2,8,128]{3,2,1,0:T(8,128)S(1)} %get-tuple-element.38), channel_id=1, source_target_pairs={{0,3},{1,2},{2,1},{3,0},{4,7},{5,6},{6,5},{7,4},{8,11},{9,10},{10,... | collective-permute-start | bytes 49160 | tf_op jit(solution)/shard_map/ppermute | solution.py:355
  7.1 3.1 %collective-permute-done.1.refs_1_ = f32[2,2,8,128]{3,2,1,0:T(8,128)S(1)} collective-permute-done((f32[2,2,8,128]{3,2,1,0:T(8,128)S(1)}, f32[2,2,8,128]{3,2,1,0:T(8,128)S(1)}, u32[]{:S(2)}, u32[]{:S(2)}) %collective-permute-start.1) | collective-permute-done | bytes 16416 | tf_op jit(solution)/shard_map/ppermute | solution.py:355
  10.2 1.6 %collective-permute-start.2 = (f32[2,2,4,8,128]{4,3,2,1,0:T(8,128)S(1)}, f32[2,2,4,8,128]{4,3,2,1,0:T(8,128)S(1)}, u32[]{:S(2)}, u32[]{:S(2)}) collective-permute-start(f32[2,2,4,8,128]{4,3,2,1,0:T(8,128)S(1)} %shard_map.79), channel_id=1, source_target_pairs={{0,16},{16,0},{1,17},{17,1},{2,18},{18,2},{3,19},{19,3},{4,20},{20... | collective-permute-start | bytes 196616 | tf_op jit(solution)/shard_map/ppermute | solution.py:355
  11.7 2.8 %collective-permute-done.2.refs_0_.refs_2_ = f32[2,2,4,8,128]{4,3,2,1,0:T(8,128)S(1)} collective-permute-done((f32[2,2,4,8,128]{4,3,2,1,0:T(8,128)S(1)}, f32[2,2,4,8,128]{4,3,2,1,0:T(8,128)S(1)}, u32[]{:S(2)}, u32[]{:S(2)}) %collective-permute-start.2) | collective-permute-done | bytes 65568 | tf_op jit(solution)/shard_map/ppermute | solution.py:355
  14.6 1.6 %collective-permute-start.4 = (f32[4,4,8,128]{3,2,1,0:T(8,128)S(1)}, f32[4,4,8,128]{3,2,1,0:T(8,128)S(1)}, u32[]{:S(2)}, u32[]{:S(2)}) collective-permute-start(f32[4,4,8,128]{3,2,1,0:T(8,128)S(1)} %get-tuple-element.43), channel_id=1, source_target_pairs={{0,12},{4,8},{8,4},{12,0},{1,13},{5,9},{9,5},{13,1},{2,14},{6,10},... | collective-permute-start | bytes 196616 | tf_op jit(solution)/shard_map/ppermute | solution.py:355
  16.2 3.2 %shard_map.77 = (bf16[8,8,128,256]{3,2,1,0:T(8,128)(2,1)S(1)}, f32[8,8,128,256]{3,2,1,0:T(8,128)S(1)}, f32[8,40,128]{2,1,0:T(8,128)S(1)}, bf16[8,128,48]{2,1,0:T(8,128)(2,1)S(1)}) custom-call(f32[2,2,2,8,128]{4,3,2,1,0:T(8,128)S(1)} %get-tuple-element.35.own_ref), custom_call_target="tpu_custom_call" | custom-call | tf_op jit(solution)/shard_map/pallas_call | solution.py:315
  19.5 2.1 %shard_map.78 = (bf16[8,4,128,256]{3,2,1,0:T(8,128)(2,1)S(1)}, f32[8,4,128,256]{3,2,1,0:T(8,128)S(1)}, f32[8,40,128]{2,1,0:T(8,128)S(1)}) custom-call(f32[2,2,8,128]{3,2,1,0:T(8,128)S(1)} %collective-permute-done.refs_0_, f32[2,2,8,128]{3,2,1,0:T(8,128)S(1)} %collective-permute-done.1.refs_1_, bf16[8,128,48]{2,1,0:T(8,128)(2,1)S(1)} %get-tuple-element.39.refs_2_.refs_1_), custom_call_target="tpu_custom_call" | custom-call | tf_op jit(solution)/shard_map/pallas_call | solution.py:315
  21.6 2.7 %shard_map.80 = (bf16[8,6,128,256]{3,2,1,0:T(8,128)(2,1)S(1)}, f32[8,6,128,256]{3,2,1,0:T(8,128)S(1)}, f32[8,40,128]{2,1,0:T(8,128)S(1)}) custom-call(f32[2,2,4,8,128]{4,3,2,1,0:T(8,128)S(1)} %collective-permute-done.2.refs_0_.refs_2_, bf16[8,128,48]{2,1,0:T(8,128)(2,1)S(1)} %get-tuple-element.39.refs_2_.refs_1_), custom_call_target="tpu_custom_call" | custom-call | tf_op jit(solution)/shard_map/pallas_call | solution.py:315
  24.4 3.8 %shard_map.82 = (bf16[8,9,128,256]{3,2,1,0:T(8,128)(2,1)S(1)}, f32[8,9,128,256]{3,2,1,0:T(8,128)S(1)}, f32[8,40,128]{2,1,0:T(8,128)S(1)}) custom-call(f32[4,4,8,128]{3,2,1,0:T(8,128)S(1)} %collective-permute-done.3.refs_0_, f32[4,4,8,128]{3,2,1,0:T(8,128)S(1)} %collective-permute-done.4.refs_1_, bf16[8,128,48]{2,1,0:T(8,128)(2,1)S(1)} %get-tuple-element.39.refs_2_.refs_1_), custom_call_target="tpu_custom_call" | custom-call | tf_op jit(solution)/shard_map/pallas_call | solution.py:315
  28.1 0.2 shard_map.83
  28.3 2.5 %collective-permute-start.6 = (f32[2,2,2,128]{3,2,1,0:T(2,128)S(1)}, f32[2,2,2,128]{3,2,1,0:T(2,128)S(1)}, u32[]{:S(2)}, u32[]{:S(2)}) collective-permute-start(f32[2,2,2,128]{3,2,1,0:T(2,128)S(1)} %get-tuple-element.52), channel_id=1, source_target_pairs={{0,3},{1,2},{2,1},{3,0},{4,7},{5,6},{6,5},{7,4},{8,11},{9,10},{10,... | collective-permute-start | bytes 12296 | tf_op jit(solution)/shard_map/ppermute | solution.py:355
  30.9 1.0 %collective-permute-done.5.refs_2_.refs_0_ = f32[2,2,2,128]{3,2,1,0:T(2,128)S(1)} collective-permute-done((f32[2,2,2,128]{3,2,1,0:T(2,128)S(1)}, f32[2,2,2,128]{3,2,1,0:T(2,128)S(1)}, u32[]{:S(2)}, u32[]{:S(2)}) %collective-permute-start.5) | collective-permute-done | bytes 4128 | tf_op jit(solution)/shard_map/ppermute | solution.py:355
  31.9 1.9 %collective-permute-done.6.refs_3_.refs_1_ = f32[2,2,2,128]{3,2,1,0:T(2,128)S(1)} collective-permute-done((f32[2,2,2,128]{3,2,1,0:T(2,128)S(1)}, f32[2,2,2,128]{3,2,1,0:T(2,128)S(1)}, u32[]{:S(2)}, u32[]{:S(2)}) %collective-permute-start.6) | collective-permute-done | bytes 4128 | tf_op jit(solution)/shard_map/ppermute | solution.py:355
  33.8 1.6 %collective-permute-start.7 = (f32[2,2,4,2,128]{4,3,2,1,0:T(2,128)S(1)}, f32[2,2,4,2,128]{4,3,2,1,0:T(2,128)S(1)}, u32[]{:S(2)}, u32[]{:S(2)}) collective-permute-start(f32[2,2,4,2,128]{4,3,2,1,0:T(2,128)S(1)} %shard_map.87), channel_id=1, source_target_pairs={{0,16},{16,0},{1,17},{17,1},{2,18},{18,2},{3,19},{19,3},{4,20},{20... | collective-permute-start | bytes 49160 | tf_op jit(solution)/shard_map/ppermute | solution.py:355
  35.4 2.2 %collective-permute-done.7.refs_1_.refs_2_ = f32[2,2,4,2,128]{4,3,2,1,0:T(2,128)S(1)} collective-permute-done((f32[2,2,4,2,128]{4,3,2,1,0:T(2,128)S(1)}, f32[2,2,4,2,128]{4,3,2,1,0:T(2,128)S(1)}, u32[]{:S(2)}, u32[]{:S(2)}) %collective-permute-start.7) | collective-permute-done | bytes 16416 | tf_op jit(solution)/shard_map/ppermute | solution.py:355
  37.7 0.6 %collective-permute-start.9 = (f32[4,4,2,128]{3,2,1,0:T(2,128)S(1)}, f32[4,4,2,128]{3,2,1,0:T(2,128)S(1)}, u32[]{:S(2)}, u32[]{:S(2)}) collective-permute-start(f32[4,4,2,128]{3,2,1,0:T(2,128)S(1)} %get-tuple-element.62), channel_id=1, source_target_pairs={{0,12},{4,8},{8,4},{12,0},{1,13},{5,9},{9,5},{13,1},{2,14},{6,10},... | collective-permute-start | bytes 49160 | tf_op jit(solution)/shard_map/ppermute | solution.py:355
  38.4 0.3 shard_map.84.spread_ref.refs_4_.refs_2_
  38.7 2.5 %shard_map.85 = (f32[8,32,128]{2,1,0:T(8,128)S(1)}, f32[8,16,128]{2,1,0:T(8,128)S(1)}) custom-call(f32[2,2,2,8,128]{4,3,2,1,0:T(8,128)S(1)} %get-tuple-element.35.own_ref, f32[2,2,2,2,128]{4,3,2,1,0:T(2,128)S(1)} %get-tuple-element.45.press_ref.own_ref, f32[8,128,128]{2,1,0:T(8,128)S(1)} %shard_map.84.spread_ref.refs_4_.refs_2_, ...), custom_call_target="tpu_custom_call" | custom-call | tf_op jit(solution)/shard_map/pallas_call | solution.py:315
  41.1 1.4 %shard_map.86 = (f32[8,32,128]{2,1,0:T(8,128)S(1)}, f32[8,16,128]{2,1,0:T(8,128)S(1)}) custom-call(f32[2,2,8,128]{3,2,1,0:T(8,128)S(1)} %collective-permute-done.refs_0_, f32[2,2,8,128]{3,2,1,0:T(8,128)S(1)} %collective-permute-done.1.refs_1_, f32[2,2,2,128]{3,2,1,0:T(2,128)S(1)} %collective-permute-done.5.refs_2_.refs_0_, ...), custom_call_target="tpu_custom_call" | custom-call | tf_op jit(solution)/shard_map/pallas_call | solution.py:315
  42.6 2.0 %shard_map.88 = (f32[8,32,128]{2,1,0:T(8,128)S(1)}, f32[8,16,128]{2,1,0:T(8,128)S(1)}) custom-call(f32[2,2,4,8,128]{4,3,2,1,0:T(8,128)S(1)} %collective-permute-done.2.refs_0_.refs_2_, f32[2,2,4,2,128]{4,3,2,1,0:T(2,128)S(1)} %collective-permute-done.7.refs_1_.refs_2_, f32[8,128,128]{2,1,0:T(8,128)S(1)} %shard_map.84.spread_ref.refs_4_.refs_2_, ...), custom_call_target="tpu_custom_call" | custom-call | tf_op jit(solution)/shard_map/pallas_call | solution.py:315
  44.6 3.0 %shard_map.90 = (f32[8,32,128]{2,1,0:T(8,128)S(1)}, f32[8,16,128]{2,1,0:T(8,128)S(1)}) custom-call(f32[4,4,8,128]{3,2,1,0:T(8,128)S(1)} %collective-permute-done.3.refs_0_, f32[4,4,8,128]{3,2,1,0:T(8,128)S(1)} %collective-permute-done.4.refs_1_, f32[4,4,2,128]{3,2,1,0:T(2,128)S(1)} %collective-permute-done.8.refs_2_, ...), custom_call_target="tpu_custom_call" | custom-call | tf_op jit(solution)/shard_map/pallas_call | solution.py:315
  47.6 0.7 %shard_map.91 = (f32[2,2,2,128]{3,2,1,0:T(2,128)}, f32[3,2,2,2,128]{4,3,2,1,0:T(2,128)}, f32[2,2,2,128]{3,2,1,0:T(2,128)}) custom-call(f32[2,2,2,8,128]{4,3,2,1,0:T(8,128)S(1)} %get-tuple-element.35.own_ref, f32[2,2,2,2,128]{4,3,2,1,0:T(2,128)S(1)} %get-tuple-element.45.press_ref.own_ref, f32[8,8,128]{2,1,0:T(8,128)S(1)} %get-tuple-element.46.first_ref, ...), custom_call_target="tpu_custom_call" | custom-call | tf_op jit(solution)/shard_map/pallas_call | solution.py:315
  (12 shorter events, 0.3 us)
Async XLA Ops:
  1.5 5.6 %collective-permute-start = (f32[2,2,8,128]{3,2,1,0:T(8,128)S(1)}, f32[2,2,8,128]{3,2,1,0:T(8,128)S(1)}, u32[]{:S(2)}, u32[]{:S(2)}) collective-permute-start(f32[2,2,8,128]{3,2,1,0:T(8,128)S(1)} %get-tuple-element.37), channel_id=1, source_target_pairs={{0,1},{1,0},{2,3},{3,2},{4,5},{5,4},{6,7},{7,6},{8,9},{9,8},{10,11... | collective-permute-start | bytes 49160 | tf_op jit(solution)/shard_map/ppermute | solution.py:355
  4.6 5.5 %collective-permute-start.1 = (f32[2,2,8,128]{3,2,1,0:T(8,128)S(1)}, f32[2,2,8,128]{3,2,1,0:T(8,128)S(1)}, u32[]{:S(2)}, u32[]{:S(2)}) collective-permute-start(f32[2,2,8,128]{3,2,1,0:T(8,128)S(1)} %get-tuple-element.38), channel_id=1, source_target_pairs={{0,3},{1,2},{2,1},{3,0},{4,7},{5,6},{6,5},{7,4},{8,11},{9,10},{10,... | collective-permute-start | bytes 49160 | tf_op jit(solution)/shard_map/ppermute | solution.py:355
  10.2 4.3 %collective-permute-start.2 = (f32[2,2,4,8,128]{4,3,2,1,0:T(8,128)S(1)}, f32[2,2,4,8,128]{4,3,2,1,0:T(8,128)S(1)}, u32[]{:S(2)}, u32[]{:S(2)}) collective-permute-start(f32[2,2,4,8,128]{4,3,2,1,0:T(8,128)S(1)} %shard_map.79), channel_id=1, source_target_pairs={{0,16},{16,0},{1,17},{17,1},{2,18},{18,2},{3,19},{19,3},{4,20},{20... | collective-permute-start | bytes 196616 | tf_op jit(solution)/shard_map/ppermute | solution.py:355
  14.5 9.8 %collective-permute-start.3 = (f32[4,4,8,128]{3,2,1,0:T(8,128)S(1)}, f32[4,4,8,128]{3,2,1,0:T(8,128)S(1)}, u32[]{:S(2)}, u32[]{:S(2)}) collective-permute-start(f32[4,4,8,128]{3,2,1,0:T(8,128)S(1)} %get-tuple-element.42), channel_id=1, source_target_pairs={{0,4},{4,0},{8,12},{12,8},{1,5},{5,1},{9,13},{13,9},{2,6},{6,2},{1... | collective-permute-start | bytes 196616 | tf_op jit(solution)/shard_map/ppermute | solution.py:355
  14.6 9.7 %collective-permute-start.4 = (f32[4,4,8,128]{3,2,1,0:T(8,128)S(1)}, f32[4,4,8,128]{3,2,1,0:T(8,128)S(1)}, u32[]{:S(2)}, u32[]{:S(2)}) collective-permute-start(f32[4,4,8,128]{3,2,1,0:T(8,128)S(1)} %get-tuple-element.43), channel_id=1, source_target_pairs={{0,12},{4,8},{8,4},{12,0},{1,13},{5,9},{9,5},{13,1},{2,14},{6,10},... | collective-permute-start | bytes 196616 | tf_op jit(solution)/shard_map/ppermute | solution.py:355
  28.3 3.7 %collective-permute-start.5 = (f32[2,2,2,128]{3,2,1,0:T(2,128)S(1)}, f32[2,2,2,128]{3,2,1,0:T(2,128)S(1)}, u32[]{:S(2)}, u32[]{:S(2)}) collective-permute-start(f32[2,2,2,128]{3,2,1,0:T(2,128)S(1)} %get-tuple-element.51), channel_id=1, source_target_pairs={{0,1},{1,0},{2,3},{3,2},{4,5},{5,4},{6,7},{7,6},{8,9},{9,8},{10,11... | collective-permute-start | bytes 12296 | tf_op jit(solution)/shard_map/ppermute | solution.py:355
  28.3 5.5 %collective-permute-start.6 = (f32[2,2,2,128]{3,2,1,0:T(2,128)S(1)}, f32[2,2,2,128]{3,2,1,0:T(2,128)S(1)}, u32[]{:S(2)}, u32[]{:S(2)}) collective-permute-start(f32[2,2,2,128]{3,2,1,0:T(2,128)S(1)} %get-tuple-element.52), channel_id=1, source_target_pairs={{0,3},{1,2},{2,1},{3,0},{4,7},{5,6},{6,5},{7,4},{8,11},{9,10},{10,... | collective-permute-start | bytes 12296 | tf_op jit(solution)/shard_map/ppermute | solution.py:355
  33.8 3.8 %collective-permute-start.7 = (f32[2,2,4,2,128]{4,3,2,1,0:T(2,128)S(1)}, f32[2,2,4,2,128]{4,3,2,1,0:T(2,128)S(1)}, u32[]{:S(2)}, u32[]{:S(2)}) collective-permute-start(f32[2,2,4,2,128]{4,3,2,1,0:T(2,128)S(1)} %shard_map.87), channel_id=1, source_target_pairs={{0,16},{16,0},{1,17},{17,1},{2,18},{18,2},{3,19},{19,3},{4,20},{20... | collective-permute-start | bytes 49160 | tf_op jit(solution)/shard_map/ppermute | solution.py:355
  37.7 7.0 %collective-permute-start.8 = (f32[4,4,2,128]{3,2,1,0:T(2,128)S(1)}, f32[4,4,2,128]{3,2,1,0:T(2,128)S(1)}, u32[]{:S(2)}, u32[]{:S(2)}) collective-permute-start(f32[4,4,2,128]{3,2,1,0:T(2,128)S(1)} %get-tuple-element.61), channel_id=1, source_target_pairs={{0,4},{4,0},{8,12},{12,8},{1,5},{5,1},{9,13},{13,9},{2,6},{6,2},{1... | collective-permute-start | bytes 49160 | tf_op jit(solution)/shard_map/ppermute | solution.py:355
  37.7 6.9 %collective-permute-start.9 = (f32[4,4,2,128]{3,2,1,0:T(2,128)S(1)}, f32[4,4,2,128]{3,2,1,0:T(2,128)S(1)}, u32[]{:S(2)}, u32[]{:S(2)}) collective-permute-start(f32[4,4,2,128]{3,2,1,0:T(2,128)S(1)} %get-tuple-element.62), channel_id=1, source_target_pairs={{0,12},{4,8},{8,4},{12,0},{1,13},{5,9},{9,5},{13,1},{2,14},{6,10},... | collective-permute-start | bytes 49160 | tf_op jit(solution)/shard_map/ppermute | solution.py:355
